TPU v7x, 128 devices: a whole 4x4x4 slice. The times are simulated.
128 devices in a mesh: tm: 16 (over z, y_lo, core), lat: 8 (over x, y_hi).
Axes of the slice: x: 4, y: 4 (y_hi: 2, y_lo: 2; y = y_hi * 2 + y_lo), z: 4, core: 2. Of those that a mesh axis runs over, the one named last changes fastest.
Arguments:
- window_snapshots: bfloat16 [16, 64, 64, 128], P('tm', None, 'lat'), may hold values from -6 to 6
- background: bfloat16 [64, 64, 128], P(None, 'lat'), may hold values from -6 to 6
- obs_values: bfloat16 [16, 64, 2048], P('tm', None, 'lat'), may hold values from -6 to 6
- obs_index: int32 [16, 2048], P('tm', 'lat'), may hold values from 0 to 8191, as said below
- input_kernel_weight: bfloat16 [3, 3, 256, 64], replicated, may hold values from -0.25 to 0.25
- hidden_bias_vector: float32 [256], replicated, may hold values from -3 to 3
- output_pointwise_weight: bfloat16 [64, 256], replicated, may hold values from -0.375 to 0.375
Outputs:
- analysis: bfloat16 [16, 64, 64, 128], P('tm', None, 'lat')
Inputs may be any that keep to these rules, and one draw needn't show every extreme that they name: `obs_index`: entry [k, j] is a grid column counted latitude by latitude over 128 longitudes; observations s * 256 to (s + 1) * 256 - 1 lie in latitudes s * 8 to (s + 1) * 8 - 1; a column may be observed more than once.
All inputs are finite; a program needn't handle non-finite values.
Results may differ from a plain program's by a relative error of at most 0.015.
Values may be sent and summed in bfloat16 or wider, within the bound.
No kernel may reach another device: no remote copies, remote signals or barrier semaphores. Data moves between devices by JAX's collectives and lax.ppermute only.
A program may use at most 64 MiB of HBM per device.

v0:
```python
import jax
import jax.numpy as jnp
from jax import lax
from jax.sharding import PartitionSpec as P

ITERS = 2


step_size = 0.3


def with_halo(cells, sides, width):
    for axis, dim in sides:
        count = lax.axis_size(axis)
        ends = count - 1
        head = lax.slice_in_dim(cells, 0, width, axis=dim)
        tail = lax.slice_in_dim(cells, cells.shape[dim] - width, cells.shape[dim], axis=dim)
        cells = jnp.concatenate(
            [
                lax.ppermute(tail, axis, [(i, (i + 1) % count) for i in range(ends)]),
                cells,
                lax.ppermute(head, axis, [((i + 1) % count, i) for i in range(ends)]),
            ],
            axis=dim,
        )
    return cells


def from_behind(value, axis, by):
    length = lax.axis_size(axis)
    pairs = [(i, i + by) for i in range(length) if 0 <= i + by < length]
    return lax.ppermute(value, axis, pairs)


def shift_cells(grid_field, offset):
    return jnp.roll(grid_field, offset, axis=grid_field.ndim - 1)


def state_with_borders(stacked):
    return with_halo(stacked, (("lat", 2),), 1)


def advance_one_interval(
    bordered_field, input_kernel_weight, hidden_bias_vector, output_pointwise_weight
):
    height = bordered_field.shape[1] - 2
    before = hidden_bias_vector[:, None, None]
    for row_step in range(3):
        stripe = bordered_field[:, row_step : row_step + height, :]
        for col_step in range(3):
            before = before + jnp.einsum(
                "hc,clm->hlm",
                input_kernel_weight[row_step, col_step],
                shift_cells(stripe, 1 - col_step),
                preferred_element_type=jnp.float32,
            )
    active = jnp.tanh(before).astype(jnp.bfloat16)
    centre = bordered_field[:, 1 : height + 1, :].astype(jnp.float32)
    anticipated_snapshot = centre + jnp.einsum(
        "ch,hlm->clm", output_pointwise_weight, active, preferred_element_type=jnp.float32
    )
    return (anticipated_snapshot.astype(jnp.bfloat16), active)


def make_cotangent(active, dynamics_mismatch, output_pointwise_weight):
    projected = jnp.einsum(
        "ch,clm->hlm",
        output_pointwise_weight,
        dynamics_mismatch,
        preferred_element_type=jnp.float32,
    )
    squashed = active.astype(jnp.float32)
    return ((1.0 - squashed * squashed) * projected).astype(jnp.bfloat16)


def collect_rows(bordered_field, input_kernel_weight):
    height = bordered_field.shape[1] - 2
    summed = None
    for row_step in range(3):
        stripe = bordered_field[:, 2 - row_step : 2 - row_step + height, :]
        for col_step in range(3):
            product = jnp.einsum(
                "hc,hlm->clm",
                input_kernel_weight[row_step, col_step],
                shift_cells(stripe, col_step - 1),
                preferred_element_type=jnp.float32,
            )
            summed = product if summed is None else summed + product
    return summed


def pull_back(active, targets, input_kernel_weight, output_pointwise_weight):
    cotangents = lax.map(
        lambda paired: make_cotangent(paired[0], paired[1], output_pointwise_weight),
        (active, targets),
    )
    bordered_field = with_halo(cotangents, (("lat", 2),), 1)
    spreads = lax.map(
        lambda lone_snapshot: collect_rows(lone_snapshot, input_kernel_weight), bordered_field
    )
    return (targets.astype(jnp.float32) + spreads).astype(jnp.bfloat16)


def misfit_map(window_snapshots, obs_values, local_index):
    windows, channels, height, columns = window_snapshots.shape
    flattened = window_snapshots.reshape(windows, channels, height * columns)

    def scatter_one(grid_field, values, column_index):
        misfit = jnp.take(grid_field, column_index, axis=1).astype(jnp.float32) - values.astype(
            jnp.float32
        )
        return jnp.zeros(grid_field.shape, jnp.float32).at[:, column_index].add(misfit)

    return jax.vmap(scatter_one)(flattened, obs_values, local_index).reshape(window_snapshots.shape)


def descend(
    window_snapshots,
    background,
    obs_values,
    local_index,
    input_kernel_weight,
    hidden_bias_vector,
    output_pointwise_weight,
):
    windows = window_snapshots.shape[0]
    at_start = lax.axis_index("tm") == 0
    earlier_snapshot = from_behind(window_snapshots[windows - 1], "tm", 1)
    input_states = jnp.concatenate(
        [earlier_snapshot[None], window_snapshots[: windows - 1]], axis=0
    )
    anticipated_snapshot, active = lax.map(
        lambda lone_snapshot: advance_one_interval(
            lone_snapshot, input_kernel_weight, hidden_bias_vector, output_pointwise_weight
        ),
        state_with_borders(input_states),
    )
    opening_snapshots = jnp.where(at_start, background, anticipated_snapshot[0])
    trajectory_of_guesses = jnp.concatenate(
        [opening_snapshots[None], anticipated_snapshot[1:]], axis=0
    )
    dynamics_mismatch = (
        window_snapshots.astype(jnp.float32) - trajectory_of_guesses.astype(jnp.float32)
    ).astype(jnp.bfloat16)
    pulled = pull_back(active, dynamics_mismatch, input_kernel_weight, output_pointwise_weight)
    from_next = from_behind(pulled[0], "tm", -1)
    adjoint = jnp.concatenate([pulled[1:], from_next[None]], axis=0)
    innovation = misfit_map(window_snapshots, obs_values, local_index)
    gradient = dynamics_mismatch.astype(jnp.float32) - adjoint.astype(jnp.float32) + innovation
    return (window_snapshots.astype(jnp.float32) - step_size * gradient).astype(jnp.bfloat16)


def on_device(
    window_snapshots,
    background,
    obs_values,
    obs_index,
    input_kernel_weight,
    hidden_bias_vector,
    output_pointwise_weight,
):
    strip_cells = window_snapshots.shape[2] * window_snapshots.shape[3]
    local_index = obs_index - lax.axis_index("lat") * strip_cells
    for repeat in range(ITERS):
        window_snapshots = descend(
            window_snapshots,
            background,
            obs_values,
            local_index,
            input_kernel_weight,
            hidden_bias_vector,
            output_pointwise_weight,
        )
    return window_snapshots


def solution(mesh):
    placed = (
        P("tm", None, "lat", None),
        P(None, "lat", None),
        P("tm", None, "lat"),
        P("tm", "lat"),
        P(),
        P(),
        P(),
    )
    return jax.shard_map(
        on_device, mesh=mesh, in_specs=placed, out_specs=P("tm", None, "lat", None), check_vma=False
    )
```

profile of v0, /device:TPU:43, one launch (start us, length us, event | category | flops | bytes accessed | tf_op | source)
XLA Modules:
  0.0 93.9 jit_solution(17179225210469956772)
XLA Ops:
  0.0 0.9 copy.99
  0.9 4.0 %collective-permute-start = (bf16[64,8,128]{2,0,1:T(8,128)(2,1)S(1)}, bf16[64,8,128]{2,0,1:T(8,128)(2,1)S(1)}, u32[]{:S(2)}, u32[]{:S(2)}) collective-permute-start(bf16[64,8,128]{2,0,1:T(8,128)(2,1)S(1)} %bitcast.271), channel_id=1, source_target_pairs={{0,8},{8,16},{16,24},{24,32},{32,40},{40,48},{48,56},{56,64},{64,7... | collective-permute-start | bytes 393224 | tf_op jit(solution)/shard_map/ppermute | solution.py:32
  4.9 1.9 %collective-permute-done = bf16[64,8,128]{2,0,1:T(8,128)(2,1)S(1)} collective-permute-done((bf16[64,8,128]{2,0,1:T(8,128)(2,1)S(1)}, bf16[64,8,128]{2,0,1:T(8,128)(2,1)S(1)}, u32[]{:S(2)}, u32[]{:S(2)}) %collective-permute-start) | collective-permute-done | bytes 131104 | tf_op jit(solution)/shard_map/ppermute | solution.py:32
  6.9 4.2 %collective-permute-start.1 = (bf16[1,64,1,128]{3,1,2,0:T(8,128)(2,1)S(1)}, bf16[1,64,1,128]{3,1,2,0:T(8,128)(2,1)S(1)}, u32[]{:S(2)}, u32[]{:S(2)}) collective-permute-start(bf16[1,64,1,128]{3,1,2,0:T(8,128)(2,1)S(1)} %get-tuple-element.158), channel_id=1, source_target_pairs={{0,1},{1,2},{2,3},{3,4},{4,5},{5,6},{6,7},{8,9},{9,10},{10,11},{11... | collective-permute-start | bytes 49160 | tf_op jit(solution)/shard_map/ppermute | solution.py:20
  11.1 3.5 %collective-permute-start.2 = (bf16[1,64,1,128]{3,1,2,0:T(8,128)(2,1)S(1)}, bf16[1,64,1,128]{3,1,2,0:T(8,128)(2,1)S(1)}, u32[]{:S(2)}, u32[]{:S(2)}) collective-permute-start(bf16[1,64,1,128]{3,1,2,0:T(8,128)(2,1)S(1)} %get-tuple-element.159), channel_id=1, source_target_pairs={{1,0},{2,1},{3,2},{4,3},{5,4},{6,5},{7,6},{9,8},{10,9},{11,10},{12... | collective-permute-start | bytes 49160 | tf_op jit(solution)/shard_map/ppermute | solution.py:22
  14.6 0.7 and_reduce_fusion
  15.3 1.1 %copy.48 = bf16[1,64,8,128]{1,3,2,0:T(8,128)(2,1)S(1)} copy(bf16[1,64,8,128]{3,2,1,0:T(8,128)(2,1)} %param.9) | data formatting | bytes 262144 | tf_op args[0]
  16.4 0.9 copy.49
  17.8 0.7 copy-done.2
  18.5 0.4 fusion.111
  18.9 0.4 fusion.115
  19.4 0.4 fusion.119
  19.8 0.4 fusion.123
  20.2 0.4 fusion.127
  20.7 0.4 convolution_add_fusion.7
  21.1 0.3 fusion.10
  21.5 0.3 fusion.11
  21.8 0.3 fusion.19
  22.2 0.5 copy-done.1
  23.4 4.2 %collective-permute-start.3 = (bf16[1,256,1,128]{1,3,2,0:T(8,128)(2,1)S(1)}, bf16[1,256,1,128]{1,3,2,0:T(8,128)(2,1)S(1)}, u32[]{:S(2)}, u32[]{:S(2)}) collective-permute-start(bf16[1,256,1,128]{1,3,2,0:T(8,128)(2,1)S(1)} %get-tuple-element.128), channel_id=1, source_target_pairs={{0,1},{1,2},{2,3},{3,4},{4,5},{5,6},{6,7},{8,9},{9,10},{10,11},{11... | collective-permute-start | bytes 196616 | tf_op jit(solution)/shard_map/ppermute | solution.py:20
  27.6 3.5 %collective-permute-start.4 = (bf16[1,256,1,128]{1,3,2,0:T(8,128)(2,1)S(1)}, bf16[1,256,1,128]{1,3,2,0:T(8,128)(2,1)S(1)}, u32[]{:S(2)}, u32[]{:S(2)}) collective-permute-start(bf16[1,256,1,128]{1,3,2,0:T(8,128)(2,1)S(1)} %get-tuple-element.130), channel_id=1, source_target_pairs={{1,0},{2,1},{3,2},{4,3},{5,4},{6,5},{7,6},{9,8},{10,9},{11,10},{12... | collective-permute-start | bytes 196616 | tf_op jit(solution)/shard_map/ppermute | solution.py:22
  31.2 3.0 %collective-permute-done.4 = bf16[1,256,1,128]{1,3,2,0:T(8,128)(2,1)S(1)} collective-permute-done((bf16[1,256,1,128]{1,3,2,0:T(8,128)(2,1)S(1)}, bf16[1,256,1,128]{1,3,2,0:T(8,128)(2,1)S(1)}, u32[]{:S(2)}, u32[]{:S(2)}) %collective-permute-start.4) | collective-permute-done | bytes 65568 | tf_op jit(solution)/shard_map/ppermute | solution.py:22
  34.2 0.4 fusion.270
  37.3 5.8 %collective-permute-start.5 = (bf16[64,8,128]{2,0,1:T(8,128)(2,1)S(1)}, bf16[64,8,128]{2,0,1:T(8,128)(2,1)S(1)}, u32[]{:S(2)}, u32[]{:S(2)}) collective-permute-start(bf16[64,8,128]{2,0,1:T(8,128)(2,1)S(1)} %fusion.38), channel_id=1, source_target_pairs={{8,0},{16,8},{24,16},{32,24},{40,32},{48,40},{56,48},{64,56},{72,6... | collective-permute-start | bytes 393224 | tf_op jit(solution)/shard_map/ppermute | solution.py:32
  43.1 2.8 %scatter_custom_fusion = f32[64,1024]{0,1:T(8,128)S(1)} fusion(s32[256]{0:T(256)S(1)} %bitcast.275, f32[]{:T(128)} %constant.80.clone.1, bf16[1,64,256]{1,2,0:T(8,128)(2,1)S(1)} %copy.49, pred[256]{0:T(512)(128)(4,1)S(1)} %get-tuple-element.68, bf16[]{:T(256)} %constant.60.clone.2, bf16[1,64,1024]{1,2,0:T(8,128)(2,1)S(1)} %bitcast.269, s32[256]{0:T(256)S(1)} %bitcast.272), kind=kCustom, calls=%fused_computation.128 | custom fusion | flops 81920 | bytes 591366 | tf_op jit(solution)/shard_map/vmap()/scatter-add | solution.py:112
  46.1 2.0 %collective-permute-done.5 = bf16[64,8,128]{2,0,1:T(8,128)(2,1)S(1)} collective-permute-done((bf16[64,8,128]{2,0,1:T(8,128)(2,1)S(1)}, bf16[64,8,128]{2,0,1:T(8,128)(2,1)S(1)}, u32[]{:S(2)}, u32[]{:S(2)}) %collective-permute-start.5) | collective-permute-done | bytes 131104 | tf_op jit(solution)/shard_map/ppermute | solution.py:32
  48.1 2.3 %collective-permute-start.6 = (bf16[64,8,128]{2,0,1:T(8,128)(2,1)S(1)}, bf16[64,8,128]{2,0,1:T(8,128)(2,1)S(1)}, u32[]{:S(2)}, u32[]{:S(2)}) collective-permute-start(bf16[64,8,128]{2,0,1:T(8,128)(2,1)S(1)} %bitcast.268), channel_id=1, source_target_pairs={{0,8},{8,16},{16,24},{24,32},{32,40},{40,48},{48,56},{56,64},{64,7... | collective-permute-start | bytes 393224 | tf_op jit(solution)/shard_map/ppermute | solution.py:32
  50.4 1.9 %collective-permute-done.6 = bf16[64,8,128]{2,0,1:T(8,128)(2,1)S(1)} collective-permute-done((bf16[64,8,128]{2,0,1:T(8,128)(2,1)S(1)}, bf16[64,8,128]{2,0,1:T(8,128)(2,1)S(1)}, u32[]{:S(2)}, u32[]{:S(2)}) %collective-permute-start.6) | collective-permute-done | bytes 131104 | tf_op jit(solution)/shard_map/ppermute | solution.py:32
  52.3 4.2 %collective-permute-start.7 = (bf16[1,64,1,128]{3,1,2,0:T(8,128)(2,1)S(1)}, bf16[1,64,1,128]{3,1,2,0:T(8,128)(2,1)S(1)}, u32[]{:S(2)}, u32[]{:S(2)}) collective-permute-start(bf16[1,64,1,128]{3,1,2,0:T(8,128)(2,1)S(1)} %get-tuple-element.156), channel_id=1, source_target_pairs={{0,1},{1,2},{2,3},{3,4},{4,5},{5,6},{6,7},{8,9},{9,10},{10,11},{11... | collective-permute-start | bytes 49160 | tf_op jit(solution)/shard_map/ppermute | solution.py:20
  56.5 3.5 %collective-permute-start.8 = (bf16[1,64,1,128]{3,1,2,0:T(8,128)(2,1)S(1)}, bf16[1,64,1,128]{3,1,2,0:T(8,128)(2,1)S(1)}, u32[]{:S(2)}, u32[]{:S(2)}) collective-permute-start(bf16[1,64,1,128]{3,1,2,0:T(8,128)(2,1)S(1)} %get-tuple-element.157), channel_id=1, source_target_pairs={{1,0},{2,1},{3,2},{4,3},{5,4},{6,5},{7,6},{9,8},{10,9},{11,10},{12... | collective-permute-start | bytes 49160 | tf_op jit(solution)/shard_map/ppermute | solution.py:22
  60.0 2.5 %collective-permute-done.8 = bf16[1,64,1,128]{3,1,2,0:T(8,128)(2,1)S(1)} collective-permute-done((bf16[1,64,1,128]{3,1,2,0:T(8,128)(2,1)S(1)}, bf16[1,64,1,128]{3,1,2,0:T(8,128)(2,1)S(1)}, u32[]{:S(2)}, u32[]{:S(2)}) %collective-permute-start.8) | collective-permute-done | bytes 16416 | tf_op jit(solution)/shard_map/ppermute | solution.py:22
  63.1 0.4 convolution_add_fusion.6
  63.5 0.4 fusion.134
  63.9 0.4 fusion.138
  64.4 0.4 fusion.142
  64.8 0.4 fusion.146
  65.2 0.4 fusion.150
  65.7 0.3 fusion.12
  66.0 0.3 fusion.13
  66.3 0.3 fusion.18
  67.3 4.4 %collective-permute-start.10 = (bf16[1,256,1,128]{1,3,2,0:T(8,128)(2,1)S(1)}, bf16[1,256,1,128]{1,3,2,0:T(8,128)(2,1)S(1)}, u32[]{:S(2)}, u32[]{:S(2)}) collective-permute-start(bf16[1,256,1,128]{1,3,2,0:T(8,128)(2,1)S(1)} %get-tuple-element.123), channel_id=1, source_target_pairs={{1,0},{2,1},{3,2},{4,3},{5,4},{6,5},{7,6},{9,8},{10,9},{11,10},{12... | collective-permute-start | bytes 196616 | tf_op jit(solution)/shard_map/ppermute | solution.py:22
  71.7 2.6 %collective-permute-start.9 = (bf16[1,256,1,128]{1,3,2,0:T(8,128)(2,1)S(1)}, bf16[1,256,1,128]{1,3,2,0:T(8,128)(2,1)S(1)}, u32[]{:S(2)}, u32[]{:S(2)}) collective-permute-start(bf16[1,256,1,128]{1,3,2,0:T(8,128)(2,1)S(1)} %get-tuple-element.122), channel_id=1, source_target_pairs={{0,1},{1,2},{2,3},{3,4},{4,5},{5,6},{6,7},{8,9},{9,10},{10,11},{11... | collective-permute-start | bytes 196616 | tf_op jit(solution)/shard_map/ppermute | solution.py:20
  74.3 4.8 %collective-permute-done.9 = bf16[1,256,1,128]{1,3,2,0:T(8,128)(2,1)S(1)} collective-permute-done((bf16[1,256,1,128]{1,3,2,0:T(8,128)(2,1)S(1)}, bf16[1,256,1,128]{1,3,2,0:T(8,128)(2,1)S(1)}, u32[]{:S(2)}, u32[]{:S(2)}) %collective-permute-start.9) | collective-permute-done | bytes 65568 | tf_op jit(solution)/shard_map/ppermute | solution.py:20
  79.2 0.4 fusion.268
  82.3 4.9 %collective-permute-start.11 = (bf16[64,8,128]{2,0,1:T(8,128)(2,1)S(1)}, bf16[64,8,128]{2,0,1:T(8,128)(2,1)S(1)}, u32[]{:S(2)}, u32[]{:S(2)}) collective-permute-start(bf16[64,8,128]{2,0,1:T(8,128)(2,1)S(1)} %fusion.39), channel_id=1, source_target_pairs={{8,0},{16,8},{24,16},{32,24},{40,32},{48,40},{56,48},{64,56},{72,6... | collective-permute-start | bytes 393224 | tf_op jit(solution)/shard_map/ppermute | solution.py:32
  87.4 2.8 %scatter_custom_fusion.1 = f32[64,1024]{0,1:T(8,128)S(1)} fusion(s32[256]{0:T(256)S(1)} %bitcast.276, f32[]{:T(128)} %constant.80.clone.1, bf16[1,64,256]{1,2,0:T(8,128)(2,1)S(1)} %copy.49, pred[256]{0:T(512)(128)(4,1)S(1)} %get-tuple-element.68, bf16[]{:T(256)} %constant.60.clone.2, bf16[1,64,1024]{1,2,0:T(8,128)(2,1)S(1)} %bitcast.270, s32[256]{0:T(256)S(1)} %bitcast.273), kind=kCustom, calls=%fused_computation.126 | custom fusion | flops 81920 | bytes 591366 | tf_op jit(solution)/shard_map/vmap()/scatter-add | solution.py:112
  90.3 2.7 %collective-permute-done.11 = bf16[64,8,128]{2,0,1:T(8,128)(2,1)S(1)} collective-permute-done((bf16[64,8,128]{2,0,1:T(8,128)(2,1)S(1)}, bf16[64,8,128]{2,0,1:T(8,128)(2,1)S(1)}, u32[]{:S(2)}, u32[]{:S(2)}) %collective-permute-start.11) | collective-permute-done | bytes 131104 | tf_op jit(solution)/shard_map/ppermute | solution.py:32
  93.1 0.7 copy.67
  (56 shorter events, 8.5 us)
Async XLA Ops:
  0.0 22.2 %copy-start = (bf16[64,256]{1,0:T(8,128)(2,1)S(1)}, bf16[64,256]{1,0:T(8,128)(2,1)}, u32[]{:S(2)}) copy-start(bf16[64,256]{1,0:T(8,128)(2,1)} %param.15) | copy-start | bytes 98308
  0.9 5.9 %collective-permute-start = (bf16[64,8,128]{2,0,1:T(8,128)(2,1)S(1)}, bf16[64,8,128]{2,0,1:T(8,128)(2,1)S(1)}, u32[]{:S(2)}, u32[]{:S(2)}) collective-permute-start(bf16[64,8,128]{2,0,1:T(8,128)(2,1)S(1)} %bitcast.271), channel_id=1, source_target_pairs={{0,8},{8,16},{16,24},{24,32},{32,40},{40,48},{48,56},{56,64},{64,7... | collective-permute-start | bytes 393224 | tf_op jit(solution)/shard_map/ppermute | solution.py:32
  6.9 10.4 %collective-permute-start.1 = (bf16[1,64,1,128]{3,1,2,0:T(8,128)(2,1)S(1)}, bf16[1,64,1,128]{3,1,2,0:T(8,128)(2,1)S(1)}, u32[]{:S(2)}, u32[]{:S(2)}) collective-permute-start(bf16[1,64,1,128]{3,1,2,0:T(8,128)(2,1)S(1)} %get-tuple-element.158), channel_id=1, source_target_pairs={{0,1},{1,2},{2,3},{3,4},{4,5},{5,6},{6,7},{8,9},{9,10},{10,11},{11... | collective-permute-start | bytes 49160 | tf_op jit(solution)/shard_map/ppermute | solution.py:20
  11.1 6.2 %collective-permute-start.2 = (bf16[1,64,1,128]{3,1,2,0:T(8,128)(2,1)S(1)}, bf16[1,64,1,128]{3,1,2,0:T(8,128)(2,1)S(1)}, u32[]{:S(2)}, u32[]{:S(2)}) collective-permute-start(bf16[1,64,1,128]{3,1,2,0:T(8,128)(2,1)S(1)} %get-tuple-element.159), channel_id=1, source_target_pairs={{1,0},{2,1},{3,2},{4,3},{5,4},{6,5},{7,6},{9,8},{10,9},{11,10},{12... | collective-permute-start | bytes 49160 | tf_op jit(solution)/shard_map/ppermute | solution.py:22
  17.5 1.0 %copy-start.2 = (bf16[3,3,256,64]{2,3,1,0:T(8,128)(2,1)S(1)}, bf16[3,3,256,64]{2,3,1,0:T(8,128)(2,1)}, u32[]{:S(2)}) copy-start(bf16[3,3,256,64]{2,3,1,0:T(8,128)(2,1)} %param.13) | copy-start | bytes 884740
  19.8 0.9 copy-start.4
  21.8 0.9 copy-start.1
  21.8 1.0 %copy-start.3 = (bf16[64,8,128]{2,1,0:T(8,128)(2,1)S(1)}, bf16[64,8,128]{2,1,0:T(8,128)(2,1)}, u32[]{:S(2)}) copy-start(bf16[64,8,128]{2,1,0:T(8,128)(2,1)} %param.10) | copy-start | bytes 393220
  23.4 7.7 %collective-permute-start.3 = (bf16[1,256,1,128]{1,3,2,0:T(8,128)(2,1)S(1)}, bf16[1,256,1,128]{1,3,2,0:T(8,128)(2,1)S(1)}, u32[]{:S(2)}, u32[]{:S(2)}) collective-permute-start(bf16[1,256,1,128]{1,3,2,0:T(8,128)(2,1)S(1)} %get-tuple-element.128), channel_id=1, source_target_pairs={{0,1},{1,2},{2,3},{3,4},{4,5},{5,6},{6,7},{8,9},{9,10},{10,11},{11... | collective-permute-start | bytes 196616 | tf_op jit(solution)/shard_map/ppermute | solution.py:20
  27.6 6.5 %collective-permute-start.4 = (bf16[1,256,1,128]{1,3,2,0:T(8,128)(2,1)S(1)}, bf16[1,256,1,128]{1,3,2,0:T(8,128)(2,1)S(1)}, u32[]{:S(2)}, u32[]{:S(2)}) collective-permute-start(bf16[1,256,1,128]{1,3,2,0:T(8,128)(2,1)S(1)} %get-tuple-element.130), channel_id=1, source_target_pairs={{1,0},{2,1},{3,2},{4,3},{5,4},{6,5},{7,6},{9,8},{10,9},{11,10},{12... | collective-permute-start | bytes 196616 | tf_op jit(solution)/shard_map/ppermute | solution.py:22
  37.3 10.8 %collective-permute-start.5 = (bf16[64,8,128]{2,0,1:T(8,128)(2,1)S(1)}, bf16[64,8,128]{2,0,1:T(8,128)(2,1)S(1)}, u32[]{:S(2)}, u32[]{:S(2)}) collective-permute-start(bf16[64,8,128]{2,0,1:T(8,128)(2,1)S(1)} %fusion.38), channel_id=1, source_target_pairs={{8,0},{16,8},{24,16},{32,24},{40,32},{48,40},{56,48},{64,56},{72,6... | collective-permute-start | bytes 393224 | tf_op jit(solution)/shard_map/ppermute | solution.py:32
  48.1 4.2 %collective-permute-start.6 = (bf16[64,8,128]{2,0,1:T(8,128)(2,1)S(1)}, bf16[64,8,128]{2,0,1:T(8,128)(2,1)S(1)}, u32[]{:S(2)}, u32[]{:S(2)}) collective-permute-start(bf16[64,8,128]{2,0,1:T(8,128)(2,1)S(1)} %bitcast.268), channel_id=1, source_target_pairs={{0,8},{8,16},{16,24},{24,32},{32,40},{40,48},{48,56},{56,64},{64,7... | collective-permute-start | bytes 393224 | tf_op jit(solution)/shard_map/ppermute | solution.py:32
  52.3 7.7 %collective-permute-start.7 = (bf16[1,64,1,128]{3,1,2,0:T(8,128)(2,1)S(1)}, bf16[1,64,1,128]{3,1,2,0:T(8,128)(2,1)S(1)}, u32[]{:S(2)}, u32[]{:S(2)}) collective-permute-start(bf16[1,64,1,128]{3,1,2,0:T(8,128)(2,1)S(1)} %get-tuple-element.156), channel_id=1, source_target_pairs={{0,1},{1,2},{2,3},{3,4},{4,5},{5,6},{6,7},{8,9},{9,10},{10,11},{11... | collective-permute-start | bytes 49160 | tf_op jit(solution)/shard_map/ppermute | solution.py:20
  56.5 6.0 %collective-permute-start.8 = (bf16[1,64,1,128]{3,1,2,0:T(8,128)(2,1)S(1)}, bf16[1,64,1,128]{3,1,2,0:T(8,128)(2,1)S(1)}, u32[]{:S(2)}, u32[]{:S(2)}) collective-permute-start(bf16[1,64,1,128]{3,1,2,0:T(8,128)(2,1)S(1)} %get-tuple-element.157), channel_id=1, source_target_pairs={{1,0},{2,1},{3,2},{4,3},{5,4},{6,5},{7,6},{9,8},{10,9},{11,10},{12... | collective-permute-start | bytes 49160 | tf_op jit(solution)/shard_map/ppermute | solution.py:22
  67.3 7.0 %collective-permute-start.10 = (bf16[1,256,1,128]{1,3,2,0:T(8,128)(2,1)S(1)}, bf16[1,256,1,128]{1,3,2,0:T(8,128)(2,1)S(1)}, u32[]{:S(2)}, u32[]{:S(2)}) collective-permute-start(bf16[1,256,1,128]{1,3,2,0:T(8,128)(2,1)S(1)} %get-tuple-element.123), channel_id=1, source_target_pairs={{1,0},{2,1},{3,2},{4,3},{5,4},{6,5},{7,6},{9,8},{10,9},{11,10},{12... | collective-permute-start | bytes 196616 | tf_op jit(solution)/shard_map/ppermute | solution.py:22
  71.7 7.4 %collective-permute-start.9 = (bf16[1,256,1,128]{1,3,2,0:T(8,128)(2,1)S(1)}, bf16[1,256,1,128]{1,3,2,0:T(8,128)(2,1)S(1)}, u32[]{:S(2)}, u32[]{:S(2)}) collective-permute-start(bf16[1,256,1,128]{1,3,2,0:T(8,128)(2,1)S(1)} %get-tuple-element.122), channel_id=1, source_target_pairs={{0,1},{1,2},{2,3},{3,4},{4,5},{5,6},{6,7},{8,9},{9,10},{10,11},{11... | collective-permute-start | bytes 196616 | tf_op jit(solution)/shard_map/ppermute | solution.py:20
  82.3 10.7 %collective-permute-start.11 = (bf16[64,8,128]{2,0,1:T(8,128)(2,1)S(1)}, bf16[64,8,128]{2,0,1:T(8,128)(2,1)S(1)}, u32[]{:S(2)}, u32[]{:S(2)}) collective-permute-start(bf16[64,8,128]{2,0,1:T(8,128)(2,1)S(1)} %fusion.39), channel_id=1, source_target_pairs={{8,0},{16,8},{24,16},{32,24},{40,32},{48,40},{56,48},{64,56},{72,6... | collective-permute-start | bytes 393224 | tf_op jit(solution)/shard_map/ppermute | solution.py:32
where the time goes:
time: 94.4 us; the launch traced here: 93.9 us
  starting transfers between devices  47 us (50%)
  waiting for transfers between devices  18.8 us (20%)
  matrix products  13.6 us (14%)
  local copies, waits for them, and re-layouts  7.34 us (8%)
  other arithmetic  6.61 us (7%)
    ppermute x4, starting transfers between devices, from_behind(): return lax.ppermute(value, axis, pairs)  17 us
    ppermute x4, starting transfers between devices, with_halo(): lax.ppermute(tail, axis, [(i, (i + 1) % count) for i in range(ends)])  15.2 us
    ppermute x4, starting transfers between devices, with_halo(): lax.ppermute(head, axis, [((i + 1) % count, i) for i in range(ends)])  14.8 us
    ppermute x4, waiting for transfers between devices, from_behind(): return lax.ppermute(value, axis, pairs)  8.52 us
    dot_general x18, matrix products, advance_one_interval(): jnp.einsum('hc,clm->hlm', input_kernel_weight[row_step, col_step], shift_...  7.19 us
    scatter-add x2, other arithmetic, scatter_one(): jnp.zeros(grid_field.shape, jnp.float32).at[:, column_index].add(misfit)  5.53 us
    ppermute x4, waiting for transfers between devices, with_halo(): lax.ppermute(head, axis, [((i + 1) % count, i) for i in range(ends)])  5.5 us
    dot_general x18, matrix products, collect_rows(): jnp.einsum('hc,hlm->clm', input_kernel_weight[row_step, col_step], shift_...  5.18 us
  transfers between devices with their start and end apart: 12, of which 7 were waited for; matrix products, arithmetic and copies ran while one was open for 9% of the time, Pallas kernels for 0%

commit v1 on v0

v1 whole, which is shorter than its diff:
```python
import functools

import jax
import jax.numpy as jnp
from jax import lax
from jax.experimental import pallas as pl
from jax.experimental.pallas import tpu as pltpu
from jax.sharding import PartitionSpec as P

C = 64
HID = 256
ROWS = 8
LON = 128
OBS = 256
STEP = 0.3

F32 = jnp.float32
BF16 = jnp.bfloat16
VMEM = pl.BlockSpec(memory_space=pltpu.VMEM)

X_PART = 4 * C
BG_PART = X_PART + 2 * C
OBS_PART = BG_PART + 2 * C
PAYLOAD = OBS_PART + 16


def call(kernel, outs, scratch, flops, bytes_accessed):
    def run(*args):
        return pl.pallas_call(
            kernel,
            out_shape=outs,
            in_specs=[VMEM] * len(args),
            out_specs=jax.tree.map(lambda _: VMEM, outs),
            scratch_shapes=scratch,
            cost_estimate=pl.CostEstimate(
                flops=flops, bytes_accessed=bytes_accessed, transcendentals=0
            ),
            compiler_params=pltpu.CompilerParams(vmem_limit_bytes=48 << 20),
        )(*args)

    return run


def rows_of(ref, first, width=C):
    return ref[first * width : (first + 1) * width, :]


def observation_sums(values, low, high, row):
    cell = lax.broadcasted_iota(jnp.int32, (LON, OBS), 0)
    hit = jnp.where((low == cell) & (high == row), 1.0, 0.0).astype(BF16)
    return lax.dot_general(
        values, hit, (((1,), (1,)), ((), ())), preferred_element_type=F32
    )


def pack_kernel(x_ref, bg_ref, obs_ref, index_ref, own_ref, bg_rows_ref, up_ref, down_ref, xs, bs):
    xs[...] = x_ref[...].astype(F32)
    bs[...] = bg_ref[...].astype(F32)
    for row in range(ROWS):
        value = xs[:, row, :].astype(BF16)
        own_ref[row * C : (row + 1) * C, :] = value
        if row < 4:
            up_ref[row * C : (row + 1) * C, :] = value
        else:
            down_ref[(row - 4) * C : (row - 3) * C, :] = value
        ground = bs[:, row, :].astype(BF16)
        bg_rows_ref[row * C : (row + 1) * C, :] = ground
        if row < 2:
            up_ref[X_PART + row * C : X_PART + (row + 1) * C, :] = ground
        if row >= 6:
            down_ref[X_PART + (row - 6) * C : X_PART + (row - 5) * C, :] = ground
    local = index_ref[...] - lax.axis_index("lat") * (ROWS * LON)
    high = lax.shift_right_arithmetic(local, 7)
    low = local - high * LON
    place = lax.broadcasted_iota(jnp.int32, (16, LON), 0)
    coded = jnp.zeros((16, LON), jnp.int32)
    for spot, part in enumerate(
        (high[:, :LON], high[:, LON:], low[:, :LON], low[:, LON:])
    ):
        coded = jnp.where(place == spot, jnp.broadcast_to(part, (16, LON)), coded)
    coded = coded.astype(F32).astype(BF16)
    for ref in (up_ref, down_ref):
        ref[BG_PART : BG_PART + C, :] = obs_ref[:, :LON]
        ref[BG_PART + C : OBS_PART, :] = obs_ref[:, LON:]
        ref[OBS_PART:PAYLOAD, :] = coded


def extend_kernel(own_ref, bg_rows_ref, above_ref, below_ref, ext_ref, sent_ref, bg_ref):
    strip = lax.axis_index("lat")
    first = strip > 0
    last = strip < lax.axis_size("lat") - 1
    zero = jnp.zeros((X_PART, LON), BF16)
    above = jnp.where(first, above_ref[:X_PART, :], zero)
    below = jnp.where(last, below_ref[:X_PART, :], zero)
    ext_ref[:X_PART, :] = above
    ext_ref[X_PART : X_PART + ROWS * C, :] = own_ref[...]
    ext_ref[X_PART + ROWS * C :, :] = below
    sent_ref[: 3 * C, :] = above[C:, :]
    sent_ref[3 * C : 11 * C, :] = own_ref[...]
    sent_ref[11 * C :, :] = below[: 3 * C, :]
    bg_ref[: 2 * C, :] = above_ref[X_PART:BG_PART, :]
    bg_ref[2 * C : 10 * C, :] = bg_rows_ref[...]
    bg_ref[10 * C :, :] = below_ref[X_PART:BG_PART, :]


def roll_rows(state_ref, shifted, count):
    for row in range(count):
        at = slice(row * C, (row + 1) * C)
        value = state_ref[at, :]
        wide = value.astype(F32)
        shifted[0, at, :] = pltpu.roll(wide, 1, 1).astype(BF16)
        shifted[1, at, :] = value
        shifted[2, at, :] = pltpu.roll(wide, LON - 1, 1).astype(BF16)


def hidden(shifted, kernel_ref, bias, row):
    def stack(first):
        return jnp.concatenate(
            [shifted[b, first * C : (first + 3) * C, :] for b in range(3)], axis=0
        )

    cells = jnp.concatenate([stack(row), stack(row + 1)], axis=1)
    before = jnp.dot(kernel_ref[...], cells, preferred_element_type=F32) + bias
    return jnp.tanh(before).astype(BF16)


def side_by_side(ref, first):
    return jnp.concatenate([rows_of(ref, first), rows_of(ref, first + 1)], axis=1)


def store_pair(ref, first, value, width=C):
    ref[first * width : (first + 1) * width, :] = value[:, :LON]
    ref[(first + 1) * width : (first + 2) * width, :] = value[:, LON:]


def forward_part(count, state_ref, kernel_ref, bias_ref, out_weight_ref, active_ref, forecast_ref, shifted):
    roll_rows(state_ref, shifted, count + 2)
    bias = jnp.broadcast_to(bias_ref[...], (HID, 2 * LON))
    for row in range(0, count, 2):
        active = hidden(shifted, kernel_ref, bias, row)
        store_pair(active_ref, row, active, HID)
        step = jnp.dot(out_weight_ref[...], active, preferred_element_type=F32)
        centre = side_by_side(state_ref, row + 1).astype(F32)
        store_pair(forecast_ref, row, (centre + step).astype(BF16))


def forward_kernel(count, *refs):
    forward_part(count, *refs)


def sums_kernel(obs_ref, index_ref, above_ref, below_ref, sums_ref):
    ones = jnp.ones((16, OBS), BF16)

    def decode(ref):
        values = jnp.concatenate(
            [ref[BG_PART : BG_PART + C, :], ref[BG_PART + C : OBS_PART, :]], axis=1
        )
        coded = ref[OBS_PART:PAYLOAD, :].astype(F32).astype(jnp.int32)
        high = jnp.concatenate([coded[0:1, :], coded[1:2, :]], axis=1)
        low = jnp.concatenate([coded[2:3, :], coded[3:4, :]], axis=1)
        return jnp.concatenate([values, ones], axis=0), low, high

    local = index_ref[...] - lax.axis_index("lat") * (ROWS * LON)
    high = lax.shift_right_arithmetic(local, 7)
    own = (jnp.concatenate([obs_ref[...], ones], axis=0), local - high * LON, high)
    above = decode(above_ref)
    below = decode(below_ref)
    for place in range(12):
        source, row = (above, 6 + place) if place < 2 else (own, place - 2)
        if place >= 10:
            source, row = below, place - 10
        sums_ref[place] = observation_sums(*source, row)[:72, :]


def gradient_part(
    count, margin, prev_ref, next_ref, own_ref, own_first, active_ref, forecast_ref, bg_ref,
    bg_first, sums_ref, kernel_ref, back_ref, bias_ref, out_weight_ref, out_back_ref,
    emit, shifted, cot, resid, target,
):
    strip = lax.axis_index("lat")
    window = lax.axis_index("tm")
    top = -strip * ROWS
    bottom = (lax.axis_size("lat") - strip) * ROWS
    roll_rows(prev_ref, shifted, count + 2)
    bias = jnp.broadcast_to(bias_ref[...], (HID, 2 * LON))
    opening = window == 0
    for row in range(0, count, 2):
        active = hidden(shifted, kernel_ref, bias, row)
        step = jnp.dot(out_weight_ref[...], active, preferred_element_type=F32)
        centre = side_by_side(prev_ref, row + 1).astype(F32)
        guess = (centre + step).astype(BF16).astype(F32)
        ground = side_by_side(bg_ref, bg_first + row).astype(F32)
        guess = jnp.where(opening, ground, guess)
        own = side_by_side(own_ref, own_first + row).astype(F32)
        store_pair(resid, row, (own - guess).astype(BF16))
    for row in range(0, count + 2, 2):
        later = side_by_side(next_ref, row).astype(F32) - side_by_side(forecast_ref, row).astype(F32)
        later = later.astype(BF16)
        store_pair(target, row, later)
        projected = jnp.dot(out_back_ref[...], later, preferred_element_type=F32)
        for half in range(2):
            place = row + half - margin - 1
            inside = (place >= top) & (place < bottom)
            active = active_ref[(row + half) * HID : (row + half + 1) * HID, :].astype(F32)
            value = (1.0 - active * active) * projected[:, half * LON : (half + 1) * LON]
            value = jnp.where(inside, value, 0.0).astype(BF16)
            cot[(row + half) * HID : (row + half + 1) * HID, :] = value
    closing = window == lax.axis_size("tm") - 1
    for row in range(0, count, 2):
        cells = jnp.concatenate(
            [cot[row * HID : (row + 3) * HID, :], cot[(row + 1) * HID : (row + 4) * HID, :]], axis=1
        )
        spread = jnp.dot(back_ref[...], cells, preferred_element_type=F32)
        for half in range(2):
            lanes = slice(half * LON, (half + 1) * LON)
            pulled = (
                pltpu.roll(spread[:C, lanes], LON - 1, 1)
                + spread[C : 2 * C, lanes]
                + pltpu.roll(spread[2 * C :, lanes], 1, 1)
            )
            place = row + half
            later = rows_of(target, place + 1).astype(F32)
            adjoint = jnp.where(closing, 0.0, (later + pulled).astype(BF16).astype(F32))
            own = rows_of(own_ref, own_first + place).astype(F32)
            sums = sums_ref[2 - margin + place]
            innovation = sums[C : C + 1, :] * own - sums[:C, :]
            gradient = rows_of(resid, place).astype(F32) - adjoint + innovation
            value = own - STEP * gradient
            latitude = place - margin
            inside = (latitude >= top) & (latitude < bottom)
            emit(place, jnp.where(inside, value, 0.0) if margin else value)


def first_kernel(
    prev_ref, next_ref, ext_ref, active_ref, forecast_ref, bg_ref, sums_ref, kernel_ref, back_ref,
    bias_ref, out_weight_ref, out_back_ref, state_ref, sent_ref, shifted, cot, resid, target,
):
    def emit(place, value):
        value = value.astype(BF16)
        state_ref[place * C : (place + 1) * C, :] = value
        if 1 <= place < 11:
            sent_ref[(place - 1) * C : place * C, :] = value

    gradient_part(
        12, 2, prev_ref, next_ref, ext_ref, 2, active_ref, forecast_ref, bg_ref, 0, sums_ref,
        kernel_ref, back_ref, bias_ref, out_weight_ref, out_back_ref, emit, shifted, cot, resid,
        target,
    )


def second_kernel(
    prev_ref, next_ref, state_ref, active_ref, forecast_ref, bg_ref, sums_ref, kernel_ref, back_ref,
    bias_ref, out_weight_ref, out_back_ref, out_ref, shifted, cot, resid, target, wide,
):
    def emit(place, value):
        wide[:, place, :] = value

    gradient_part(
        8, 0, prev_ref, next_ref, state_ref, 2, active_ref, forecast_ref, bg_ref, 2, sums_ref,
        kernel_ref, back_ref, bias_ref, out_weight_ref, out_back_ref, emit, shifted, cot, resid,
        target,
    )
    out_ref[...] = wide[...].astype(BF16)


def ring(value, axis, by):
    count = lax.axis_size(axis)
    return lax.ppermute(value, axis, [(i, (i + by) % count) for i in range(count)])


def shape(rows, dtype=BF16):
    return jax.ShapeDtypeStruct((rows, LON), dtype)


def gradient_scratch(count):
    return [
        pltpu.VMEM((3, (count + 2) * C, LON), BF16),
        pltpu.VMEM(((count + 2) * HID, LON), BF16),
        pltpu.VMEM((count * C, LON), BF16),
        pltpu.VMEM(((count + 2) * C, LON), BF16),
    ]


def on_device(
    window_snapshots, background, obs_values, obs_index, input_kernel_weight, hidden_bias_vector,
    output_pointwise_weight,
):
    own, bg_rows, up, down = call(
        pack_kernel,
        (shape(ROWS * C), shape(ROWS * C), shape(PAYLOAD), shape(PAYLOAD)),
        [pltpu.VMEM((C, ROWS, LON), F32), pltpu.VMEM((C, ROWS, LON), F32)],
        0, 1 << 20,
    )(window_snapshots[0], background, obs_values[0], obs_index)
    below = ring(up, "lat", -1)
    above = ring(down, "lat", 1)

    forward_weight = jnp.transpose(input_kernel_weight, (2, 1, 0, 3)).reshape(HID, 9 * C)
    back_weight = jnp.transpose(input_kernel_weight[::-1], (1, 3, 0, 2)).reshape(3 * C, 3 * HID)
    bias = hidden_bias_vector[:, None]
    out_weight = output_pointwise_weight
    out_back = output_pointwise_weight.T

    ext, sent, ground = call(
        extend_kernel, (shape(16 * C), shape(14 * C), shape(12 * C)), [], 0, 1 << 20
    )(own, bg_rows, above, below)
    earlier = ring(sent, "tm", 1)
    later = ring(sent, "tm", -1)
    sums = call(
        sums_kernel, jax.ShapeDtypeStruct((12, 72, LON), F32), [], 12 * 2 * 80 * OBS * LON, 1 << 20
    )(obs_values[0], obs_index, above, below)
    active, forecast = call(
        functools.partial(forward_kernel, 14),
        (shape(14 * HID), shape(14 * C)),
        [pltpu.VMEM((3, 16 * C, LON), BF16)],
        14 * 2 * LON * HID * 10 * C, 2 << 20,
    )(ext, forward_weight, bias, out_weight)
    state, sent = call(
        first_kernel,
        (shape(12 * C), shape(10 * C)),
        gradient_scratch(12),
        28 * 2 * LON * HID * 10 * C, 2 << 20,
    )(
        earlier, later, ext, active, forecast, ground, sums, forward_weight, back_weight, bias,
        out_weight, out_back,
    )
    earlier = ring(sent, "tm", 1)
    later = ring(sent, "tm", -1)
    active, forecast = call(
        functools.partial(forward_kernel, 10),
        (shape(10 * HID), shape(10 * C)),
        [pltpu.VMEM((3, 12 * C, LON), BF16)],
        10 * 2 * LON * HID * 10 * C, 2 << 20,
    )(state, forward_weight, bias, out_weight)
    analysis = call(
        second_kernel,
        jax.ShapeDtypeStruct((C, ROWS, LON), BF16),
        gradient_scratch(8) + [pltpu.VMEM((C, ROWS, LON), F32)],
        20 * 2 * LON * HID * 10 * C, 2 << 20,
    )(
        earlier, later, state, active, forecast, ground, sums, forward_weight, back_weight, bias,
        out_weight, out_back,
    )
    return analysis[None]


def solution(mesh):
    placed = (
        P("tm", None, "lat", None),
        P(None, "lat", None),
        P("tm", None, "lat"),
        P("tm", "lat"),
        P(),
        P(),
        P(),
    )
    return jax.shard_map(
        on_device, mesh=mesh, in_specs=placed, out_specs=P("tm", None, "lat", None), check_vma=False
    )
```

time: 94.4 us -> 43.4 us (0.46)
  the two profiles are of different devices: /device:TPU:43 before, /device:TPU:0 now
where the time goes in v1:
time: 43.4 us; the launch traced here: 43.1 us
  waiting for transfers between devices  13.6 us (31%)
  Pallas kernels  12.3 us (28%)
  starting transfers between devices  11.8 us (27%)
  local copies, waits for them, and re-layouts  5.26 us (12%)
    ppermute x6, waiting for transfers between devices, ring(): lax.ppermute(value, axis, [(i, (i + by) % count) for i in range(count)])  13.6 us
    pallas_call x7, Pallas kernels, run(): pl.pallas_call(kernel, out_shape=outs, in_specs=[VMEM] * len(args), out_s...  12.3 us
    ppermute x6, starting transfers between devices, ring(): lax.ppermute(value, axis, [(i, (i + by) % count) for i in range(count)])  11.8 us
    unnamed x19, local copies, waits for them, and re-layouts  4.65 us
  transfers between devices with their start and end apart: 6, of which 5 were waited for; matrix products, arithmetic and copies ran while one was open for 2% of the time, Pallas kernels for 12%

profile of v1, /device:TPU:0, one launch (start us, length us, event | category | flops | bytes accessed | tf_op | source)
XLA Modules:
  0.0 43.1 jit_solution(14219887145074744184)
XLA Ops:
  0.0 0.0 copy-start.5
  0.0 0.7 %copy-done.5 = s32[1,256]{1,0:T(1,128)S(1)} copy-done((s32[1,256]{1,0:T(1,128)S(1)}, s32[1,256]{1,0:T(1,128)}, u32[]{:S(2)}) %copy-start.5) | copy-done | bytes 1048
  0.7 0.0 copy-start
  0.7 0.8 %copy-done = bf16[1,64,256]{2,1,0:T(8,128)(2,1)S(1)} copy-done((bf16[1,64,256]{2,1,0:T(8,128)(2,1)S(1)}, bf16[1,64,256]{2,1,0:T(8,128)(2,1)}, u32[]{:S(2)}) %copy-start) | copy-done | bytes 32792
  1.4 0.0 copy-start.2
  1.4 0.9 %copy-done.2 = bf16[1,64,8,128]{3,2,1,0:T(8,128)(2,1)S(1)} copy-done((bf16[1,64,8,128]{3,2,1,0:T(8,128)(2,1)S(1)}, bf16[1,64,8,128]{3,2,1,0:T(8,128)(2,1)}, u32[]{:S(2)}) %copy-start.2) | copy-done | bytes 131096
  2.3 0.0 copy-start.3
  2.3 0.9 %copy-done.3 = bf16[64,8,128]{2,1,0:T(8,128)(2,1)S(1)} copy-done((bf16[64,8,128]{2,1,0:T(8,128)(2,1)S(1)}, bf16[64,8,128]{2,1,0:T(8,128)(2,1)}, u32[]{:S(2)}) %copy-start.3) | copy-done | bytes 131096
  3.2 0.7 %shard_map.73 = (bf16[512,128]{1,0:T(8,128)(2,1)S(1)}, bf16[512,128]{1,0:T(8,128)(2,1)S(1)}, bf16[528,128]{1,0:T(8,128)(2,1)S(1)}, bf16[528,128]{1,0:T(8,128)(2,1)S(1)}) custom-call(bf16[64,8,128]{2,1,0:T(8,128)(2,1)S(1)} %bitcast.17, bf16[64,8,128]{2,1,0:T(8,128)(2,1)S(1)} %copy-done.3, bf16[64,256]{1,0:T(8,128)(2,1)S(1)} %bitcast.15, s32[1,256]{1,0:T(1,128)S(1)} %copy-done.5), custom_call_target="tpu_custom_call" | custom-call | bytes 1048576 | tf_op jit(solution)/shard_map/pallas_call | solution.py:29
  3.9 3.4 %collective-permute-start = (bf16[528,128]{1,0:T(8,128)(2,1)S(1)}, bf16[528,128]{1,0:T(8,128)(2,1)S(1)}, u32[]{:S(2)}, u32[]{:S(2)}) collective-permute-start(bf16[528,128]{1,0:T(8,128)(2,1)S(1)} %get-tuple-element.20), channel_id=1, source_target_pairs={{0,1},{1,2},{2,3},{3,4},{4,5},{5,6},{6,7},{7,0},{8,9},{9,10},{10,1... | collective-permute-start | bytes 405512 | tf_op jit(solution)/shard_map/ppermute | solution.py:268
  7.3 2.3 %collective-permute-start.1 = (bf16[528,128]{1,0:T(8,128)(2,1)S(1)}, bf16[528,128]{1,0:T(8,128)(2,1)S(1)}, u32[]{:S(2)}, u32[]{:S(2)}) collective-permute-start(bf16[528,128]{1,0:T(8,128)(2,1)S(1)} %get-tuple-element.21), channel_id=1, source_target_pairs={{0,7},{1,0},{2,1},{3,2},{4,3},{5,4},{6,5},{7,6},{8,15},{9,8},{10,9... | collective-permute-start | bytes 405512 | tf_op jit(solution)/shard_map/ppermute | solution.py:268
  9.6 3.5 %collective-permute-done.above_ref = bf16[528,128]{1,0:T(8,128)(2,1)S(1)} collective-permute-done((bf16[528,128]{1,0:T(8,128)(2,1)S(1)}, bf16[528,128]{1,0:T(8,128)(2,1)S(1)}, u32[]{:S(2)}, u32[]{:S(2)}) %collective-permute-start) | collective-permute-done | bytes 135200 | tf_op jit(solution)/shard_map/ppermute | solution.py:268
  13.2 2.8 %collective-permute-done.1.below_ref = bf16[528,128]{1,0:T(8,128)(2,1)S(1)} collective-permute-done((bf16[528,128]{1,0:T(8,128)(2,1)S(1)}, bf16[528,128]{1,0:T(8,128)(2,1)S(1)}, u32[]{:S(2)}, u32[]{:S(2)}) %collective-permute-start.1) | collective-permute-done | bytes 135200 | tf_op jit(solution)/shard_map/ppermute | solution.py:268
  16.0 0.0 copy-start.4
  16.0 0.0 copy-start.6
  16.0 0.1 shard_map.74
  16.1 4.5 %collective-permute-start.3 = (bf16[896,128]{1,0:T(8,128)(2,1)S(1)}, bf16[896,128]{1,0:T(8,128)(2,1)S(1)}, u32[]{:S(2)}, u32[]{:S(2)}) collective-permute-start(bf16[896,128]{1,0:T(8,128)(2,1)S(1)} %get-tuple-element.22), channel_id=1, source_target_pairs={{0,120},{8,0},{16,8},{24,16},{32,24},{40,32},{48,40},{56,48},{64,5... | collective-permute-start | bytes 688136 | tf_op jit(solution)/shard_map/ppermute | solution.py:268
  20.6 0.0 collective-permute-start.2
  20.6 0.0 copy-done.4
  20.6 0.1 copy.15
  20.7 0.0 copy-start.7
  20.7 0.7 %copy-done.7 = f32[256]{0:T(256)S(1)} copy-done((f32[256]{0:T(256)S(1)}, f32[256]{0:T(256)}, u32[]{:S(2)}) %copy-start.7) | copy-done | bytes 1048
  21.4 0.1 copy.13.refs_2_.bias_ref
  21.5 0.0 copy-done.6
  21.6 0.3 copy.14
  21.9 0.0 copy-start.1
  21.9 0.2 copy.12.refs_1_.kernel_ref
  22.1 0.5 %copy-done.1 = bf16[1,64,256]{2,1,0:T(8,128)(2,1)S(1)} copy-done((bf16[1,64,256]{2,1,0:T(8,128)(2,1)S(1)}, bf16[1,64,256]{2,1,0:T(8,128)(2,1)}, u32[]{:S(2)}) %copy-start.1) | copy-done | bytes 32792
  22.7 0.4 shard_map.76.sums_ref
  23.1 2.7 %shard_map.75 = (bf16[3584,128]{1,0:T(8,128)(2,1)S(1)}, bf16[896,128]{1,0:T(8,128)(2,1)S(1)}) custom-call(bf16[1024,128]{1,0:T(8,128)(2,1)S(1)} %get-tuple-element.23.refs_0_.ext_ref, bf16[256,576]{1,0:T(8,128)(2,1)S(1)} %copy.12.refs_1_.kernel_ref, f32[256,1]{1,0:T(8,128)S(1)} %copy.13.refs_2_.bias_ref, bf16[64,256]{1,0:T(8,128)(2,1)S(1)} %copy-done.4), custom_call_target="tpu_custom_call" | custom-call | flops 587202560 | bytes 2097152 | tf_op jit(solution)/shard_map/pallas_call | solution.py:29
  25.8 0.0 collective-permute-done.3.next_ref
  25.8 2.4 %collective-permute-done.2.prev_ref = bf16[896,128]{1,0:T(8,128)(2,1)S(1)} collective-permute-done((bf16[896,128]{1,0:T(8,128)(2,1)S(1)}, bf16[896,128]{1,0:T(8,128)(2,1)S(1)}, u32[]{:S(2)}, u32[]{:S(2)}) %collective-permute-start.2) | collective-permute-done | bytes 229408 | tf_op jit(solution)/shard_map/ppermute | solution.py:268
  28.1 3.4 %shard_map.77 = (bf16[768,128]{1,0:T(8,128)(2,1)S(1)}, bf16[640,128]{1,0:T(8,128)(2,1)S(1)}) custom-call(bf16[896,128]{1,0:T(8,128)(2,1)S(1)} %collective-permute-done.2.prev_ref, bf16[896,128]{1,0:T(8,128)(2,1)S(1)} %collective-permute-done.3.next_ref, bf16[1024,128]{1,0:T(8,128)(2,1)S(1)} %get-tuple-element.23.refs_0_.ext_ref, ...), custom_call_target="tpu_custom_call" | custom-call | flops 1174405120 | bytes 2097152 | tf_op jit(solution)/shard_map/pallas_call | solution.py:29
  31.5 1.6 %collective-permute-start.5 = (bf16[640,128]{1,0:T(8,128)(2,1)S(1)}, bf16[640,128]{1,0:T(8,128)(2,1)S(1)}, u32[]{:S(2)}, u32[]{:S(2)}) collective-permute-start(bf16[640,128]{1,0:T(8,128)(2,1)S(1)} %get-tuple-element.27), channel_id=1, source_target_pairs={{0,120},{8,0},{16,8},{24,16},{32,24},{40,32},{48,40},{56,48},{64,5... | collective-permute-start | bytes 491528 | tf_op jit(solution)/shard_map/ppermute | solution.py:268
  33.1 0.0 collective-permute-start.4
  33.1 1.9 %shard_map.78 = (bf16[2560,128]{1,0:T(8,128)(2,1)S(1)}, bf16[640,128]{1,0:T(8,128)(2,1)S(1)}) custom-call(bf16[768,128]{1,0:T(8,128)(2,1)S(1)} %get-tuple-element.28.refs_0_.state_ref, bf16[256,576]{1,0:T(8,128)(2,1)S(1)} %copy.12.refs_1_.kernel_ref, f32[256,1]{1,0:T(8,128)S(1)} %copy.13.refs_2_.bias_ref, bf16[64,256]{1,0:T(8,128)(2,1)S(1)} %copy-done.4), custom_call_target="tpu_custom_call" | custom-call | flops 419430400 | bytes 2097152 | tf_op jit(solution)/shard_map/pallas_call | solution.py:29
  35.0 1.0 %collective-permute-done.5.next_ref = bf16[640,128]{1,0:T(8,128)(2,1)S(1)} collective-permute-done((bf16[640,128]{1,0:T(8,128)(2,1)S(1)}, bf16[640,128]{1,0:T(8,128)(2,1)S(1)}, u32[]{:S(2)}, u32[]{:S(2)}) %collective-permute-start.5) | collective-permute-done | bytes 163872 | tf_op jit(solution)/shard_map/ppermute | solution.py:268
  36.0 3.9 %collective-permute-done.4.prev_ref = bf16[640,128]{1,0:T(8,128)(2,1)S(1)} collective-permute-done((bf16[640,128]{1,0:T(8,128)(2,1)S(1)}, bf16[640,128]{1,0:T(8,128)(2,1)S(1)}, u32[]{:S(2)}, u32[]{:S(2)}) %collective-permute-start.4) | collective-permute-done | bytes 163872 | tf_op jit(solution)/shard_map/ppermute | solution.py:268
  40.0 3.1 %shard_map.79 = bf16[64,8,128]{2,1,0:T(8,128)(2,1)} custom-call(bf16[640,128]{1,0:T(8,128)(2,1)S(1)} %collective-permute-done.4.prev_ref, bf16[640,128]{1,0:T(8,128)(2,1)S(1)} %collective-permute-done.5.next_ref, bf16[768,128]{1,0:T(8,128)(2,1)S(1)} %get-tuple-element.28.refs_0_.state_ref, bf16[2560,128]{1,0:T(8,128)(2,1)S(1)} %get-tuple-element.29.active_ref, ...), custom_call_target="tpu_custom_call" | custom-call | flops 838860800 | bytes 2097152 | tf_op jit(solution)/shard_map/pallas_call | solution.py:29
  (3 shorter events, 0.1 us)
Async XLA Ops:
  0.0 0.7 %copy-start.5 = (s32[1,256]{1,0:T(1,128)S(1)}, s32[1,256]{1,0:T(1,128)}, u32[]{:S(2)}) copy-start(s32[1,256]{1,0:T(1,128)} %index_ref.3) | copy-start | bytes 3076
  0.7 0.8 %copy-start = (bf16[1,64,256]{2,1,0:T(8,128)(2,1)S(1)}, bf16[1,64,256]{2,1,0:T(8,128)(2,1)}, u32[]{:S(2)}) copy-start(bf16[1,64,256]{2,1,0:T(8,128)(2,1)} %param.9) | copy-start | bytes 98308
  1.4 0.9 %copy-start.2 = (bf16[1,64,8,128]{3,2,1,0:T(8,128)(2,1)S(1)}, bf16[1,64,8,128]{3,2,1,0:T(8,128)(2,1)}, u32[]{:S(2)}) copy-start(bf16[1,64,8,128]{3,2,1,0:T(8,128)(2,1)} %param.7) | copy-start | bytes 393220
  2.3 0.9 %copy-start.3 = (bf16[64,8,128]{2,1,0:T(8,128)(2,1)S(1)}, bf16[64,8,128]{2,1,0:T(8,128)(2,1)}, u32[]{:S(2)}) copy-start(bf16[64,8,128]{2,1,0:T(8,128)(2,1)} %bg_ref.1) | copy-start | bytes 393220
  3.9 9.3 %collective-permute-start = (bf16[528,128]{1,0:T(8,128)(2,1)S(1)}, bf16[528,128]{1,0:T(8,128)(2,1)S(1)}, u32[]{:S(2)}, u32[]{:S(2)}) collective-permute-start(bf16[528,128]{1,0:T(8,128)(2,1)S(1)} %get-tuple-element.20), channel_id=1, source_target_pairs={{0,1},{1,2},{2,3},{3,4},{4,5},{5,6},{6,7},{7,0},{8,9},{9,10},{10,1... | collective-permute-start | bytes 405512 | tf_op jit(solution)/shard_map/ppermute | solution.py:268
  7.3 8.7 %collective-permute-start.1 = (bf16[528,128]{1,0:T(8,128)(2,1)S(1)}, bf16[528,128]{1,0:T(8,128)(2,1)S(1)}, u32[]{:S(2)}, u32[]{:S(2)}) collective-permute-start(bf16[528,128]{1,0:T(8,128)(2,1)S(1)} %get-tuple-element.21), channel_id=1, source_target_pairs={{0,7},{1,0},{2,1},{3,2},{4,3},{5,4},{6,5},{7,6},{8,15},{9,8},{10,9... | collective-permute-start | bytes 405512 | tf_op jit(solution)/shard_map/ppermute | solution.py:268
  16.0 4.6 %copy-start.4 = (bf16[64,256]{1,0:T(8,128)(2,1)S(1)}, bf16[64,256]{1,0:T(8,128)(2,1)}, u32[]{:S(2)}) copy-start(bf16[64,256]{1,0:T(8,128)(2,1)} %out_weight_ref.3) | copy-start | bytes 98308
  16.0 5.6 %copy-start.6 = (bf16[3,3,256,64]{2,3,1,0:T(8,128)(2,1)S(1)}, bf16[3,3,256,64]{2,3,1,0:T(8,128)(2,1)}, u32[]{:S(2)}) copy-start(bf16[3,3,256,64]{2,3,1,0:T(8,128)(2,1)} %param.11) | copy-start | bytes 884740
  16.1 9.7 %collective-permute-start.3 = (bf16[896,128]{1,0:T(8,128)(2,1)S(1)}, bf16[896,128]{1,0:T(8,128)(2,1)S(1)}, u32[]{:S(2)}, u32[]{:S(2)}) collective-permute-start(bf16[896,128]{1,0:T(8,128)(2,1)S(1)} %get-tuple-element.22), channel_id=1, source_target_pairs={{0,120},{8,0},{16,8},{24,16},{32,24},{40,32},{48,40},{56,48},{64,5... | collective-permute-start | bytes 688136 | tf_op jit(solution)/shard_map/ppermute | solution.py:268
  20.6 7.6 %collective-permute-start.2 = (bf16[896,128]{1,0:T(8,128)(2,1)S(1)}, bf16[896,128]{1,0:T(8,128)(2,1)S(1)}, u32[]{:S(2)}, u32[]{:S(2)}) collective-permute-start(bf16[896,128]{1,0:T(8,128)(2,1)S(1)} %get-tuple-element.22), channel_id=1, source_target_pairs={{0,8},{8,16},{16,24},{24,32},{32,40},{40,48},{48,56},{56,64},{64,7... | collective-permute-start | bytes 688136 | tf_op jit(solution)/shard_map/ppermute | solution.py:268
  20.7 0.7 %copy-start.7 = (f32[256]{0:T(256)S(1)}, f32[256]{0:T(256)}, u32[]{:S(2)}) copy-start(f32[256]{0:T(256)} %param.12) | copy-start | bytes 3076
  21.9 0.8 %copy-start.1 = (bf16[1,64,256]{2,1,0:T(8,128)(2,1)S(1)}, bf16[1,64,256]{2,1,0:T(8,128)(2,1)}, u32[]{:S(2)}) copy-start(bf16[1,64,256]{2,1,0:T(8,128)(2,1)} %param.9) | copy-start | bytes 98308
  31.5 4.5 %collective-permute-start.5 = (bf16[640,128]{1,0:T(8,128)(2,1)S(1)}, bf16[640,128]{1,0:T(8,128)(2,1)S(1)}, u32[]{:S(2)}, u32[]{:S(2)}) collective-permute-start(bf16[640,128]{1,0:T(8,128)(2,1)S(1)} %get-tuple-element.27), channel_id=1, source_target_pairs={{0,120},{8,0},{16,8},{24,16},{32,24},{40,32},{48,40},{56,48},{64,5... | collective-permute-start | bytes 491528 | tf_op jit(solution)/shard_map/ppermute | solution.py:268
  33.1 6.9 %collective-permute-start.4 = (bf16[640,128]{1,0:T(8,128)(2,1)S(1)}, bf16[640,128]{1,0:T(8,128)(2,1)S(1)}, u32[]{:S(2)}, u32[]{:S(2)}) collective-permute-start(bf16[640,128]{1,0:T(8,128)(2,1)S(1)} %get-tuple-element.27), channel_id=1, source_target_pairs={{0,8},{8,16},{16,24},{24,32},{32,40},{40,48},{48,56},{56,64},{64,7... | collective-permute-start | bytes 491528 | tf_op jit(solution)/shard_map/ppermute | solution.py:268

commit v2 on v1

v2 whole, which is shorter than its diff:
```python
import functools

import jax
import jax.numpy as jnp
from jax import lax
from jax.experimental import pallas as pl
from jax.experimental.pallas import tpu as pltpu
from jax.sharding import PartitionSpec as P

C = 64
HID = 256
ROWS = 8
LON = 128
OBS = 256
STEP = 0.3

F32 = jnp.float32
BF16 = jnp.bfloat16
VMEM = pl.BlockSpec(memory_space=pltpu.VMEM)

X_PART = 4 * C
PAYLOAD = X_PART + 2 * C


def call(kernel, outs, scratch, flops, bytes_accessed, spec=VMEM, grant=48 << 20):
    def run(*args):
        return pl.pallas_call(
            kernel,
            out_shape=outs,
            in_specs=[spec] * len(args),
            out_specs=jax.tree.map(lambda _: VMEM, outs),
            scratch_shapes=scratch,
            cost_estimate=pl.CostEstimate(
                flops=flops, bytes_accessed=bytes_accessed, transcendentals=0
            ),
            compiler_params=pltpu.CompilerParams(vmem_limit_bytes=grant),
        )(*args)

    return run


def rows_of(ref, first, width=C):
    return ref[first * width : (first + 1) * width, :]


def local_cells(index):
    local = index - lax.axis_index("lat") * (ROWS * LON)
    high = lax.shift_right_arithmetic(local, 7)
    return local - high * LON, high


def with_ones(values):
    return jnp.concatenate([values, jnp.ones((16, OBS), BF16)], axis=0)


def observation_sums(values, low, high, row):
    cell = lax.broadcasted_iota(jnp.int32, (LON, OBS), 0)
    hit = jnp.where((low == cell) & (high == row), 1.0, 0.0).astype(BF16)
    return lax.dot_general(
        values, hit, (((1,), (1,)), ((), ())), preferred_element_type=F32
    )


def innovation_of(sums, own):
    return sums[C : C + 1, :] * own - sums[:C, :]


def pack_kernel(
    x_hbm, bg_hbm, obs_hbm, index_hbm, own_ref, bg_rows_ref, up_ref, down_ref,
    x_ref, bg_ref, obs_ref, index_ref, xs, bs, sems,
):
    copies = [
        pltpu.make_async_copy(source, target, sems.at[place])
        for place, (source, target) in enumerate(
            ((x_hbm, x_ref), (obs_hbm, obs_ref), (index_hbm, index_ref), (bg_hbm, bg_ref))
        )
    ]
    for copy in copies:
        copy.start()
    copies[0].wait()
    xs[...] = x_ref[...].astype(F32)
    for row in range(ROWS):
        value = xs[:, row, :].astype(BF16)
        own_ref[row * C : (row + 1) * C, :] = value
        if row < 4:
            up_ref[row * C : (row + 1) * C, :] = value
        else:
            down_ref[(row - 4) * C : (row - 3) * C, :] = value
    copies[1].wait()
    copies[2].wait()
    low, high = local_cells(index_ref[...])
    values = with_ones(obs_ref[...])
    sums = [observation_sums(values, low, high, row) for row in (0, 1, 6, 7)]
    copies[3].wait()
    bs[...] = bg_ref[...].astype(F32)
    opening = lax.axis_index("tm") == 0
    for row in range(ROWS):
        ground = bs[:, row, :]
        bg_rows_ref[row * C : (row + 1) * C, :] = ground.astype(BF16)
        if row < 2 or row >= 6:
            own = xs[:, row, :]
            edge = innovation_of(sums[row if row < 2 else row - 4], own)
            edge = edge + jnp.where(opening, own - ground, 0.0)
            ref, place = (up_ref, row) if row < 2 else (down_ref, row - 6)
            ref[X_PART + place * C : X_PART + (place + 1) * C, :] = edge.astype(BF16)


def extend_kernel(own_ref, above_ref, below_ref, ext_ref, sent_ref):
    strip = lax.axis_index("lat")
    first = strip > 0
    last = strip < lax.axis_size("lat") - 1
    zero = jnp.zeros((X_PART, LON), BF16)
    above = jnp.where(first, above_ref[:X_PART, :], zero)
    below = jnp.where(last, below_ref[:X_PART, :], zero)
    ext_ref[:X_PART, :] = above
    ext_ref[X_PART : X_PART + ROWS * C, :] = own_ref[...]
    ext_ref[X_PART + ROWS * C :, :] = below
    sent_ref[: 3 * C, :] = above[C:, :]
    sent_ref[3 * C : 11 * C, :] = own_ref[...]
    sent_ref[11 * C :, :] = below[: 3 * C, :]


def roll_rows(state_ref, shifted, count):
    for row in range(count):
        at = slice(row * C, (row + 1) * C)
        value = state_ref[at, :]
        wide = value.astype(F32)
        shifted[0, at, :] = pltpu.roll(wide, 1, 1).astype(BF16)
        shifted[1, at, :] = value
        shifted[2, at, :] = pltpu.roll(wide, LON - 1, 1).astype(BF16)


def hidden(shifted, kernel_ref, bias, row):
    def stack(first):
        return jnp.concatenate(
            [
                shifted[b, (first + a) * C : (first + a + 1) * C, :]
                for a in range(3)
                for b in range(3)
            ],
            axis=0,
        )

    cells = jnp.concatenate([stack(row), stack(row + 1)], axis=1)
    before = jnp.dot(kernel_ref[...], cells, preferred_element_type=F32) + bias
    return jnp.tanh(before).astype(BF16)


def side_by_side(ref, first):
    return jnp.concatenate([rows_of(ref, first), rows_of(ref, first + 1)], axis=1)


def store_pair(ref, first, value, width=C):
    ref[first * width : (first + 1) * width, :] = value[:, :LON]
    ref[(first + 1) * width : (first + 2) * width, :] = value[:, LON:]


def forward_part(count, state_ref, kernel_ref, bias_ref, out_weight_ref, active_ref, forecast_ref, shifted):
    roll_rows(state_ref, shifted, count + 2)
    bias = jnp.concatenate([bias_ref[...], bias_ref[...]], axis=1)
    for row in range(0, count, 2):
        active = hidden(shifted, kernel_ref, bias, row)
        store_pair(active_ref, row, active, HID)
        step = jnp.dot(out_weight_ref[...], active, preferred_element_type=F32)
        centre = side_by_side(state_ref, row + 1).astype(F32)
        store_pair(forecast_ref, row, (centre + step).astype(BF16))


def prepare_kernel(
    obs_ref, index_ref, kernel_ref, bias_ref, out_weight_ref, sums_ref, forward_ref, back_ref,
    wide_bias_ref, out_back_ref,
):
    low, high = local_cells(index_ref[...])
    values = with_ones(obs_ref[...])
    for row in range(ROWS):
        sums_ref[row] = observation_sums(values, low, high, row)[:72, :]
    forward_ref[...] = kernel_ref[...].T
    out_back_ref[...] = out_weight_ref[...].T
    wide_bias_ref[...] = jnp.broadcast_to(bias_ref[...], (LON, HID)).T
    for a in range(3):
        back_ref[:, a * HID : (a + 1) * HID] = kernel_ref[(2 - a) * 3 * C : (3 - a) * 3 * C, :]


def residual_kernel(
    count, margin, prev_ref, own_ref, bg_ref, kernel_ref, bias_ref, out_weight_ref, resid_ref, shifted
):
    roll_rows(prev_ref, shifted, count + 2)
    bias = jnp.concatenate([bias_ref[...], bias_ref[...]], axis=1)
    opening = lax.axis_index("tm") == 0
    for row in range(0, count, 2):
        active = hidden(shifted, kernel_ref, bias, row)
        step = jnp.dot(out_weight_ref[...], active, preferred_element_type=F32)
        centre = side_by_side(prev_ref, row + 1).astype(F32)
        guess = (centre + step).astype(BF16).astype(F32)
        own = side_by_side(own_ref, row + 2).astype(F32)
        latitude = row - margin
        known = side_by_side(bg_ref, latitude).astype(F32) if 0 <= latitude < ROWS else own
        guess = jnp.where(opening, known, guess)
        store_pair(resid_ref, row, (own - guess).astype(BF16))


def gradient_part(
    count, margin, next_ref, own_ref, active_ref, forecast_ref, resid_ref, innovation, back_ref,
    out_back_ref, emit, cot, target,
):
    strip = lax.axis_index("lat")
    top = -strip * ROWS
    bottom = (lax.axis_size("lat") - strip) * ROWS
    for row in range(0, count + 2, 2):
        later = side_by_side(next_ref, row).astype(F32) - side_by_side(forecast_ref, row).astype(F32)
        later = later.astype(BF16)
        store_pair(target, row, later)
        projected = jnp.dot(out_back_ref[...], later, preferred_element_type=F32)
        for half in range(2):
            place = row + half - margin - 1
            active = rows_of(active_ref, row + half, HID).astype(F32)
            value = (1.0 - active * active) * projected[:, half * LON : (half + 1) * LON]
            if not 0 <= place < ROWS:
                value = jnp.where((place >= top) & (place < bottom), value, 0.0)
            cot[(row + half) * HID : (row + half + 1) * HID, :] = value.astype(BF16)
    closing = lax.axis_index("tm") == lax.axis_size("tm") - 1
    for row in range(0, count, 2):
        cells = jnp.concatenate(
            [cot[row * HID : (row + 3) * HID, :], cot[(row + 1) * HID : (row + 4) * HID, :]], axis=1
        )
        spread = jnp.dot(back_ref[...], cells, preferred_element_type=F32)
        for half in range(2):
            lanes = slice(half * LON, (half + 1) * LON)
            pulled = (
                pltpu.roll(spread[:C, lanes], LON - 1, 1)
                + spread[C : 2 * C, lanes]
                + pltpu.roll(spread[2 * C :, lanes], 1, 1)
            )
            place = row + half
            later = rows_of(target, place + 1).astype(F32)
            adjoint = jnp.where(closing, 0.0, (later + pulled).astype(BF16).astype(F32))
            own = rows_of(own_ref, place + 2).astype(F32)
            latitude = place - margin
            gradient = rows_of(resid_ref, place).astype(F32) - adjoint + innovation(latitude, own)
            value = own - STEP * gradient
            if not 0 <= latitude < ROWS:
                value = jnp.where((latitude >= top) & (latitude < bottom), value, 0.0)
            emit(place, value)


def first_kernel(
    next_ref, ext_ref, active_ref, forecast_ref, resid_ref, sums_ref, above_ref, below_ref,
    back_ref, out_back_ref, state_ref, sent_ref, cot, target,
):
    def innovation(latitude, own):
        if latitude < 0:
            return rows_of(above_ref, 6 + latitude).astype(F32)
        if latitude >= ROWS:
            return rows_of(below_ref, 4 + latitude - ROWS).astype(F32)
        return innovation_of(sums_ref[latitude], own)

    def emit(place, value):
        value = value.astype(BF16)
        state_ref[place * C : (place + 1) * C, :] = value
        if 1 <= place < 11:
            sent_ref[(place - 1) * C : place * C, :] = value

    gradient_part(
        12, 2, next_ref, ext_ref, active_ref, forecast_ref, resid_ref, innovation, back_ref,
        out_back_ref, emit, cot, target,
    )


def second_kernel(
    next_ref, state_ref, active_ref, forecast_ref, resid_ref, sums_ref, back_ref, out_back_ref,
    out_ref, cot, target, wide,
):
    def emit(place, value):
        wide[:, place, :] = value

    gradient_part(
        8, 0, next_ref, state_ref, active_ref, forecast_ref, resid_ref,
        lambda latitude, own: innovation_of(sums_ref[latitude], own), back_ref, out_back_ref, emit,
        cot, target,
    )
    out_ref[...] = wide[...].astype(BF16)


def ring(value, axis, by):
    count = lax.axis_size(axis)
    return lax.ppermute(value, axis, [(i, (i + by) % count) for i in range(count)])


def shape(rows, dtype=BF16):
    return jax.ShapeDtypeStruct((rows, LON), dtype)


def shifted_scratch(count):
    return [pltpu.VMEM((3, (count + 2) * C, LON), BF16)]


def gradient_scratch(count):
    return [
        pltpu.VMEM(((count + 2) * HID, LON), BF16),
        pltpu.VMEM(((count + 2) * C, LON), BF16),
    ]


def row_flops(rows):
    return rows * 2 * LON * HID * 10 * C


def on_device(
    window_snapshots, background, obs_values, obs_index, input_kernel_weight, hidden_bias_vector,
    output_pointwise_weight,
):
    own, ground, up, down = call(
        pack_kernel,
        (shape(ROWS * C), shape(ROWS * C), shape(PAYLOAD), shape(PAYLOAD)),
        [
            pltpu.VMEM((C, ROWS, LON), BF16),
            pltpu.VMEM((C, ROWS, LON), BF16),
            pltpu.VMEM((C, OBS), BF16),
            pltpu.VMEM((1, OBS), jnp.int32),
            pltpu.VMEM((C, ROWS, LON), F32),
            pltpu.VMEM((C, ROWS, LON), F32),
            pltpu.SemaphoreType.DMA((4,)),
        ],
        0, 1 << 20, pl.BlockSpec(memory_space=pltpu.HBM),
    )(
        *(
            pltpu.with_memory_space_constraint(value, pltpu.HBM)
            for value in (window_snapshots[0], background, obs_values[0], obs_index)
        )
    )
    below = ring(up, "lat", -1)
    above = ring(down, "lat", 1)

    out_weight = output_pointwise_weight
    taps = jnp.transpose(input_kernel_weight, (0, 1, 3, 2)).reshape(9 * C, HID)
    prepared = call(
        prepare_kernel,
        (
            jax.ShapeDtypeStruct((ROWS, 72, LON), F32),
            jax.ShapeDtypeStruct((HID, 9 * C), BF16),
            jax.ShapeDtypeStruct((3 * C, 3 * HID), BF16),
            jax.ShapeDtypeStruct((HID, LON), F32),
            jax.ShapeDtypeStruct((HID, C), BF16),
        ),
        [], ROWS * 2 * 80 * OBS * LON, 1 << 20,
    )(obs_values[0], obs_index, taps, hidden_bias_vector[None, :], out_weight)
    above, below, prepared = lax.optimization_barrier((above, below, prepared))
    sums, forward_weight, back_weight, bias, out_back = prepared

    ext, sent = call(extend_kernel, (shape(16 * C), shape(14 * C)), [], 0, 1 << 20)(
        own, above, below
    )
    earlier = ring(sent, "tm", 1)
    later = ring(sent, "tm", -1)

    def forward(count, state):
        return call(
            functools.partial(forward_part, count),
            (shape(count * HID), shape(count * C)),
            shifted_scratch(count),
            row_flops(count), 2 << 20,
        )(state, forward_weight, bias, out_weight)

    def residual(count, margin, prev, state):
        return call(
            functools.partial(residual_kernel, count, margin),
            shape(count * C), shifted_scratch(count), row_flops(count), 2 << 20,
        )(prev, state, ground, forward_weight, bias, out_weight)

    active, forecast = forward(14, ext)
    resid = residual(12, 2, earlier, ext)
    state, sent = call(
        first_kernel, (shape(12 * C), shape(10 * C)), gradient_scratch(12), row_flops(12), 2 << 20
    )(later, ext, active, forecast, resid, sums, above, below, back_weight, out_back)
    earlier = ring(sent, "tm", 1)
    later = ring(sent, "tm", -1)
    active, forecast = forward(10, state)
    resid = residual(8, 0, earlier, state)
    analysis = call(
        second_kernel,
        jax.ShapeDtypeStruct((C, ROWS, LON), BF16),
        gradient_scratch(8) + [pltpu.VMEM((C, ROWS, LON), F32)],
        row_flops(8), 2 << 20,
    )(later, state, active, forecast, resid, sums, back_weight, out_back)
    return analysis[None]


def solution(mesh):
    placed = (
        P("tm", None, "lat", None),
        P(None, "lat", None),
        P("tm", None, "lat"),
        P("tm", "lat"),
        P(),
        P(),
        P(),
    )
    return jax.shard_map(
        on_device, mesh=mesh, in_specs=placed, out_specs=P("tm", None, "lat", None), check_vma=False
    )
```

time: 43.4 us -> 35.6 us (0.82)
  waiting for transfers between devices: 13.6 us -> 4.89 us
  local copies, waits for them, and re-layouts: 5.26 us -> 2.2 us
  starting transfers between devices: 11.8 us -> 14.2 us
  Pallas kernels: 12.3 us -> 14 us
    ppermute x6, waiting for transfers between devices: 13.6 us -> 4.89 us  [ring(): lax.ppermute(value, axis, [(i, (i + by) % count) for i in range(count)])]
    unnamed x19 -> x10, local copies, waits for them, and re-layouts: 4.65 us -> 2.2 us
    ppermute x6, starting transfers between devices: 11.8 us -> 14.2 us  [ring(): lax.ppermute(value, axis, [(i, (i + by) % count) for i in range(count)])]
    pallas_call x7 -> x9, Pallas kernels: 12.3 us -> 14 us  [run(): pl.pallas_call(kernel, out_shape=outs, in_specs=[spec] * len(args), out_s...]
  transfers between devices with their start and end apart: 6 -> 6, of which waited for: 5 -> 4; matrix products, arithmetic and copies ran while one was open for 2% -> 0% of each run, Pallas kernels for 12% -> 26%
where the time goes in v2:
time: 35.6 us; the launch traced here: 35.4 us
  starting transfers between devices  14.2 us (40%)
  Pallas kernels  14 us (39%)
  waiting for transfers between devices  4.89 us (14%)
  local copies, waits for them, and re-layouts  2.2 us (6%)
    ppermute x6, starting transfers between devices, ring(): lax.ppermute(value, axis, [(i, (i + by) % count) for i in range(count)])  14.2 us
    pallas_call x9, Pallas kernels, run(): pl.pallas_call(kernel, out_shape=outs, in_specs=[spec] * len(args), out_s...  14 us
    ppermute x6, waiting for transfers between devices, ring(): lax.ppermute(value, axis, [(i, (i + by) % count) for i in range(count)])  4.89 us
    unnamed x10, local copies, waits for them, and re-layouts  2.2 us
  transfers between devices with their start and end apart: 6, of which 4 were waited for; matrix products, arithmetic and copies ran while one was open for 0% of the time, Pallas kernels for 26%

profile of v2, /device:TPU:0, one launch (start us, length us, event | category | flops | bytes accessed | tf_op | source)
XLA Modules:
  0.0 35.4 jit_solution(6539441569124316396)
XLA Ops:
  0.0 0.0 copy-start
  0.0 2.2 %shard_map.73 = (bf16[512,128]{1,0:T(8,128)(2,1)S(1)}, bf16[512,128]{1,0:T(8,128)(2,1)S(1)}, bf16[384,128]{1,0:T(8,128)(2,1)S(1)}, bf16[384,128]{1,0:T(8,128)(2,1)S(1)}) custom-call(bf16[64,8,128]{2,1,0:T(8,128)(2,1)} %bitcast.11, bf16[64,8,128]{2,1,0:T(8,128)(2,1)} %bg_hbm.1, bf16[64,256]{1,0:T(8,128)(2,1)} %bitcast.8, s32[1,256]{1,0:T(1,128)} %index_ref.1), custom_call_target="tpu_custom_call" | custom-call | bytes 1048576 | tf_op jit(solution)/shard_map/pallas_call | solution.py:27
  2.2 3.4 %collective-permute-start = (bf16[384,128]{1,0:T(8,128)(2,1)S(1)}, bf16[384,128]{1,0:T(8,128)(2,1)S(1)}, u32[]{:S(2)}, u32[]{:S(2)}) collective-permute-start(bf16[384,128]{1,0:T(8,128)(2,1)S(1)} %get-tuple-element.30), channel_id=1, source_target_pairs={{0,1},{1,2},{2,3},{3,4},{4,5},{5,6},{6,7},{7,0},{8,9},{9,10},{10,1... | collective-permute-start | bytes 294920 | tf_op jit(solution)/shard_map/ppermute | solution.py:286
  5.6 0.0 copy-start.4
  5.6 2.3 %collective-permute-start.1 = (bf16[384,128]{1,0:T(8,128)(2,1)S(1)}, bf16[384,128]{1,0:T(8,128)(2,1)S(1)}, u32[]{:S(2)}, u32[]{:S(2)}) collective-permute-start(bf16[384,128]{1,0:T(8,128)(2,1)S(1)} %get-tuple-element.31), channel_id=1, source_target_pairs={{0,7},{1,0},{2,1},{3,2},{4,3},{5,4},{6,5},{7,6},{8,15},{9,8},{10,9... | collective-permute-start | bytes 294920 | tf_op jit(solution)/shard_map/ppermute | solution.py:286
  7.9 0.0 copy-start.3
  7.9 0.0 copy-done
  7.9 0.0 copy-done.4
  7.9 0.7 %copy-done.3 = s32[1,256]{1,0:T(1,128)S(1)} copy-done((s32[1,256]{1,0:T(1,128)S(1)}, s32[1,256]{1,0:T(1,128)}, u32[]{:S(2)}) %copy-start.3) | copy-done | bytes 1048
  8.6 0.0 copy-start.1
  8.6 0.8 %copy-done.1 = bf16[1,64,256]{2,1,0:T(8,128)(2,1)S(1)} copy-done((bf16[1,64,256]{2,1,0:T(8,128)(2,1)S(1)}, bf16[1,64,256]{2,1,0:T(8,128)(2,1)}, u32[]{:S(2)}) %copy-start.1) | copy-done | bytes 32792
  9.3 0.0 copy-start.2
  9.3 0.8 %copy-done.2 = bf16[64,256]{1,0:T(8,128)(2,1)S(1)} copy-done((bf16[64,256]{1,0:T(8,128)(2,1)S(1)}, bf16[64,256]{1,0:T(8,128)(2,1)}, u32[]{:S(2)}) %copy-start.2) | copy-done | bytes 32792
  10.1 0.3 shard_map.74
  10.4 0.2 collective-permute-done.above_ref
  10.7 2.0 %collective-permute-done.1.below_ref = bf16[384,128]{1,0:T(8,128)(2,1)S(1)} collective-permute-done((bf16[384,128]{1,0:T(8,128)(2,1)S(1)}, bf16[384,128]{1,0:T(8,128)(2,1)S(1)}, u32[]{:S(2)}, u32[]{:S(2)}) %collective-permute-start.1) | collective-permute-done | bytes 98336 | tf_op jit(solution)/shard_map/ppermute | solution.py:286
  12.7 0.1 shard_map.75
  12.7 0.1 collective-permute-start.3
  12.8 4.5 %collective-permute-start.2 = (bf16[896,128]{1,0:T(8,128)(2,1)S(1)}, bf16[896,128]{1,0:T(8,128)(2,1)S(1)}, u32[]{:S(2)}, u32[]{:S(2)}) collective-permute-start(bf16[896,128]{1,0:T(8,128)(2,1)S(1)} %get-tuple-element.39), channel_id=1, source_target_pairs={{0,120},{8,0},{16,8},{24,16},{32,24},{40,32},{48,40},{56,48},{64,5... | collective-permute-start | bytes 688136 | tf_op jit(solution)/shard_map/ppermute | solution.py:286
  17.3 2.7 %shard_map.76 = (bf16[3584,128]{1,0:T(8,128)(2,1)S(1)}, bf16[896,128]{1,0:T(8,128)(2,1)S(1)}) custom-call(bf16[1024,128]{1,0:T(8,128)(2,1)S(1)} %get-tuple-element.40.state_ref.own_ref.ext_ref, bf16[256,576]{1,0:T(8,128)(2,1)S(1)} %get-tuple-element.41.kernel_ref, f32[256,128]{1,0:T(8,128)S(1)} %get-tuple-element.42.bias_ref, bf16[64,256]{1,0:T(8,128)(2,1)S(1)} %copy-done.2), custom_call_target="tpu_custom_call" | custom-call | flops 587202560 | bytes 2097152 | tf_op jit(solution)/shard_map/pallas_call | solution.py:27
  20.0 0.9 %collective-permute-done.3.prev_ref = bf16[896,128]{1,0:T(8,128)(2,1)S(1)} collective-permute-done((bf16[896,128]{1,0:T(8,128)(2,1)S(1)}, bf16[896,128]{1,0:T(8,128)(2,1)S(1)}, u32[]{:S(2)}, u32[]{:S(2)}) %collective-permute-start.3) | collective-permute-done | bytes 229408 | tf_op jit(solution)/shard_map/ppermute | solution.py:286
  21.0 2.4 %shard_map.77.resid_ref = bf16[768,128]{1,0:T(8,128)(2,1)S(1)} custom-call(bf16[896,128]{1,0:T(8,128)(2,1)S(1)} %collective-permute-done.3.prev_ref, bf16[1024,128]{1,0:T(8,128)(2,1)S(1)} %get-tuple-element.40.state_ref.own_ref.ext_ref, bf16[512,128]{1,0:T(8,128)(2,1)S(1)} %get-tuple-element.45.bg_ref, bf16[256,576]{1,0:T(8,128)(2,1)S(1)} %get-tuple-element.41.kernel_ref, ...), custom_call_target="tpu_custom_call" | custom-call | flops 503316480 | bytes 2097152 | tf_op jit(solution)/shard_map/pallas_call | solution.py:27
  23.4 0.0 collective-permute-done.2.next_ref
  23.4 1.1 %shard_map.78 = (bf16[768,128]{1,0:T(8,128)(2,1)S(1)}, bf16[640,128]{1,0:T(8,128)(2,1)S(1)}) custom-call(bf16[896,128]{1,0:T(8,128)(2,1)S(1)} %collective-permute-done.2.next_ref, bf16[1024,128]{1,0:T(8,128)(2,1)S(1)} %get-tuple-element.40.state_ref.own_ref.ext_ref, bf16[3584,128]{1,0:T(8,128)(2,1)S(1)} %get-tuple-element.43.active_ref, ...), custom_call_target="tpu_custom_call" | custom-call | flops 503316480 | bytes 2097152 | tf_op jit(solution)/shard_map/pallas_call | solution.py:27
  24.5 0.1 collective-permute-start.5
  24.6 3.8 %collective-permute-start.4 = (bf16[640,128]{1,0:T(8,128)(2,1)S(1)}, bf16[640,128]{1,0:T(8,128)(2,1)S(1)}, u32[]{:S(2)}, u32[]{:S(2)}) collective-permute-start(bf16[640,128]{1,0:T(8,128)(2,1)S(1)} %get-tuple-element.49), channel_id=1, source_target_pairs={{0,120},{8,0},{16,8},{24,16},{32,24},{40,32},{48,40},{56,48},{64,5... | collective-permute-start | bytes 491528 | tf_op jit(solution)/shard_map/ppermute | solution.py:286
  28.4 2.0 %shard_map.79 = (bf16[2560,128]{1,0:T(8,128)(2,1)S(1)}, bf16[640,128]{1,0:T(8,128)(2,1)S(1)}) custom-call(bf16[768,128]{1,0:T(8,128)(2,1)S(1)} %get-tuple-element.50.state_ref.own_ref, bf16[256,576]{1,0:T(8,128)(2,1)S(1)} %get-tuple-element.41.kernel_ref, f32[256,128]{1,0:T(8,128)S(1)} %get-tuple-element.42.bias_ref, bf16[64,256]{1,0:T(8,128)(2,1)S(1)} %copy-done.2), custom_call_target="tpu_custom_call" | custom-call | flops 419430400 | bytes 2097152 | tf_op jit(solution)/shard_map/pallas_call | solution.py:27
  30.4 1.7 %collective-permute-done.5.prev_ref = bf16[640,128]{1,0:T(8,128)(2,1)S(1)} collective-permute-done((bf16[640,128]{1,0:T(8,128)(2,1)S(1)}, bf16[640,128]{1,0:T(8,128)(2,1)S(1)}, u32[]{:S(2)}, u32[]{:S(2)}) %collective-permute-start.5) | collective-permute-done | bytes 163872 | tf_op jit(solution)/shard_map/ppermute | solution.py:286
  32.1 1.7 %shard_map.80.resid_ref = bf16[512,128]{1,0:T(8,128)(2,1)S(1)} custom-call(bf16[640,128]{1,0:T(8,128)(2,1)S(1)} %collective-permute-done.5.prev_ref, bf16[768,128]{1,0:T(8,128)(2,1)S(1)} %get-tuple-element.50.state_ref.own_ref, bf16[512,128]{1,0:T(8,128)(2,1)S(1)} %get-tuple-element.45.bg_ref, bf16[256,576]{1,0:T(8,128)(2,1)S(1)} %get-tuple-element.41.kernel_ref, ...), custom_call_target="tpu_custom_call" | custom-call | flops 335544320 | bytes 2097152 | tf_op jit(solution)/shard_map/pallas_call | solution.py:27
  33.7 0.0 collective-permute-done.4.next_ref
  33.8 1.6 %shard_map.81 = bf16[64,8,128]{2,1,0:T(8,128)(2,1)} custom-call(bf16[640,128]{1,0:T(8,128)(2,1)S(1)} %collective-permute-done.4.next_ref, bf16[768,128]{1,0:T(8,128)(2,1)S(1)} %get-tuple-element.50.state_ref.own_ref, bf16[2560,128]{1,0:T(8,128)(2,1)S(1)} %get-tuple-element.51.active_ref, bf16[640,128]{1,0:T(8,128)(2,1)S(1)} %get-tuple-element.52.forecast_ref, ...), custom_call_target="tpu_custom_call" | custom-call | flops 335544320 | bytes 2097152 | tf_op jit(solution)/shard_map/pallas_call | solution.py:27
Async XLA Ops:
  0.0 7.9 %copy-start = (bf16[3,3,256,64]{2,3,1,0:T(8,128)(2,1)S(1)}, bf16[3,3,256,64]{2,3,1,0:T(8,128)(2,1)}, u32[]{:S(2)}) copy-start(bf16[3,3,256,64]{2,3,1,0:T(8,128)(2,1)} %param.11) | copy-start | bytes 884740
  2.2 8.5 %collective-permute-start = (bf16[384,128]{1,0:T(8,128)(2,1)S(1)}, bf16[384,128]{1,0:T(8,128)(2,1)S(1)}, u32[]{:S(2)}, u32[]{:S(2)}) collective-permute-start(bf16[384,128]{1,0:T(8,128)(2,1)S(1)} %get-tuple-element.30), channel_id=1, source_target_pairs={{0,1},{1,2},{2,3},{3,4},{4,5},{5,6},{6,7},{7,0},{8,9},{9,10},{10,1... | collective-permute-start | bytes 294920 | tf_op jit(solution)/shard_map/ppermute | solution.py:286
  5.6 2.3 %copy-start.4 = (f32[256]{0:T(256)S(1)}, f32[256]{0:T(256)}, u32[]{:S(2)}) copy-start(f32[256]{0:T(256)} %param.12) | copy-start | bytes 3076
  5.6 7.1 %collective-permute-start.1 = (bf16[384,128]{1,0:T(8,128)(2,1)S(1)}, bf16[384,128]{1,0:T(8,128)(2,1)S(1)}, u32[]{:S(2)}, u32[]{:S(2)}) collective-permute-start(bf16[384,128]{1,0:T(8,128)(2,1)S(1)} %get-tuple-element.31), channel_id=1, source_target_pairs={{0,7},{1,0},{2,1},{3,2},{4,3},{5,4},{6,5},{7,6},{8,15},{9,8},{10,9... | collective-permute-start | bytes 294920 | tf_op jit(solution)/shard_map/ppermute | solution.py:286
  7.9 0.7 %copy-start.3 = (s32[1,256]{1,0:T(1,128)S(1)}, s32[1,256]{1,0:T(1,128)}, u32[]{:S(2)}) copy-start(s32[1,256]{1,0:T(1,128)} %index_ref.1) | copy-start | bytes 3076
  8.6 0.8 %copy-start.1 = (bf16[1,64,256]{2,1,0:T(8,128)(2,1)S(1)}, bf16[1,64,256]{2,1,0:T(8,128)(2,1)}, u32[]{:S(2)}) copy-start(bf16[1,64,256]{2,1,0:T(8,128)(2,1)} %param.9) | copy-start | bytes 98308
  9.3 0.8 %copy-start.2 = (bf16[64,256]{1,0:T(8,128)(2,1)S(1)}, bf16[64,256]{1,0:T(8,128)(2,1)}, u32[]{:S(2)}) copy-start(bf16[64,256]{1,0:T(8,128)(2,1)} %out_weight_ref.9) | copy-start | bytes 98308
  12.7 8.2 %collective-permute-start.3 = (bf16[896,128]{1,0:T(8,128)(2,1)S(1)}, bf16[896,128]{1,0:T(8,128)(2,1)S(1)}, u32[]{:S(2)}, u32[]{:S(2)}) collective-permute-start(bf16[896,128]{1,0:T(8,128)(2,1)S(1)} %get-tuple-element.39), channel_id=1, source_target_pairs={{0,8},{8,16},{16,24},{24,32},{32,40},{40,48},{48,56},{56,64},{64,7... | collective-permute-start | bytes 688136 | tf_op jit(solution)/shard_map/ppermute | solution.py:286
  12.8 10.6 %collective-permute-start.2 = (bf16[896,128]{1,0:T(8,128)(2,1)S(1)}, bf16[896,128]{1,0:T(8,128)(2,1)S(1)}, u32[]{:S(2)}, u32[]{:S(2)}) collective-permute-start(bf16[896,128]{1,0:T(8,128)(2,1)S(1)} %get-tuple-element.39), channel_id=1, source_target_pairs={{0,120},{8,0},{16,8},{24,16},{32,24},{40,32},{48,40},{56,48},{64,5... | collective-permute-start | bytes 688136 | tf_op jit(solution)/shard_map/ppermute | solution.py:286
  24.5 7.6 %collective-permute-start.5 = (bf16[640,128]{1,0:T(8,128)(2,1)S(1)}, bf16[640,128]{1,0:T(8,128)(2,1)S(1)}, u32[]{:S(2)}, u32[]{:S(2)}) collective-permute-start(bf16[640,128]{1,0:T(8,128)(2,1)S(1)} %get-tuple-element.49), channel_id=1, source_target_pairs={{0,8},{8,16},{16,24},{24,32},{32,40},{40,48},{48,56},{56,64},{64,7... | collective-permute-start | bytes 491528 | tf_op jit(solution)/shard_map/ppermute | solution.py:286
  24.6 9.2 %collective-permute-start.4 = (bf16[640,128]{1,0:T(8,128)(2,1)S(1)}, bf16[640,128]{1,0:T(8,128)(2,1)S(1)}, u32[]{:S(2)}, u32[]{:S(2)}) collective-permute-start(bf16[640,128]{1,0:T(8,128)(2,1)S(1)} %get-tuple-element.49), channel_id=1, source_target_pairs={{0,120},{8,0},{16,8},{24,16},{32,24},{40,32},{48,40},{56,48},{64,5... | collective-permute-start | bytes 491528 | tf_op jit(solution)/shard_map/ppermute | solution.py:286

commit v3 on v2

--- a/solution.py
+++ b/solution.py
@@ -6,6 +6,7 @@
 from jax.experimental import pallas as pl
 from jax.experimental.pallas import tpu as pltpu
 from jax.sharding import PartitionSpec as P
+
 
 C = 64
 HID = 256
@@ -43,6 +44,10 @@
     return ref[first * width : (first + 1) * width, :]
 
 
+def latitude(row):
+    return pl.ds(row, C, stride=ROWS)
+
+
 def local_cells(index):
     local = index - lax.axis_index("lat") * (ROWS * LON)
     high = lax.shift_right_arithmetic(local, 7)
@@ -78,9 +83,9 @@
     for copy in copies:
         copy.start()
     copies[0].wait()
-    xs[...] = x_ref[...].astype(F32)
+    xs[...] = x_ref[...].astype(F32).reshape(ROWS * C, LON)
     for row in range(ROWS):
-        value = xs[:, row, :].astype(BF16)
+        value = xs[latitude(row), :].astype(BF16)
         own_ref[row * C : (row + 1) * C, :] = value
         if row < 4:
             up_ref[row * C : (row + 1) * C, :] = value
@@ -92,13 +97,13 @@
     values = with_ones(obs_ref[...])
     sums = [observation_sums(values, low, high, row) for row in (0, 1, 6, 7)]
     copies[3].wait()
-    bs[...] = bg_ref[...].astype(F32)
+    bs[...] = bg_ref[...].astype(F32).reshape(ROWS * C, LON)
     opening = lax.axis_index("tm") == 0
     for row in range(ROWS):
-        ground = bs[:, row, :]
+        ground = bs[latitude(row), :]
         bg_rows_ref[row * C : (row + 1) * C, :] = ground.astype(BF16)
         if row < 2 or row >= 6:
-            own = xs[:, row, :]
+            own = xs[latitude(row), :]
             edge = innovation_of(sums[row if row < 2 else row - 4], own)
             edge = edge + jnp.where(opening, own - ground, 0.0)
             ref, place = (up_ref, row) if row < 2 else (down_ref, row - 6)
@@ -181,8 +186,8 @@
         back_ref[:, a * HID : (a + 1) * HID] = kernel_ref[(2 - a) * 3 * C : (3 - a) * 3 * C, :]
 
 
-def residual_kernel(
-    count, margin, prev_ref, own_ref, bg_ref, kernel_ref, bias_ref, out_weight_ref, resid_ref, shifted
+def residual_part(
+    count, margin, prev_ref, own_ref, bg_ref, kernel_ref, bias_ref, out_weight_ref, shifted, take
 ):
     roll_rows(prev_ref, shifted, count + 2)
     bias = jnp.concatenate([bias_ref[...], bias_ref[...]], axis=1)
@@ -193,19 +198,22 @@
         centre = side_by_side(prev_ref, row + 1).astype(F32)
         guess = (centre + step).astype(BF16).astype(F32)
         own = side_by_side(own_ref, row + 2).astype(F32)
-        latitude = row - margin
-        known = side_by_side(bg_ref, latitude).astype(F32) if 0 <= latitude < ROWS else own
-        guess = jnp.where(opening, known, guess)
-        store_pair(resid_ref, row, (own - guess).astype(BF16))
-
-
-def gradient_part(
-    count, margin, next_ref, own_ref, active_ref, forecast_ref, resid_ref, innovation, back_ref,
-    out_back_ref, emit, cot, target,
-):
+        place = row - margin
+        known = side_by_side(bg_ref, place).astype(F32) if 0 <= place < ROWS else own
+        resid = (own - jnp.where(opening, known, guess)).astype(BF16)
+        take(row, resid[:, :LON])
+        take(row + 1, resid[:, LON:])
+
+
+def strip_ends():
     strip = lax.axis_index("lat")
-    top = -strip * ROWS
-    bottom = (lax.axis_size("lat") - strip) * ROWS
+    return -strip * ROWS, (lax.axis_size("lat") - strip) * ROWS
+
+
+def adjoint_part(
+    count, margin, next_ref, active_ref, forecast_ref, back_ref, out_back_ref, cot, target, take
+):
+    top, bottom = strip_ends()
     for row in range(0, count + 2, 2):
         later = side_by_side(next_ref, row).astype(F32) - side_by_side(forecast_ref, row).astype(F32)
         later = later.astype(BF16)
@@ -231,54 +239,105 @@
                 + spread[C : 2 * C, lanes]
                 + pltpu.roll(spread[2 * C :, lanes], 1, 1)
             )
-            place = row + half
-            later = rows_of(target, place + 1).astype(F32)
-            adjoint = jnp.where(closing, 0.0, (later + pulled).astype(BF16).astype(F32))
-            own = rows_of(own_ref, place + 2).astype(F32)
-            latitude = place - margin
-            gradient = rows_of(resid_ref, place).astype(F32) - adjoint + innovation(latitude, own)
-            value = own - STEP * gradient
-            if not 0 <= latitude < ROWS:
-                value = jnp.where((latitude >= top) & (latitude < bottom), value, 0.0)
-            emit(place, value)
+            later = rows_of(target, row + half + 1).astype(F32)
+            take(row + half, jnp.where(closing, 0.0, later + pulled).astype(BF16))
+
+
+def is_even():
+    return lax.rem(lax.axis_index("tm"), 2) == 0
+
+
+def near_kernel(
+    count, margin, near_ref, own_ref, bg_ref, active_ref, forecast_ref, kernel_ref, bias_ref,
+    out_weight_ref, back_ref, out_back_ref, part_ref, shifted, cot, target,
+):
+    def take(row, value):
+        part_ref[row * C : (row + 1) * C, :] = value
+
+    even = is_even()
+
+    @pl.when(even)
+    def _():
+        adjoint_part(
+            count, margin, near_ref, active_ref, forecast_ref, back_ref, out_back_ref, cot, target, take
+        )
+
+    @pl.when(jnp.logical_not(even))
+    def _():
+        residual_part(
+            count, margin, near_ref, own_ref, bg_ref, kernel_ref, bias_ref, out_weight_ref, shifted, take
+        )
+
+
+def far_part(
+    count, margin, far_ref, part_ref, own_ref, bg_ref, active_ref, forecast_ref, kernel_ref, bias_ref,
+    out_weight_ref, back_ref, out_back_ref, innovation, emit, shifted, cot, target,
+):
+    top, bottom = strip_ends()
+
+    def step(row, resid, adjoint):
+        own = rows_of(own_ref, row + 2).astype(F32)
+        place = row - margin
+        gradient = resid.astype(F32) - adjoint.astype(F32) + innovation(place, own)
+        value = own - STEP * gradient
+        if not 0 <= place < ROWS:
+            value = jnp.where((place >= top) & (place < bottom), value, 0.0)
+        emit(row, value)
+
+    even = is_even()
+
+    @pl.when(even)
+    def _():
+        residual_part(
+            count, margin, far_ref, own_ref, bg_ref, kernel_ref, bias_ref, out_weight_ref, shifted,
+            lambda row, resid: step(row, resid, rows_of(part_ref, row)),
+        )
+
+    @pl.when(jnp.logical_not(even))
+    def _():
+        adjoint_part(
+            count, margin, far_ref, active_ref, forecast_ref, back_ref, out_back_ref, cot, target,
+            lambda row, adjoint: step(row, rows_of(part_ref, row), adjoint),
+        )
 
 
 def first_kernel(
-    next_ref, ext_ref, active_ref, forecast_ref, resid_ref, sums_ref, above_ref, below_ref,
-    back_ref, out_back_ref, state_ref, sent_ref, cot, target,
-):
-    def innovation(latitude, own):
-        if latitude < 0:
-            return rows_of(above_ref, 6 + latitude).astype(F32)
-        if latitude >= ROWS:
-            return rows_of(below_ref, 4 + latitude - ROWS).astype(F32)
-        return innovation_of(sums_ref[latitude], own)
-
+    far_ref, part_ref, own_ref, bg_ref, active_ref, forecast_ref, kernel_ref, bias_ref,
+    out_weight_ref, back_ref, out_back_ref, sums_ref, above_ref, below_ref, state_ref, sent_ref,
+    shifted, cot, target,
+):
+    def innovation(place, own):
+        if place < 0:
+            return rows_of(above_ref, 6 + place).astype(F32)
+        if place >= ROWS:
+            return rows_of(below_ref, 4 + place - ROWS).astype(F32)
+        return innovation_of(sums_ref[place], own)
+
+    def emit(row, value):
+        value = value.astype(BF16)
+        state_ref[row * C : (row + 1) * C, :] = value
+        if 1 <= row < 11:
+            sent_ref[(row - 1) * C : row * C, :] = value
+
+    far_part(
+        12, 2, far_ref, part_ref, own_ref, bg_ref, active_ref, forecast_ref, kernel_ref, bias_ref,
+        out_weight_ref, back_ref, out_back_ref, innovation, emit, shifted, cot, target,
+    )
+
+
+def second_kernel(
+    far_ref, part_ref, own_ref, bg_ref, active_ref, forecast_ref, kernel_ref, bias_ref,
+    out_weight_ref, back_ref, out_back_ref, sums_ref, out_ref, shifted, cot, target, wide,
+):
     def emit(place, value):
-        value = value.astype(BF16)
-        state_ref[place * C : (place + 1) * C, :] = value
-        if 1 <= place < 11:
-            sent_ref[(place - 1) * C : place * C, :] = value
-
-    gradient_part(
-        12, 2, next_ref, ext_ref, active_ref, forecast_ref, resid_ref, innovation, back_ref,
-        out_back_ref, emit, cot, target,
-    )
-
-
-def second_kernel(
-    next_ref, state_ref, active_ref, forecast_ref, resid_ref, sums_ref, back_ref, out_back_ref,
-    out_ref, cot, target, wide,
-):
-    def emit(place, value):
-        wide[:, place, :] = value
-
-    gradient_part(
-        8, 0, next_ref, state_ref, active_ref, forecast_ref, resid_ref,
-        lambda latitude, own: innovation_of(sums_ref[latitude], own), back_ref, out_back_ref, emit,
-        cot, target,
-    )
-    out_ref[...] = wide[...].astype(BF16)
+        wide[latitude(place), :] = value
+
+    far_part(
+        8, 0, far_ref, part_ref, own_ref, bg_ref, active_ref, forecast_ref, kernel_ref, bias_ref,
+        out_weight_ref, back_ref, out_back_ref,
+        lambda place, own: innovation_of(sums_ref[place], own), emit, shifted, cot, target,
+    )
+    out_ref[...] = wide[...].reshape(C, ROWS, LON).astype(BF16)
 
 
 def ring(value, axis, by):
@@ -286,6 +345,12 @@
     return lax.ppermute(value, axis, [(i, (i + by) % count) for i in range(count)])
 
 
+def swap(value, first):
+    count = lax.axis_size("tm")
+    pairs = [(i, (i + 1) % count) for i in range(first, count, 2)]
+    return lax.ppermute(value, "tm", pairs + [(j, i) for i, j in pairs])
+
+
 def shape(rows, dtype=BF16):
     return jax.ShapeDtypeStruct((rows, LON), dtype)
 
@@ -295,7 +360,7 @@
 
 
 def gradient_scratch(count):
-    return [
+    return shifted_scratch(count) + [
         pltpu.VMEM(((count + 2) * HID, LON), BF16),
         pltpu.VMEM(((count + 2) * C, LON), BF16),
     ]
@@ -317,8 +382,8 @@
             pltpu.VMEM((C, ROWS, LON), BF16),
             pltpu.VMEM((C, OBS), BF16),
             pltpu.VMEM((1, OBS), jnp.int32),
-            pltpu.VMEM((C, ROWS, LON), F32),
-            pltpu.VMEM((C, ROWS, LON), F32),
+            pltpu.VMEM((C * ROWS, LON), F32),
+            pltpu.VMEM((C * ROWS, LON), F32),
             pltpu.SemaphoreType.DMA((4,)),
         ],
         0, 1 << 20, pl.BlockSpec(memory_space=pltpu.HBM),
@@ -350,8 +415,12 @@
     ext, sent = call(extend_kernel, (shape(16 * C), shape(14 * C)), [], 0, 1 << 20)(
         own, above, below
     )
-    earlier = ring(sent, "tm", 1)
-    later = ring(sent, "tm", -1)
+    weights = (forward_weight, bias, out_weight, back_weight, out_back)
+
+    def exchange(sent):
+        far = swap(sent, 1)
+        near = swap(sent, 0)
+        return far, near
 
     def forward(count, state):
         return call(
@@ -361,27 +430,27 @@
             row_flops(count), 2 << 20,
         )(state, forward_weight, bias, out_weight)
 
-    def residual(count, margin, prev, state):
+    def near_part(count, margin, near, *given):
         return call(
-            functools.partial(residual_kernel, count, margin),
-            shape(count * C), shifted_scratch(count), row_flops(count), 2 << 20,
-        )(prev, state, ground, forward_weight, bias, out_weight)
-
-    active, forecast = forward(14, ext)
-    resid = residual(12, 2, earlier, ext)
+            functools.partial(near_kernel, count, margin),
+            shape(count * C), gradient_scratch(count), row_flops(count), 2 << 20,
+        )(near, *given)
+
+    far, near = exchange(sent)
+    given = (ext, ground, *forward(14, ext), *weights)
+    part = near_part(12, 2, near, *given)
     state, sent = call(
         first_kernel, (shape(12 * C), shape(10 * C)), gradient_scratch(12), row_flops(12), 2 << 20
-    )(later, ext, active, forecast, resid, sums, above, below, back_weight, out_back)
-    earlier = ring(sent, "tm", 1)
-    later = ring(sent, "tm", -1)
-    active, forecast = forward(10, state)
-    resid = residual(8, 0, earlier, state)
+    )(far, part, *given, sums, above, below)
+    far, near = exchange(sent)
+    given = (state, ground, *forward(10, state), *weights)
+    part = near_part(8, 0, near, *given)
     analysis = call(
         second_kernel,
         jax.ShapeDtypeStruct((C, ROWS, LON), BF16),
-        gradient_scratch(8) + [pltpu.VMEM((C, ROWS, LON), F32)],
+        gradient_scratch(8) + [pltpu.VMEM((C * ROWS, LON), F32)],
         row_flops(8), 2 << 20,
-    )(later, state, active, forecast, resid, sums, back_weight, out_back)
+    )(far, part, *given, sums)
     return analysis[None]
 
 

time: 35.6 us -> 36 us (1.011)
  waiting for transfers between devices: 4.89 us -> 7.9 us
  starting transfers between devices: 14.2 us -> 13.2 us
  Pallas kernels: 14 us -> 13.1 us
  local copies, waits for them, and re-layouts: 2.2 us -> 1.64 us
    ppermute x6 -> x2, starting transfers between devices: 14.2 us -> 5.71 us  [ring(): lax.ppermute(value, axis, [(i, (i + by) % count) for i in range(count)])]
    ppermute x0 -> x4, starting transfers between devices: none -> 7.46 us  [swap(): return lax.ppermute(value, 'tm', pairs + [(j, i) for i, j in pairs])]
    ppermute x0 -> x4, waiting for transfers between devices: none -> 5.09 us  [swap(): return lax.ppermute(value, 'tm', pairs + [(j, i) for i, j in pairs])]
    ppermute x6 -> x2, waiting for transfers between devices: 4.89 us -> 2.8 us  [ring(): lax.ppermute(value, axis, [(i, (i + by) % count) for i in range(count)])]
    pallas_call x9, Pallas kernels: 14 us -> 13.1 us  [run(): pl.pallas_call(kernel, out_shape=outs, in_specs=[spec] * len(args), out_s...]
    unnamed x10, local copies, waits for them, and re-layouts: 2.2 us -> 1.64 us
  transfers between devices with their start and end apart: 6 -> 6, of which waited for: 4 -> 4; matrix products, arithmetic and copies ran while one was open for 0% -> 0% of each run, Pallas kernels for 26% -> 19%
where the time goes in v3:
time: 36 us; the launch traced here: 35.9 us
  starting transfers between devices  13.2 us (37%)
  Pallas kernels  13.1 us (36%)
  waiting for transfers between devices  7.9 us (22%)
  local copies, waits for them, and re-layouts  1.64 us (5%)
    pallas_call x9, Pallas kernels, run(): pl.pallas_call(kernel, out_shape=outs, in_specs=[spec] * len(args), out_s...  13.1 us
    ppermute x4, starting transfers between devices, swap(): return lax.ppermute(value, 'tm', pairs + [(j, i) for i, j in pairs])  7.46 us
    ppermute x2, starting transfers between devices, ring(): lax.ppermute(value, axis, [(i, (i + by) % count) for i in range(count)])  5.71 us
    ppermute x4, waiting for transfers between devices, swap(): return lax.ppermute(value, 'tm', pairs + [(j, i) for i, j in pairs])  5.09 us
    ppermute x2, waiting for transfers between devices, ring(): lax.ppermute(value, axis, [(i, (i + by) % count) for i in range(count)])  2.8 us
    unnamed x10, local copies, waits for them, and re-layouts  1.64 us
  transfers between devices with their start and end apart: 6, of which 4 were waited for; matrix products, arithmetic and copies ran while one was open for 0% of the time, Pallas kernels for 19%

profile of v3, /device:TPU:0, one launch (start us, length us, event | category | flops | bytes accessed | tf_op | source)
XLA Modules:
  0.0 35.9 jit_solution(1071959377701454110)
XLA Ops:
  0.0 0.0 copy-start
  0.0 0.0 copy-start.2
  0.0 1.3 %shard_map.73 = (bf16[512,128]{1,0:T(8,128)(2,1)S(1)}, bf16[512,128]{1,0:T(8,128)(2,1)S(1)}, bf16[384,128]{1,0:T(8,128)(2,1)S(1)}, bf16[384,128]{1,0:T(8,128)(2,1)S(1)}) custom-call(bf16[64,8,128]{2,1,0:T(8,128)(2,1)} %bitcast.11, bf16[64,8,128]{2,1,0:T(8,128)(2,1)} %bg_hbm.1, bf16[64,256]{1,0:T(8,128)(2,1)} %bitcast.8, s32[1,256]{1,0:T(1,128)} %index_ref.1), custom_call_target="tpu_custom_call" | custom-call | bytes 1048576 | tf_op jit(solution)/shard_map/pallas_call | solution.py:28
  1.3 3.4 %collective-permute-start = (bf16[384,128]{1,0:T(8,128)(2,1)S(1)}, bf16[384,128]{1,0:T(8,128)(2,1)S(1)}, u32[]{:S(2)}, u32[]{:S(2)}) collective-permute-start(bf16[384,128]{1,0:T(8,128)(2,1)S(1)} %get-tuple-element.30), channel_id=1, source_target_pairs={{0,1},{1,2},{2,3},{3,4},{4,5},{5,6},{6,7},{7,0},{8,9},{9,10},{10,1... | collective-permute-start | bytes 294920 | tf_op jit(solution)/shard_map/ppermute | solution.py:345
  4.7 0.0 copy-start.4
  4.7 2.3 %collective-permute-start.1 = (bf16[384,128]{1,0:T(8,128)(2,1)S(1)}, bf16[384,128]{1,0:T(8,128)(2,1)S(1)}, u32[]{:S(2)}, u32[]{:S(2)}) collective-permute-start(bf16[384,128]{1,0:T(8,128)(2,1)S(1)} %get-tuple-element.31), channel_id=1, source_target_pairs={{0,7},{1,0},{2,1},{3,2},{4,3},{5,4},{6,5},{7,6},{8,15},{9,8},{10,9... | collective-permute-start | bytes 294920 | tf_op jit(solution)/shard_map/ppermute | solution.py:345
  7.0 0.0 copy-start.3
  7.1 0.0 copy-done
  7.1 0.0 copy-done.2
  7.1 0.0 copy-done.4
  7.1 0.7 %copy-done.3 = s32[1,256]{1,0:T(1,128)S(1)} copy-done((s32[1,256]{1,0:T(1,128)S(1)}, s32[1,256]{1,0:T(1,128)}, u32[]{:S(2)}) %copy-start.3) | copy-done | bytes 1048
  7.7 0.0 copy-start.1
  7.7 1.0 %copy-done.1 = bf16[3,3,256,64]{2,3,1,0:T(8,128)(2,1)S(1)} copy-done((bf16[3,3,256,64]{2,3,1,0:T(8,128)(2,1)S(1)}, bf16[3,3,256,64]{2,3,1,0:T(8,128)(2,1)}, u32[]{:S(2)}) %copy-start.1) | copy-done | bytes 294936
  8.7 0.3 shard_map.74
  9.0 0.8 %collective-permute-done.above_ref = bf16[384,128]{1,0:T(8,128)(2,1)S(1)} collective-permute-done((bf16[384,128]{1,0:T(8,128)(2,1)S(1)}, bf16[384,128]{1,0:T(8,128)(2,1)S(1)}, u32[]{:S(2)}, u32[]{:S(2)}) %collective-permute-start) | collective-permute-done | bytes 98336 | tf_op jit(solution)/shard_map/ppermute | solution.py:345
  9.8 2.0 %collective-permute-done.1.below_ref = bf16[384,128]{1,0:T(8,128)(2,1)S(1)} collective-permute-done((bf16[384,128]{1,0:T(8,128)(2,1)S(1)}, bf16[384,128]{1,0:T(8,128)(2,1)S(1)}, u32[]{:S(2)}, u32[]{:S(2)}) %collective-permute-start.1) | collective-permute-done | bytes 98336 | tf_op jit(solution)/shard_map/ppermute | solution.py:345
  11.8 0.1 shard_map.75
  11.9 0.1 collective-permute-start.3
  12.0 5.0 %collective-permute-start.2 = (bf16[896,128]{1,0:T(8,128)(2,1)S(1)}, bf16[896,128]{1,0:T(8,128)(2,1)S(1)}, u32[]{:S(2)}, u32[]{:S(2)}) collective-permute-start(bf16[896,128]{1,0:T(8,128)(2,1)S(1)} %get-tuple-element.39), channel_id=1, source_target_pairs={{8,16},{24,32},{40,48},{56,64},{72,80},{88,96},{104,112},{120,0},{... | collective-permute-start | bytes 688136 | tf_op jit(solution)/shard_map/ppermute | solution.py:351
  17.0 2.7 %shard_map.76 = (bf16[3584,128]{1,0:T(8,128)(2,1)S(1)}, bf16[896,128]{1,0:T(8,128)(2,1)S(1)}) custom-call(bf16[1024,128]{1,0:T(8,128)(2,1)S(1)} %get-tuple-element.40.state_ref.own_ref, bf16[256,576]{1,0:T(8,128)(2,1)S(1)} %get-tuple-element.42.kernel_ref, f32[256,128]{1,0:T(8,128)S(1)} %get-tuple-element.43.bias_ref, bf16[64,256]{1,0:T(8,128)(2,1)S(1)} %copy-done), custom_call_target="tpu_custom_call" | custom-call | flops 587202560 | bytes 2097152 | tf_op jit(solution)/shard_map/pallas_call | solution.py:28
  19.7 0.0 collective-permute-done.3.near_ref
  19.7 1.0 %shard_map.77.part_ref = bf16[768,128]{1,0:T(8,128)(2,1)S(1)} custom-call(bf16[896,128]{1,0:T(8,128)(2,1)S(1)} %collective-permute-done.3.near_ref, bf16[1024,128]{1,0:T(8,128)(2,1)S(1)} %get-tuple-element.40.state_ref.own_ref, bf16[512,128]{1,0:T(8,128)(2,1)S(1)} %get-tuple-element.41.bg_ref, bf16[3584,128]{1,0:T(8,128)(2,1)S(1)} %get-tuple-element.44.active_ref, ...), custom_call_target="tpu_custom_call" | custom-call | flops 503316480 | bytes 2097152 | tf_op jit(solution)/shard_map/pallas_call | solution.py:28
  20.8 1.5 %collective-permute-done.2.far_ref = bf16[896,128]{1,0:T(8,128)(2,1)S(1)} collective-permute-done((bf16[896,128]{1,0:T(8,128)(2,1)S(1)}, bf16[896,128]{1,0:T(8,128)(2,1)S(1)}, u32[]{:S(2)}, u32[]{:S(2)}) %collective-permute-start.2) | collective-permute-done | bytes 229408 | tf_op jit(solution)/shard_map/ppermute | solution.py:351
  22.3 2.5 %shard_map.78 = (bf16[768,128]{1,0:T(8,128)(2,1)S(1)}, bf16[640,128]{1,0:T(8,128)(2,1)S(1)}) custom-call(bf16[896,128]{1,0:T(8,128)(2,1)S(1)} %collective-permute-done.2.far_ref, bf16[768,128]{1,0:T(8,128)(2,1)S(1)} %shard_map.77.part_ref, bf16[1024,128]{1,0:T(8,128)(2,1)S(1)} %get-tuple-element.40.state_ref.own_ref, ...), custom_call_target="tpu_custom_call" | custom-call | flops 503316480 | bytes 2097152 | tf_op jit(solution)/shard_map/pallas_call | solution.py:28
  24.8 0.1 collective-permute-start.5
  24.9 2.3 %collective-permute-start.4 = (bf16[640,128]{1,0:T(8,128)(2,1)S(1)}, bf16[640,128]{1,0:T(8,128)(2,1)S(1)}, u32[]{:S(2)}, u32[]{:S(2)}) collective-permute-start(bf16[640,128]{1,0:T(8,128)(2,1)S(1)} %get-tuple-element.49), channel_id=1, source_target_pairs={{8,16},{24,32},{40,48},{56,64},{72,80},{88,96},{104,112},{120,0},{... | collective-permute-start | bytes 491528 | tf_op jit(solution)/shard_map/ppermute | solution.py:351
  27.1 2.0 %shard_map.79 = (bf16[2560,128]{1,0:T(8,128)(2,1)S(1)}, bf16[640,128]{1,0:T(8,128)(2,1)S(1)}) custom-call(bf16[768,128]{1,0:T(8,128)(2,1)S(1)} %get-tuple-element.50.state_ref.own_ref, bf16[256,576]{1,0:T(8,128)(2,1)S(1)} %get-tuple-element.42.kernel_ref, f32[256,128]{1,0:T(8,128)S(1)} %get-tuple-element.43.bias_ref, bf16[64,256]{1,0:T(8,128)(2,1)S(1)} %copy-done), custom_call_target="tpu_custom_call" | custom-call | flops 419430400 | bytes 2097152 | tf_op jit(solution)/shard_map/pallas_call | solution.py:28
  29.1 0.0 collective-permute-done.5.near_ref
  29.1 0.8 %shard_map.80.part_ref = bf16[512,128]{1,0:T(8,128)(2,1)S(1)} custom-call(bf16[640,128]{1,0:T(8,128)(2,1)S(1)} %collective-permute-done.5.near_ref, bf16[768,128]{1,0:T(8,128)(2,1)S(1)} %get-tuple-element.50.state_ref.own_ref, bf16[512,128]{1,0:T(8,128)(2,1)S(1)} %get-tuple-element.41.bg_ref, bf16[2560,128]{1,0:T(8,128)(2,1)S(1)} %get-tuple-element.51.active_ref, ...), custom_call_target="tpu_custom_call" | custom-call | flops 335544320 | bytes 2097152 | tf_op jit(solution)/shard_map/pallas_call | solution.py:28
  29.9 3.5 %collective-permute-done.4.far_ref = bf16[640,128]{1,0:T(8,128)(2,1)S(1)} collective-permute-done((bf16[640,128]{1,0:T(8,128)(2,1)S(1)}, bf16[640,128]{1,0:T(8,128)(2,1)S(1)}, u32[]{:S(2)}, u32[]{:S(2)}) %collective-permute-start.4) | collective-permute-done | bytes 163872 | tf_op jit(solution)/shard_map/ppermute | solution.py:351
  33.5 2.4 %shard_map.81 = bf16[64,8,128]{2,1,0:T(8,128)(2,1)} custom-call(bf16[640,128]{1,0:T(8,128)(2,1)S(1)} %collective-permute-done.4.far_ref, bf16[512,128]{1,0:T(8,128)(2,1)S(1)} %shard_map.80.part_ref, bf16[768,128]{1,0:T(8,128)(2,1)S(1)} %get-tuple-element.50.state_ref.own_ref, bf16[512,128]{1,0:T(8,128)(2,1)S(1)} %get-tuple-element.41.bg_ref, ...), custom_call_target="tpu_custom_call" | custom-call | flops 335544320 | bytes 2097152 | tf_op jit(solution)/shard_map/pallas_call | solution.py:28
Async XLA Ops:
  0.0 7.1 %copy-start = (bf16[64,256]{1,0:T(8,128)(2,1)S(1)}, bf16[64,256]{1,0:T(8,128)(2,1)}, u32[]{:S(2)}) copy-start(bf16[64,256]{1,0:T(8,128)(2,1)} %out_weight_ref.13) | copy-start | bytes 98308
  0.0 7.1 %copy-start.2 = (bf16[1,64,256]{2,1,0:T(8,128)(2,1)S(1)}, bf16[1,64,256]{2,1,0:T(8,128)(2,1)}, u32[]{:S(2)}) copy-start(bf16[1,64,256]{2,1,0:T(8,128)(2,1)} %param.9) | copy-start | bytes 98308
  1.3 8.5 %collective-permute-start = (bf16[384,128]{1,0:T(8,128)(2,1)S(1)}, bf16[384,128]{1,0:T(8,128)(2,1)S(1)}, u32[]{:S(2)}, u32[]{:S(2)}) collective-permute-start(bf16[384,128]{1,0:T(8,128)(2,1)S(1)} %get-tuple-element.30), channel_id=1, source_target_pairs={{0,1},{1,2},{2,3},{3,4},{4,5},{5,6},{6,7},{7,0},{8,9},{9,10},{10,1... | collective-permute-start | bytes 294920 | tf_op jit(solution)/shard_map/ppermute | solution.py:345
  4.7 2.3 %copy-start.4 = (f32[256]{0:T(256)S(1)}, f32[256]{0:T(256)}, u32[]{:S(2)}) copy-start(f32[256]{0:T(256)} %param.12) | copy-start | bytes 3076
  4.7 7.1 %collective-permute-start.1 = (bf16[384,128]{1,0:T(8,128)(2,1)S(1)}, bf16[384,128]{1,0:T(8,128)(2,1)S(1)}, u32[]{:S(2)}, u32[]{:S(2)}) collective-permute-start(bf16[384,128]{1,0:T(8,128)(2,1)S(1)} %get-tuple-element.31), channel_id=1, source_target_pairs={{0,7},{1,0},{2,1},{3,2},{4,3},{5,4},{6,5},{7,6},{8,15},{9,8},{10,9... | collective-permute-start | bytes 294920 | tf_op jit(solution)/shard_map/ppermute | solution.py:345
  7.0 0.7 %copy-start.3 = (s32[1,256]{1,0:T(1,128)S(1)}, s32[1,256]{1,0:T(1,128)}, u32[]{:S(2)}) copy-start(s32[1,256]{1,0:T(1,128)} %index_ref.1) | copy-start | bytes 3076
  7.7 1.0 %copy-start.1 = (bf16[3,3,256,64]{2,3,1,0:T(8,128)(2,1)S(1)}, bf16[3,3,256,64]{2,3,1,0:T(8,128)(2,1)}, u32[]{:S(2)}) copy-start(bf16[3,3,256,64]{2,3,1,0:T(8,128)(2,1)} %param.11) | copy-start | bytes 884740
  11.9 7.8 %collective-permute-start.3 = (bf16[896,128]{1,0:T(8,128)(2,1)S(1)}, bf16[896,128]{1,0:T(8,128)(2,1)S(1)}, u32[]{:S(2)}, u32[]{:S(2)}) collective-permute-start(bf16[896,128]{1,0:T(8,128)(2,1)S(1)} %get-tuple-element.39), channel_id=1, source_target_pairs={{0,8},{16,24},{32,40},{48,56},{64,72},{80,88},{96,104},{112,120},{... | collective-permute-start | bytes 688136 | tf_op jit(solution)/shard_map/ppermute | solution.py:351
  12.0 10.3 %collective-permute-start.2 = (bf16[896,128]{1,0:T(8,128)(2,1)S(1)}, bf16[896,128]{1,0:T(8,128)(2,1)S(1)}, u32[]{:S(2)}, u32[]{:S(2)}) collective-permute-start(bf16[896,128]{1,0:T(8,128)(2,1)S(1)} %get-tuple-element.39), channel_id=1, source_target_pairs={{8,16},{24,32},{40,48},{56,64},{72,80},{88,96},{104,112},{120,0},{... | collective-permute-start | bytes 688136 | tf_op jit(solution)/shard_map/ppermute | solution.py:351
  24.8 4.3 %collective-permute-start.5 = (bf16[640,128]{1,0:T(8,128)(2,1)S(1)}, bf16[640,128]{1,0:T(8,128)(2,1)S(1)}, u32[]{:S(2)}, u32[]{:S(2)}) collective-permute-start(bf16[640,128]{1,0:T(8,128)(2,1)S(1)} %get-tuple-element.49), channel_id=1, source_target_pairs={{0,8},{16,24},{32,40},{48,56},{64,72},{80,88},{96,104},{112,120},{... | collective-permute-start | bytes 491528 | tf_op jit(solution)/shard_map/ppermute | solution.py:351
  24.9 8.6 %collective-permute-start.4 = (bf16[640,128]{1,0:T(8,128)(2,1)S(1)}, bf16[640,128]{1,0:T(8,128)(2,1)S(1)}, u32[]{:S(2)}, u32[]{:S(2)}) collective-permute-start(bf16[640,128]{1,0:T(8,128)(2,1)S(1)} %get-tuple-element.49), channel_id=1, source_target_pairs={{8,16},{24,32},{40,48},{56,64},{72,80},{88,96},{104,112},{120,0},{... | collective-permute-start | bytes 491528 | tf_op jit(solution)/shard_map/ppermute | solution.py:351

commit v4 on v3

--- a/solution.py
+++ b/solution.py
@@ -71,7 +71,7 @@
 
 
 def pack_kernel(
-    x_hbm, bg_hbm, obs_hbm, index_hbm, own_ref, bg_rows_ref, up_ref, down_ref,
+    x_hbm, bg_hbm, obs_hbm, index_hbm, own_ref, bg_rows_ref, first_ref, second_ref,
     x_ref, bg_ref, obs_ref, index_ref, xs, bs, sems,
 ):
     copies = [
@@ -83,40 +83,49 @@
     for copy in copies:
         copy.start()
     copies[0].wait()
+    even = lax.rem(lax.axis_index("lat"), 2) == 0
+
+    def send(place, up, down):
+        at = slice(place * C, (place + 1) * C)
+        first_ref[at, :] = jnp.where(even, down, up).astype(BF16)
+        second_ref[at, :] = jnp.where(even, up, down).astype(BF16)
+
     xs[...] = x_ref[...].astype(F32).reshape(ROWS * C, LON)
-    for row in range(ROWS):
-        value = xs[latitude(row), :].astype(BF16)
-        own_ref[row * C : (row + 1) * C, :] = value
-        if row < 4:
-            up_ref[row * C : (row + 1) * C, :] = value
-        else:
-            down_ref[(row - 4) * C : (row - 3) * C, :] = value
+    for row in range(4):
+        up, down = xs[latitude(row), :], xs[latitude(row + 4), :]
+        own_ref[row * C : (row + 1) * C, :] = up.astype(BF16)
+        own_ref[(row + 4) * C : (row + 5) * C, :] = down.astype(BF16)
+        send(row, up, down)
     copies[1].wait()
     copies[2].wait()
     low, high = local_cells(index_ref[...])
     values = with_ones(obs_ref[...])
-    sums = [observation_sums(values, low, high, row) for row in (0, 1, 6, 7)]
     copies[3].wait()
     bs[...] = bg_ref[...].astype(F32).reshape(ROWS * C, LON)
     opening = lax.axis_index("tm") == 0
+
+    def edge(row):
+        own = xs[latitude(row), :]
+        ground = bs[latitude(row), :]
+        value = innovation_of(observation_sums(values, low, high, row), own)
+        return value + jnp.where(opening, own - ground, 0.0)
+
+    for row in range(2):
+        send(4 + row, edge(row), edge(row + 6))
     for row in range(ROWS):
-        ground = bs[latitude(row), :]
-        bg_rows_ref[row * C : (row + 1) * C, :] = ground.astype(BF16)
-        if row < 2 or row >= 6:
-            own = xs[latitude(row), :]
-            edge = innovation_of(sums[row if row < 2 else row - 4], own)
-            edge = edge + jnp.where(opening, own - ground, 0.0)
-            ref, place = (up_ref, row) if row < 2 else (down_ref, row - 6)
-            ref[X_PART + place * C : X_PART + (place + 1) * C, :] = edge.astype(BF16)
-
-
-def extend_kernel(own_ref, above_ref, below_ref, ext_ref, sent_ref):
+        bg_rows_ref[row * C : (row + 1) * C, :] = bs[latitude(row), :].astype(BF16)
+
+
+def extend_kernel(own_ref, first_ref, second_ref, ext_ref, sent_ref, above_edge_ref, below_edge_ref):
     strip = lax.axis_index("lat")
-    first = strip > 0
-    last = strip < lax.axis_size("lat") - 1
+    even = lax.rem(strip, 2) == 0
     zero = jnp.zeros((X_PART, LON), BF16)
-    above = jnp.where(first, above_ref[:X_PART, :], zero)
-    below = jnp.where(last, below_ref[:X_PART, :], zero)
+    above = jnp.where(even, second_ref[...], first_ref[...])
+    below = jnp.where(even, first_ref[...], second_ref[...])
+    above_edge_ref[...] = above[X_PART:, :]
+    below_edge_ref[...] = below[X_PART:, :]
+    above = jnp.where(strip > 0, above[:X_PART, :], zero)
+    below = jnp.where(strip < lax.axis_size("lat") - 1, below[:X_PART, :], zero)
     ext_ref[:X_PART, :] = above
     ext_ref[X_PART : X_PART + ROWS * C, :] = own_ref[...]
     ext_ref[X_PART + ROWS * C :, :] = below
@@ -308,9 +317,9 @@
 ):
     def innovation(place, own):
         if place < 0:
-            return rows_of(above_ref, 6 + place).astype(F32)
+            return rows_of(above_ref, 2 + place).astype(F32)
         if place >= ROWS:
-            return rows_of(below_ref, 4 + place - ROWS).astype(F32)
+            return rows_of(below_ref, place - ROWS).astype(F32)
         return innovation_of(sums_ref[place], own)
 
     def emit(row, value):
@@ -340,15 +349,34 @@
     out_ref[...] = wide[...].reshape(C, ROWS, LON).astype(BF16)
 
 
-def ring(value, axis, by):
-    count = lax.axis_size(axis)
-    return lax.ppermute(value, axis, [(i, (i + by) % count) for i in range(count)])
-
-
-def swap(value, first):
-    count = lax.axis_size("tm")
-    pairs = [(i, (i + 1) % count) for i in range(first, count, 2)]
-    return lax.ppermute(value, "tm", pairs + [(j, i) for i, j in pairs])
+def exchange(value, partner):
+    windows, strips = lax.axis_size("tm"), lax.axis_size("lat")
+    pairs = []
+    for window in range(windows):
+        for strip in range(strips):
+            to_window, to_strip = partner(window, strip, windows - 1, strips - 1)
+            pairs.append((window * strips + strip, to_window * strips + to_strip))
+    return lax.ppermute(value, ("tm", "lat"), pairs)
+
+
+def near_strip(window, strip, last_window, last_strip):
+    return window, strip ^ 1
+
+
+def far_strip(window, strip, last_window, last_strip):
+    if strip in (0, last_strip):
+        return window ^ 1, strip
+    return window, ((strip + 1) ^ 1) - 1
+
+
+def near_window(window, strip, last_window, last_strip):
+    return window ^ 1, strip
+
+
+def far_window(window, strip, last_window, last_strip):
+    if window in (0, last_window):
+        return window, strip ^ 1
+    return ((window + 1) ^ 1) - 1, strip
 
 
 def shape(rows, dtype=BF16):
@@ -374,7 +402,7 @@
     window_snapshots, background, obs_values, obs_index, input_kernel_weight, hidden_bias_vector,
     output_pointwise_weight,
 ):
-    own, ground, up, down = call(
+    own, ground, first, second = call(
         pack_kernel,
         (shape(ROWS * C), shape(ROWS * C), shape(PAYLOAD), shape(PAYLOAD)),
         [
@@ -393,8 +421,8 @@
             for value in (window_snapshots[0], background, obs_values[0], obs_index)
         )
     )
-    below = ring(up, "lat", -1)
-    above = ring(down, "lat", 1)
+    first = exchange(first, near_strip)
+    second = exchange(second, far_strip)
 
     out_weight = output_pointwise_weight
     taps = jnp.transpose(input_kernel_weight, (0, 1, 3, 2)).reshape(9 * C, HID)
@@ -409,17 +437,17 @@
         ),
         [], ROWS * 2 * 80 * OBS * LON, 1 << 20,
     )(obs_values[0], obs_index, taps, hidden_bias_vector[None, :], out_weight)
-    above, below, prepared = lax.optimization_barrier((above, below, prepared))
+    first, second, prepared = lax.optimization_barrier((first, second, prepared))
     sums, forward_weight, back_weight, bias, out_back = prepared
 
-    ext, sent = call(extend_kernel, (shape(16 * C), shape(14 * C)), [], 0, 1 << 20)(
-        own, above, below
-    )
+    ext, sent, above, below = call(
+        extend_kernel, (shape(16 * C), shape(14 * C), shape(2 * C), shape(2 * C)), [], 0, 1 << 20
+    )(own, first, second)
     weights = (forward_weight, bias, out_weight, back_weight, out_back)
 
-    def exchange(sent):
-        far = swap(sent, 1)
-        near = swap(sent, 0)
+    def share(sent):
+        far = exchange(sent, far_window)
+        near = exchange(sent, near_window)
         return far, near
 
     def forward(count, state):
@@ -436,13 +464,13 @@
             shape(count * C), gradient_scratch(count), row_flops(count), 2 << 20,
         )(near, *given)
 
-    far, near = exchange(sent)
+    far, near = share(sent)
     given = (ext, ground, *forward(14, ext), *weights)
     part = near_part(12, 2, near, *given)
     state, sent = call(
         first_kernel, (shape(12 * C), shape(10 * C)), gradient_scratch(12), row_flops(12), 2 << 20
     )(far, part, *given, sums, above, below)
-    far, near = exchange(sent)
+    far, near = share(sent)
     given = (state, ground, *forward(10, state), *weights)
     part = near_part(8, 0, near, *given)
     analysis = call(

time: 36 us -> 32.3 us (0.90)
  the two profiles are of different devices: /device:TPU:0 before, /device:TPU:4 now
where the time goes in v4:
time: 32.3 us; the launch traced here: 32.1 us
  Pallas kernels  13.1 us (41%)
  waiting for transfers between devices  10.6 us (33%)
  starting transfers between devices  6.73 us (21%)
  local copies, waits for them, and re-layouts  1.64 us (5%)
    pallas_call x9, Pallas kernels, run(): pl.pallas_call(kernel, out_shape=outs, in_specs=[spec] * len(args), out_s...  13.1 us
    ppermute x6, waiting for transfers between devices, exchange(): return lax.ppermute(value, ('tm', 'lat'), pairs)  10.6 us
    ppermute x6, starting transfers between devices, exchange(): return lax.ppermute(value, ('tm', 'lat'), pairs)  6.73 us
    unnamed x10, local copies, waits for them, and re-layouts  1.64 us
  transfers between devices with their start and end apart: 6, of which 4 were waited for; matrix products, arithmetic and copies ran while one was open for 0% of the time, Pallas kernels for 21%

profile of v4, /device:TPU:4, one launch (start us, length us, event | category | flops | bytes accessed | tf_op | source)
XLA Modules:
  0.0 32.1 jit_solution(5823531255033447136)
XLA Ops:
  0.0 0.0 copy-start
  0.0 0.0 copy-start.2
  0.0 1.3 %shard_map.73 = (bf16[512,128]{1,0:T(8,128)(2,1)S(1)}, bf16[512,128]{1,0:T(8,128)(2,1)S(1)}, bf16[384,128]{1,0:T(8,128)(2,1)S(1)}, bf16[384,128]{1,0:T(8,128)(2,1)S(1)}) custom-call(bf16[64,8,128]{2,1,0:T(8,128)(2,1)} %bitcast.11, bf16[64,8,128]{2,1,0:T(8,128)(2,1)} %bg_hbm.1, bf16[64,256]{1,0:T(8,128)(2,1)} %bitcast.8, s32[1,256]{1,0:T(1,128)} %index_ref.1), custom_call_target="tpu_custom_call" | custom-call | bytes 1048576 | tf_op jit(solution)/shard_map/pallas_call | solution.py:28
  1.3 3.3 %collective-permute-start = (bf16[384,128]{1,0:T(8,128)(2,1)S(1)}, bf16[384,128]{1,0:T(8,128)(2,1)S(1)}, u32[]{:S(2)}, u32[]{:S(2)}) collective-permute-start(bf16[384,128]{1,0:T(8,128)(2,1)S(1)} %get-tuple-element.32), channel_id=1, source_target_pairs={{0,1},{1,0},{2,3},{3,2},{4,5},{5,4},{6,7},{7,6},{8,9},{9,8},{10,11... | collective-permute-start | bytes 294920 | tf_op jit(solution)/shard_map/ppermute | solution.py:359
  4.6 0.0 copy-start.4
  4.6 0.3 collective-permute-start.1
  4.9 0.0 copy-start.3
  4.9 0.0 copy-done
  4.9 0.0 copy-done.2
  4.9 0.4 %copy-done.4 = f32[256]{0:T(256)S(1)} copy-done((f32[256]{0:T(256)S(1)}, f32[256]{0:T(256)}, u32[]{:S(2)}) %copy-start.4) | copy-done | bytes 1048
  5.2 0.3 copy-done.3
  5.6 0.0 copy-start.1
  5.6 1.0 %copy-done.1 = bf16[3,3,256,64]{2,3,1,0:T(8,128)(2,1)S(1)} copy-done((bf16[3,3,256,64]{2,3,1,0:T(8,128)(2,1)S(1)}, bf16[3,3,256,64]{2,3,1,0:T(8,128)(2,1)}, u32[]{:S(2)}) %copy-start.1) | copy-done | bytes 294936
  6.5 0.3 shard_map.74
  6.8 1.9 %collective-permute-done.first_ref = bf16[384,128]{1,0:T(8,128)(2,1)S(1)} collective-permute-done((bf16[384,128]{1,0:T(8,128)(2,1)S(1)}, bf16[384,128]{1,0:T(8,128)(2,1)S(1)}, u32[]{:S(2)}, u32[]{:S(2)}) %collective-permute-start) | collective-permute-done | bytes 98336 | tf_op jit(solution)/shard_map/ppermute | solution.py:359
  8.7 2.9 %collective-permute-done.1.second_ref = bf16[384,128]{1,0:T(8,128)(2,1)S(1)} collective-permute-done((bf16[384,128]{1,0:T(8,128)(2,1)S(1)}, bf16[384,128]{1,0:T(8,128)(2,1)S(1)}, u32[]{:S(2)}, u32[]{:S(2)}) %collective-permute-start.1) | collective-permute-done | bytes 98336 | tf_op jit(solution)/shard_map/ppermute | solution.py:359
  11.6 0.1 shard_map.75
  11.7 0.1 collective-permute-start.3
  11.8 1.2 %collective-permute-start.2 = (bf16[896,128]{1,0:T(8,128)(2,1)S(1)}, bf16[896,128]{1,0:T(8,128)(2,1)S(1)}, u32[]{:S(2)}, u32[]{:S(2)}) collective-permute-start(bf16[896,128]{1,0:T(8,128)(2,1)S(1)} %get-tuple-element.41), channel_id=1, source_target_pairs={{0,1},{1,0},{2,3},{3,2},{4,5},{5,4},{6,7},{7,6},{8,16},{9,17},{10,... | collective-permute-start | bytes 688136 | tf_op jit(solution)/shard_map/ppermute | solution.py:359
  13.0 2.7 %shard_map.76 = (bf16[3584,128]{1,0:T(8,128)(2,1)S(1)}, bf16[896,128]{1,0:T(8,128)(2,1)S(1)}) custom-call(bf16[1024,128]{1,0:T(8,128)(2,1)S(1)} %get-tuple-element.42.state_ref.own_ref, bf16[256,576]{1,0:T(8,128)(2,1)S(1)} %get-tuple-element.44.kernel_ref, f32[256,128]{1,0:T(8,128)S(1)} %get-tuple-element.45.bias_ref, bf16[64,256]{1,0:T(8,128)(2,1)S(1)} %copy-done), custom_call_target="tpu_custom_call" | custom-call | flops 587202560 | bytes 2097152 | tf_op jit(solution)/shard_map/pallas_call | solution.py:28
  15.7 0.0 collective-permute-done.3.near_ref
  15.7 1.0 %shard_map.77.part_ref = bf16[768,128]{1,0:T(8,128)(2,1)S(1)} custom-call(bf16[896,128]{1,0:T(8,128)(2,1)S(1)} %collective-permute-done.3.near_ref, bf16[1024,128]{1,0:T(8,128)(2,1)S(1)} %get-tuple-element.42.state_ref.own_ref, bf16[512,128]{1,0:T(8,128)(2,1)S(1)} %get-tuple-element.43.bg_ref, bf16[3584,128]{1,0:T(8,128)(2,1)S(1)} %get-tuple-element.46.active_ref, ...), custom_call_target="tpu_custom_call" | custom-call | flops 503316480 | bytes 2097152 | tf_op jit(solution)/shard_map/pallas_call | solution.py:28
  16.7 3.5 %collective-permute-done.2.far_ref = bf16[896,128]{1,0:T(8,128)(2,1)S(1)} collective-permute-done((bf16[896,128]{1,0:T(8,128)(2,1)S(1)}, bf16[896,128]{1,0:T(8,128)(2,1)S(1)}, u32[]{:S(2)}, u32[]{:S(2)}) %collective-permute-start.2) | collective-permute-done | bytes 229408 | tf_op jit(solution)/shard_map/ppermute | solution.py:359
  20.3 2.5 %shard_map.78 = (bf16[768,128]{1,0:T(8,128)(2,1)S(1)}, bf16[640,128]{1,0:T(8,128)(2,1)S(1)}) custom-call(bf16[896,128]{1,0:T(8,128)(2,1)S(1)} %collective-permute-done.2.far_ref, bf16[768,128]{1,0:T(8,128)(2,1)S(1)} %shard_map.77.part_ref, bf16[1024,128]{1,0:T(8,128)(2,1)S(1)} %get-tuple-element.42.state_ref.own_ref, ...), custom_call_target="tpu_custom_call" | custom-call | flops 503316480 | bytes 2097152 | tf_op jit(solution)/shard_map/pallas_call | solution.py:28
  22.7 0.1 collective-permute-start.5
  22.8 1.8 %collective-permute-start.4 = (bf16[640,128]{1,0:T(8,128)(2,1)S(1)}, bf16[640,128]{1,0:T(8,128)(2,1)S(1)}, u32[]{:S(2)}, u32[]{:S(2)}) collective-permute-start(bf16[640,128]{1,0:T(8,128)(2,1)S(1)} %get-tuple-element.53), channel_id=1, source_target_pairs={{0,1},{1,0},{2,3},{3,2},{4,5},{5,4},{6,7},{7,6},{8,16},{9,17},{10,... | collective-permute-start | bytes 491528 | tf_op jit(solution)/shard_map/ppermute | solution.py:359
  24.6 2.0 %shard_map.79 = (bf16[2560,128]{1,0:T(8,128)(2,1)S(1)}, bf16[640,128]{1,0:T(8,128)(2,1)S(1)}) custom-call(bf16[768,128]{1,0:T(8,128)(2,1)S(1)} %get-tuple-element.54.state_ref.own_ref, bf16[256,576]{1,0:T(8,128)(2,1)S(1)} %get-tuple-element.44.kernel_ref, f32[256,128]{1,0:T(8,128)S(1)} %get-tuple-element.45.bias_ref, bf16[64,256]{1,0:T(8,128)(2,1)S(1)} %copy-done), custom_call_target="tpu_custom_call" | custom-call | flops 419430400 | bytes 2097152 | tf_op jit(solution)/shard_map/pallas_call | solution.py:28
  26.5 0.0 collective-permute-done.5.near_ref
  26.6 0.9 %shard_map.80.part_ref = bf16[512,128]{1,0:T(8,128)(2,1)S(1)} custom-call(bf16[640,128]{1,0:T(8,128)(2,1)S(1)} %collective-permute-done.5.near_ref, bf16[768,128]{1,0:T(8,128)(2,1)S(1)} %get-tuple-element.54.state_ref.own_ref, bf16[512,128]{1,0:T(8,128)(2,1)S(1)} %get-tuple-element.43.bg_ref, bf16[2560,128]{1,0:T(8,128)(2,1)S(1)} %get-tuple-element.55.active_ref, ...), custom_call_target="tpu_custom_call" | custom-call | flops 335544320 | bytes 2097152 | tf_op jit(solution)/shard_map/pallas_call | solution.py:28
  27.4 2.3 %collective-permute-done.4.far_ref = bf16[640,128]{1,0:T(8,128)(2,1)S(1)} collective-permute-done((bf16[640,128]{1,0:T(8,128)(2,1)S(1)}, bf16[640,128]{1,0:T(8,128)(2,1)S(1)}, u32[]{:S(2)}, u32[]{:S(2)}) %collective-permute-start.4) | collective-permute-done | bytes 163872 | tf_op jit(solution)/shard_map/ppermute | solution.py:359
  29.7 2.4 %shard_map.81 = bf16[64,8,128]{2,1,0:T(8,128)(2,1)} custom-call(bf16[640,128]{1,0:T(8,128)(2,1)S(1)} %collective-permute-done.4.far_ref, bf16[512,128]{1,0:T(8,128)(2,1)S(1)} %shard_map.80.part_ref, bf16[768,128]{1,0:T(8,128)(2,1)S(1)} %get-tuple-element.54.state_ref.own_ref, bf16[512,128]{1,0:T(8,128)(2,1)S(1)} %get-tuple-element.43.bg_ref, ...), custom_call_target="tpu_custom_call" | custom-call | flops 335544320 | bytes 2097152 | tf_op jit(solution)/shard_map/pallas_call | solution.py:28
Async XLA Ops:
  0.0 4.9 %copy-start = (bf16[64,256]{1,0:T(8,128)(2,1)S(1)}, bf16[64,256]{1,0:T(8,128)(2,1)}, u32[]{:S(2)}) copy-start(bf16[64,256]{1,0:T(8,128)(2,1)} %out_weight_ref.13) | copy-start | bytes 98308
  0.0 4.9 %copy-start.2 = (bf16[1,64,256]{2,1,0:T(8,128)(2,1)S(1)}, bf16[1,64,256]{2,1,0:T(8,128)(2,1)}, u32[]{:S(2)}) copy-start(bf16[1,64,256]{2,1,0:T(8,128)(2,1)} %param.9) | copy-start | bytes 98308
  1.3 7.4 %collective-permute-start = (bf16[384,128]{1,0:T(8,128)(2,1)S(1)}, bf16[384,128]{1,0:T(8,128)(2,1)S(1)}, u32[]{:S(2)}, u32[]{:S(2)}) collective-permute-start(bf16[384,128]{1,0:T(8,128)(2,1)S(1)} %get-tuple-element.32), channel_id=1, source_target_pairs={{0,1},{1,0},{2,3},{3,2},{4,5},{5,4},{6,7},{7,6},{8,9},{9,8},{10,11... | collective-permute-start | bytes 294920 | tf_op jit(solution)/shard_map/ppermute | solution.py:359
  4.6 0.7 %copy-start.4 = (f32[256]{0:T(256)S(1)}, f32[256]{0:T(256)}, u32[]{:S(2)}) copy-start(f32[256]{0:T(256)} %param.12) | copy-start | bytes 3076
  4.6 7.0 %collective-permute-start.1 = (bf16[384,128]{1,0:T(8,128)(2,1)S(1)}, bf16[384,128]{1,0:T(8,128)(2,1)S(1)}, u32[]{:S(2)}, u32[]{:S(2)}) collective-permute-start(bf16[384,128]{1,0:T(8,128)(2,1)S(1)} %get-tuple-element.33), channel_id=1, source_target_pairs={{0,8},{1,2},{2,1},{3,4},{4,3},{5,6},{6,5},{7,15},{8,0},{9,10},{10,... | collective-permute-start | bytes 294920 | tf_op jit(solution)/shard_map/ppermute | solution.py:359
  4.9 0.7 %copy-start.3 = (s32[1,256]{1,0:T(1,128)S(1)}, s32[1,256]{1,0:T(1,128)}, u32[]{:S(2)}) copy-start(s32[1,256]{1,0:T(1,128)} %index_ref.1) | copy-start | bytes 3076
  5.6 1.0 %copy-start.1 = (bf16[3,3,256,64]{2,3,1,0:T(8,128)(2,1)S(1)}, bf16[3,3,256,64]{2,3,1,0:T(8,128)(2,1)}, u32[]{:S(2)}) copy-start(bf16[3,3,256,64]{2,3,1,0:T(8,128)(2,1)} %param.11) | copy-start | bytes 884740
  11.7 4.0 %collective-permute-start.3 = (bf16[896,128]{1,0:T(8,128)(2,1)S(1)}, bf16[896,128]{1,0:T(8,128)(2,1)S(1)}, u32[]{:S(2)}, u32[]{:S(2)}) collective-permute-start(bf16[896,128]{1,0:T(8,128)(2,1)S(1)} %get-tuple-element.41), channel_id=1, source_target_pairs={{0,8},{1,9},{2,10},{3,11},{4,12},{5,13},{6,14},{7,15},{8,0},{9,1},... | collective-permute-start | bytes 688136 | tf_op jit(solution)/shard_map/ppermute | solution.py:359
  11.8 8.5 %collective-permute-start.2 = (bf16[896,128]{1,0:T(8,128)(2,1)S(1)}, bf16[896,128]{1,0:T(8,128)(2,1)S(1)}, u32[]{:S(2)}, u32[]{:S(2)}) collective-permute-start(bf16[896,128]{1,0:T(8,128)(2,1)S(1)} %get-tuple-element.41), channel_id=1, source_target_pairs={{0,1},{1,0},{2,3},{3,2},{4,5},{5,4},{6,7},{7,6},{8,16},{9,17},{10,... | collective-permute-start | bytes 688136 | tf_op jit(solution)/shard_map/ppermute | solution.py:359
  22.7 3.8 %collective-permute-start.5 = (bf16[640,128]{1,0:T(8,128)(2,1)S(1)}, bf16[640,128]{1,0:T(8,128)(2,1)S(1)}, u32[]{:S(2)}, u32[]{:S(2)}) collective-permute-start(bf16[640,128]{1,0:T(8,128)(2,1)S(1)} %get-tuple-element.53), channel_id=1, source_target_pairs={{0,8},{1,9},{2,10},{3,11},{4,12},{5,13},{6,14},{7,15},{8,0},{9,1},... | collective-permute-start | bytes 491528 | tf_op jit(solution)/shard_map/ppermute | solution.py:359
  22.8 6.9 %collective-permute-start.4 = (bf16[640,128]{1,0:T(8,128)(2,1)S(1)}, bf16[640,128]{1,0:T(8,128)(2,1)S(1)}, u32[]{:S(2)}, u32[]{:S(2)}) collective-permute-start(bf16[640,128]{1,0:T(8,128)(2,1)S(1)} %get-tuple-element.53), channel_id=1, source_target_pairs={{0,1},{1,0},{2,3},{3,2},{4,5},{5,4},{6,7},{7,6},{8,16},{9,17},{10,... | collective-permute-start | bytes 491528 | tf_op jit(solution)/shard_map/ppermute | solution.py:359

commit v5 on v4

v5 whole, which is shorter than its diff:
```python
import functools

import jax
import jax.numpy as jnp
from jax import lax
from jax.experimental import pallas as pl
from jax.experimental.pallas import tpu as pltpu
from jax.sharding import PartitionSpec as P


C = 64
HID = 256
ROWS = 8
LON = 128
OBS = 256
STEP = 0.3

F32 = jnp.float32
BF16 = jnp.bfloat16
VMEM = pl.BlockSpec(memory_space=pltpu.VMEM)

X_PART = 4 * C
PAYLOAD = X_PART + 2 * C


def call(kernel, outs, scratch, flops, bytes_accessed, spec=VMEM, grant=48 << 20):
    def run(*args):
        return pl.pallas_call(
            kernel,
            out_shape=outs,
            in_specs=[spec] * len(args),
            out_specs=jax.tree.map(lambda _: VMEM, outs),
            scratch_shapes=scratch,
            cost_estimate=pl.CostEstimate(
                flops=flops, bytes_accessed=bytes_accessed, transcendentals=0
            ),
            compiler_params=pltpu.CompilerParams(vmem_limit_bytes=grant),
        )(*args)

    return run


def rows_of(ref, first, width=C):
    return ref[first * width : (first + 1) * width, :]


def rows_in(ref, first, count):
    return [(ref, row) for row in range(first, first + count)]


def at(rows, place, width=C):
    ref, row = rows[place]
    return rows_of(ref, row, width)


def beside(rows, a, b):
    return jnp.concatenate([at(rows, a), at(rows, b)], axis=1)


def latitude(row):
    return pl.ds(row, C, stride=ROWS)


def local_cells(index):
    local = index - lax.axis_index("lat") * (ROWS * LON)
    high = lax.shift_right_arithmetic(local, 7)
    return local - high * LON, high


def with_ones(values):
    return jnp.concatenate([values, jnp.ones((16, OBS), BF16)], axis=0)


def observation_sums(values, low, high, row):
    cell = lax.broadcasted_iota(jnp.int32, (LON, OBS), 0)
    hit = jnp.where((low == cell) & (high == row), 1.0, 0.0).astype(BF16)
    return lax.dot_general(
        values, hit, (((1,), (1,)), ((), ())), preferred_element_type=F32
    )


def innovation_of(sums, own):
    return sums[C : C + 1, :] * own - sums[:C, :]


def pack_kernel(
    x_hbm, bg_hbm, obs_hbm, index_hbm, own_ref, bg_rows_ref, first_ref, second_ref,
    x_ref, bg_ref, obs_ref, index_ref, xs, bs, sems,
):
    copies = [
        pltpu.make_async_copy(source, target, sems.at[place])
        for place, (source, target) in enumerate(
            ((x_hbm, x_ref), (obs_hbm, obs_ref), (index_hbm, index_ref), (bg_hbm, bg_ref))
        )
    ]
    for copy in copies:
        copy.start()
    copies[0].wait()
    even = lax.rem(lax.axis_index("lat"), 2) == 0

    def send(place, up, down):
        at = slice(place * C, (place + 1) * C)
        first_ref[at, :] = jnp.where(even, down, up).astype(BF16)
        second_ref[at, :] = jnp.where(even, up, down).astype(BF16)

    xs[...] = x_ref[...].astype(F32).reshape(ROWS * C, LON)
    for row in range(4):
        up, down = xs[latitude(row), :], xs[latitude(row + 4), :]
        own_ref[row * C : (row + 1) * C, :] = up.astype(BF16)
        own_ref[(row + 4) * C : (row + 5) * C, :] = down.astype(BF16)
        send(row, up, down)
    copies[1].wait()
    copies[2].wait()
    low, high = local_cells(index_ref[...])
    values = with_ones(obs_ref[...])
    copies[3].wait()
    bs[...] = bg_ref[...].astype(F32).reshape(ROWS * C, LON)
    opening = lax.axis_index("tm") == 0

    def edge(row):
        own = xs[latitude(row), :]
        ground = bs[latitude(row), :]
        value = innovation_of(observation_sums(values, low, high, row), own)
        return value + jnp.where(opening, own - ground, 0.0)

    for row in range(2):
        send(4 + row, edge(row), edge(row + 6))
    for row in range(ROWS):
        bg_rows_ref[row * C : (row + 1) * C, :] = bs[latitude(row), :].astype(BF16)


def extend_kernel(
    own_ref, first_ref, second_ref, ext_ref, near_ref, far_ref, above_edge_ref, below_edge_ref
):
    strip = lax.axis_index("lat")
    even = lax.rem(strip, 2) == 0
    zero = jnp.zeros((X_PART, LON), BF16)
    above = jnp.where(even, second_ref[...], first_ref[...])
    below = jnp.where(even, first_ref[...], second_ref[...])
    above_edge_ref[...] = above[X_PART:, :]
    below_edge_ref[...] = below[X_PART:, :]
    above = jnp.where(strip > 0, above[:X_PART, :], zero)
    below = jnp.where(strip < lax.axis_size("lat") - 1, below[:X_PART, :], zero)
    far_ref[: 3 * C, :] = above[C:, :]
    far_ref[3 * C :, :] = below[: 3 * C, :]
    near_ref[: 3 * C, :] = above[C:, :]
    near_ref[3 * C : 11 * C, :] = own_ref[...]
    near_ref[11 * C :, :] = below[: 3 * C, :]
    ext_ref[:X_PART, :] = above
    ext_ref[X_PART : X_PART + ROWS * C, :] = own_ref[...]
    ext_ref[X_PART + ROWS * C :, :] = below


def roll_rows(rows, shifted, pairs):
    for place in sorted({first + a for pair in pairs for first in pair for a in range(3)}):
        into = slice(place * C, (place + 1) * C)
        value = at(rows, place)
        wide = value.astype(F32)
        shifted[0, into, :] = pltpu.roll(wide, 1, 1).astype(BF16)
        shifted[1, into, :] = value
        shifted[2, into, :] = pltpu.roll(wide, LON - 1, 1).astype(BF16)


def hidden(shifted, kernel_ref, bias, pair):
    def stack(first):
        return jnp.concatenate(
            [
                shifted[b, (first + a) * C : (first + a + 1) * C, :]
                for a in range(3)
                for b in range(3)
            ],
            axis=0,
        )

    cells = jnp.concatenate([stack(row) for row in pair], axis=1)
    before = jnp.dot(kernel_ref[...], cells, preferred_element_type=F32) + bias
    return jnp.tanh(before).astype(BF16)


def store_pair(ref, first, value, width=C):
    ref[first * width : (first + 1) * width, :] = value[:, :LON]
    ref[(first + 1) * width : (first + 2) * width, :] = value[:, LON:]


def wide_bias(bias_ref):
    return jnp.concatenate([bias_ref[...], bias_ref[...]], axis=1)


def forward_kernel(
    pairs, state_ref, kernel_ref, bias_ref, out_weight_ref, active_ref, forecast_ref, shifted
):
    rows = rows_in(state_ref, 0, state_ref.shape[0] // C)
    roll_rows(rows, shifted, pairs)
    bias = wide_bias(bias_ref)
    for place, (a, b) in enumerate(pairs):
        active = hidden(shifted, kernel_ref, bias, (a, b))
        store_pair(active_ref, 2 * place, active, HID)
        step = jnp.dot(out_weight_ref[...], active, preferred_element_type=F32)
        centre = beside(rows, a + 1, b + 1).astype(F32)
        store_pair(forecast_ref, 2 * place, (centre + step).astype(BF16))


def prepare_kernel(
    obs_ref, index_ref, kernel_ref, bias_ref, out_weight_ref, sums_ref, forward_ref, back_ref,
    wide_bias_ref, out_back_ref,
):
    low, high = local_cells(index_ref[...])
    values = with_ones(obs_ref[...])
    for row in range(ROWS):
        sums_ref[row] = observation_sums(values, low, high, row)[:72, :]
    forward_ref[...] = kernel_ref[...].T
    out_back_ref[...] = out_weight_ref[...].T
    wide_bias_ref[...] = jnp.broadcast_to(bias_ref[...], (LON, HID)).T
    for a in range(3):
        back_ref[:, a * HID : (a + 1) * HID] = kernel_ref[(2 - a) * 3 * C : (3 - a) * 3 * C, :]


def residual_part(
    pairs, prev, own_ref, kernel_ref, bias_ref, out_weight_ref, shifted, take
):
    roll_rows(prev, shifted, pairs)
    bias = wide_bias(bias_ref)
    own_rows = rows_in(own_ref, 2, max(b for _, b in pairs) + 1)
    for a, b in pairs:
        active = hidden(shifted, kernel_ref, bias, (a, b))
        step = jnp.dot(out_weight_ref[...], active, preferred_element_type=F32)
        centre = beside(prev, a + 1, b + 1).astype(F32)
        guess = (centre + step).astype(BF16).astype(F32)
        resid = (beside(own_rows, a, b).astype(F32) - guess).astype(BF16)
        take(a, resid[:, :LON])
        take(b, resid[:, LON:])


def strip_ends():
    strip = lax.axis_index("lat")
    return -strip * ROWS, (lax.axis_size("lat") - strip) * ROWS


def adjoint_part(
    count, margin, later, active, forecast, back_ref, out_back_ref, cot, target, take
):
    top, bottom = strip_ends()
    for row in range(0, count + 2, 2):
        resid = beside(later, row, row + 1).astype(F32) - beside(forecast, row, row + 1).astype(F32)
        resid = resid.astype(BF16)
        store_pair(target, row, resid)
        projected = jnp.dot(out_back_ref[...], resid, preferred_element_type=F32)
        for half in range(2):
            place = row + half - margin - 1
            value = at(active, row + half, HID).astype(F32)
            value = (1.0 - value * value) * projected[:, half * LON : (half + 1) * LON]
            if not 0 <= place < ROWS:
                value = jnp.where((place >= top) & (place < bottom), value, 0.0)
            cot[(row + half) * HID : (row + half + 1) * HID, :] = value.astype(BF16)
    closing = lax.axis_index("tm") == lax.axis_size("tm") - 1
    for row in range(0, count, 2):
        cells = jnp.concatenate(
            [cot[row * HID : (row + 3) * HID, :], cot[(row + 1) * HID : (row + 4) * HID, :]], axis=1
        )
        spread = jnp.dot(back_ref[...], cells, preferred_element_type=F32)
        for half in range(2):
            lanes = slice(half * LON, (half + 1) * LON)
            pulled = (
                pltpu.roll(spread[:C, lanes], LON - 1, 1)
                + spread[C : 2 * C, lanes]
                + pltpu.roll(spread[2 * C :, lanes], 1, 1)
            )
            resid = rows_of(target, row + half + 1).astype(F32)
            take(row + half, jnp.where(closing, 0.0, resid + pulled).astype(BF16))


def branches():
    window = lax.axis_index("tm")
    even = lax.rem(window, 2) == 0
    opening = window == 0
    return even & jnp.logical_not(opening), opening, jnp.logical_not(even)


def in_order(count):
    return tuple((row, row + 1) for row in range(0, count, 2))


INNER = ((3, 4), (5, 6), (7, 8))
OUTER = ((0, 1), (2, 9), (10, 11))


def first_near_kernel(
    near_ref, far_own_ref, own_ref, active_in_ref, forecast_in_ref, active_out_ref, forecast_out_ref,
    kernel_ref, bias_ref, out_weight_ref, back_ref, out_back_ref, part_ref, inner_ref, shifted, cot,
    target,
):
    def put(ref):
        def take(row, value):
            ref[row * C : (row + 1) * C, :] = value

        return take

    even, _, odd = branches()

    @pl.when(jnp.logical_not(odd))
    def _():
        adjoint_part(
            12, 2, rows_in(near_ref, 0, 14), split_rows(active_out_ref, active_in_ref),
            split_rows(forecast_out_ref, forecast_in_ref), back_ref, out_back_ref, cot, target,
            put(part_ref),
        )

    @pl.when(even)
    def _():
        prev = [None] * 3 + rows_in(far_own_ref, 0, ROWS)
        residual_part(
            INNER, prev, own_ref, kernel_ref, bias_ref, out_weight_ref, shifted, put(inner_ref)
        )

    @pl.when(odd)
    def _():
        residual_part(
            in_order(12), rows_in(near_ref, 0, 14), own_ref, kernel_ref, bias_ref, out_weight_ref,
            shifted, put(part_ref),
        )


def split_rows(outside_ref, inside_ref):
    return rows_in(outside_ref, 0, 4) + rows_in(inside_ref, 0, 6) + rows_in(outside_ref, 4, 4)


def first_kernel(
    far_ref, far_own_ref, part_ref, inner_ref, own_ref, bg_ref, active_in_ref, forecast_in_ref,
    active_out_ref, forecast_out_ref, kernel_ref, bias_ref, out_weight_ref, back_ref, out_back_ref,
    sums_ref, above_ref, below_ref, state_ref, sent_ref, shifted, cot, target,
):
    top, bottom = strip_ends()

    def step(row, resid, adjoint):
        own = rows_of(own_ref, row + 2).astype(F32)
        place = row - 2
        if place < 0:
            innovation = rows_of(above_ref, row).astype(F32)
        elif place >= ROWS:
            innovation = rows_of(below_ref, place - ROWS).astype(F32)
        else:
            innovation = innovation_of(sums_ref[place], own)
        value = own - STEP * (resid.astype(F32) - adjoint.astype(F32) + innovation)
        if not 0 <= place < ROWS:
            value = jnp.where((place >= top) & (place < bottom), value, 0.0)
        value = value.astype(BF16)
        state_ref[row * C : (row + 1) * C, :] = value
        if 1 <= row < 11:
            sent_ref[(row - 1) * C : row * C, :] = value

    even, opening, odd = branches()
    far = rows_in(far_ref, 0, 3) + rows_in(far_own_ref, 0, ROWS) + rows_in(far_ref, 3, 3)

    @pl.when(even)
    def _():
        residual_part(
            OUTER, far, own_ref, kernel_ref, bias_ref, out_weight_ref, shifted,
            lambda row, resid: step(row, resid, rows_of(part_ref, row)),
        )
        for row in range(3, 9):
            step(row, rows_of(inner_ref, row), rows_of(part_ref, row))

    @pl.when(opening)
    def _():
        for row in range(12):
            place = row - 2
            resid = jnp.zeros((C, LON), BF16)
            if 0 <= place < ROWS:
                own = rows_of(own_ref, row + 2).astype(F32)
                resid = (own - rows_of(bg_ref, place).astype(F32)).astype(BF16)
            step(row, resid, rows_of(part_ref, row))

    @pl.when(odd)
    def _():
        adjoint_part(
            12, 2, far, split_rows(active_out_ref, active_in_ref),
            split_rows(forecast_out_ref, forecast_in_ref), back_ref, out_back_ref, cot, target,
            lambda row, adjoint: step(row, rows_of(part_ref, row), adjoint),
        )


def second_near_kernel(
    near_ref, own_ref, active_ref, forecast_ref, kernel_ref, bias_ref, out_weight_ref, back_ref,
    out_back_ref, part_ref, shifted, cot, target,
):
    def take(row, value):
        part_ref[row * C : (row + 1) * C, :] = value

    _, _, odd = branches()
    near = rows_in(near_ref, 0, 10)

    @pl.when(jnp.logical_not(odd))
    def _():
        adjoint_part(
            8, 0, near, rows_in(active_ref, 0, 10), rows_in(forecast_ref, 0, 10), back_ref,
            out_back_ref, cot, target, take,
        )

    @pl.when(odd)
    def _():
        residual_part(
            in_order(8), near, own_ref, kernel_ref, bias_ref, out_weight_ref, shifted, take
        )


def second_kernel(
    far_ref, part_ref, own_ref, bg_ref, active_ref, forecast_ref, kernel_ref, bias_ref,
    out_weight_ref, back_ref, out_back_ref, sums_ref, out_ref, shifted, cot, target, wide,
):
    def step(row, resid, adjoint):
        own = rows_of(own_ref, row + 2).astype(F32)
        innovation = innovation_of(sums_ref[row], own)
        value = own - STEP * (resid.astype(F32) - adjoint.astype(F32) + innovation)
        wide[latitude(row), :] = value

    even, opening, odd = branches()
    far = rows_in(far_ref, 0, 10)

    @pl.when(even)
    def _():
        residual_part(
            in_order(8), far, own_ref, kernel_ref, bias_ref, out_weight_ref, shifted,
            lambda row, resid: step(row, resid, rows_of(part_ref, row)),
        )

    @pl.when(opening)
    def _():
        for row in range(ROWS):
            own = rows_of(own_ref, row + 2).astype(F32)
            resid = (own - rows_of(bg_ref, row).astype(F32)).astype(BF16)
            step(row, resid, rows_of(part_ref, row))

    @pl.when(odd)
    def _():
        adjoint_part(
            8, 0, far, rows_in(active_ref, 0, 10), rows_in(forecast_ref, 0, 10), back_ref,
            out_back_ref, cot, target, lambda row, adjoint: step(row, rows_of(part_ref, row), adjoint),
        )

    out_ref[...] = wide[...].reshape(C, ROWS, LON).astype(BF16)


def exchange(value, partner):
    windows, strips = lax.axis_size("tm"), lax.axis_size("lat")
    pairs = []
    for window in range(windows):
        for strip in range(strips):
            to_window, to_strip = partner(window, strip, windows - 1, strips - 1)
            pairs.append((window * strips + strip, to_window * strips + to_strip))
    return lax.ppermute(value, ("tm", "lat"), pairs)


def near_strip(window, strip, last_window, last_strip):
    return window, strip ^ 1


def far_strip(window, strip, last_window, last_strip):
    if strip in (0, last_strip):
        return window ^ 1, strip
    return window, ((strip + 1) ^ 1) - 1


def near_window(window, strip, last_window, last_strip):
    return window ^ 1, strip


def far_window(window, strip, last_window, last_strip):
    if window in (0, last_window):
        return window, strip ^ 2
    return ((window + 1) ^ 1) - 1, strip


def shape(rows, dtype=BF16):
    return jax.ShapeDtypeStruct((rows, LON), dtype)


def shifted_scratch(count):
    return [pltpu.VMEM((3, (count + 2) * C, LON), BF16)]


def gradient_scratch(count):
    return shifted_scratch(count) + [
        pltpu.VMEM(((count + 2) * HID, LON), BF16),
        pltpu.VMEM(((count + 2) * C, LON), BF16),
    ]


def row_flops(rows):
    return rows * 2 * LON * HID * 10 * C


def on_device(
    window_snapshots, background, obs_values, obs_index, input_kernel_weight, hidden_bias_vector,
    output_pointwise_weight,
):
    out_weight = output_pointwise_weight

    def forward(pairs, state):
        count = state.shape[0] // C - 2
        return call(
            functools.partial(forward_kernel, pairs),
            (shape(2 * len(pairs) * HID), shape(2 * len(pairs) * C)),
            shifted_scratch(count),
            row_flops(2 * len(pairs)), 2 << 20,
        )(state, forward_weight, bias, out_weight)

    own, ground, first, second = call(
        pack_kernel,
        (shape(ROWS * C), shape(ROWS * C), shape(PAYLOAD), shape(PAYLOAD)),
        [
            pltpu.VMEM((C, ROWS, LON), BF16),
            pltpu.VMEM((C, ROWS, LON), BF16),
            pltpu.VMEM((C, OBS), BF16),
            pltpu.VMEM((1, OBS), jnp.int32),
            pltpu.VMEM((C * ROWS, LON), F32),
            pltpu.VMEM((C * ROWS, LON), F32),
            pltpu.SemaphoreType.DMA((4,)),
        ],
        0, 1 << 20, pl.BlockSpec(memory_space=pltpu.HBM),
    )(
        *(
            pltpu.with_memory_space_constraint(value, pltpu.HBM)
            for value in (window_snapshots[0], background, obs_values[0], obs_index)
        )
    )
    first = exchange(first, near_strip)
    second = exchange(second, far_strip)
    far_own = exchange(own, far_window)

    taps = jnp.transpose(input_kernel_weight, (0, 1, 3, 2)).reshape(9 * C, HID)
    sums, forward_weight, back_weight, bias, out_back = call(
        prepare_kernel,
        (
            jax.ShapeDtypeStruct((ROWS, 72, LON), F32),
            jax.ShapeDtypeStruct((HID, 9 * C), BF16),
            jax.ShapeDtypeStruct((3 * C, 3 * HID), BF16),
            jax.ShapeDtypeStruct((HID, LON), F32),
            jax.ShapeDtypeStruct((HID, C), BF16),
        ),
        [], ROWS * 2 * 80 * OBS * LON, 1 << 20,
    )(obs_values[0], obs_index, taps, hidden_bias_vector[None, :], out_weight)
    weights = (forward_weight, bias, out_weight, back_weight, out_back)
    inside = forward(in_order(6), own)
    first, second, inside, sums = lax.optimization_barrier((first, second, inside, sums))

    ext, sent, halo, above, below = call(
        extend_kernel,
        (shape(16 * C), shape(14 * C), shape(6 * C), shape(2 * C), shape(2 * C)),
        [], 0, 1 << 20,
    )(own, first, second)
    far = exchange(halo, far_window)
    near = exchange(sent, near_window)
    outside = forward(((0, 1), (2, 3), (10, 11), (12, 13)), ext)
    part, inner = call(
        first_near_kernel, (shape(12 * C), shape(12 * C)), gradient_scratch(12),
        row_flops(12), 2 << 20,
    )(near, far_own, ext, *inside, *outside, *weights)
    state, sent = call(
        first_kernel, (shape(12 * C), shape(10 * C)), gradient_scratch(12), row_flops(12),
        2 << 20,
    )(
        far, far_own, part, inner, ext, ground, *inside, *outside, *weights, sums, above, below
    )
    far = exchange(sent, far_window)
    near = exchange(sent, near_window)
    given = (state, ground, *forward(in_order(10), state), *weights)
    part = call(
        second_near_kernel, shape(8 * C), gradient_scratch(8), row_flops(8), 2 << 20
    )(near, state, *given[2:])
    analysis = call(
        second_kernel,
        jax.ShapeDtypeStruct((C, ROWS, LON), BF16),
        gradient_scratch(8) + [pltpu.VMEM((C * ROWS, LON), F32)],
        row_flops(8), 2 << 20,
    )(far, part, *given, sums)
    return analysis[None]


def solution(mesh):
    placed = (
        P("tm", None, "lat", None),
        P(None, "lat", None),
        P("tm", None, "lat"),
        P("tm", "lat"),
        P(),
        P(),
        P(),
    )
    return jax.shard_map(
        on_device, mesh=mesh, in_specs=placed, out_specs=P("tm", None, "lat", None), check_vma=False
    )
```

time: 32.3 us -> 31.8 us (0.985)
  the two profiles are of different devices: /device:TPU:4 before, /device:TPU:102 now
where the time goes in v5:
time: 31.8 us; the launch traced here: 31.6 us
  Pallas kernels  13.3 us (42%)
  waiting for transfers between devices  9.23 us (29%)
  starting transfers between devices  7.33 us (23%)
  local copies, waits for them, and re-layouts  1.64 us (5%)
    pallas_call x10, Pallas kernels, run(): pl.pallas_call(kernel, out_shape=outs, in_specs=[spec] * len(args), out_s...  13.3 us
    ppermute x7, waiting for transfers between devices, exchange(): return lax.ppermute(value, ('tm', 'lat'), pairs)  9.23 us
    ppermute x7, starting transfers between devices, exchange(): return lax.ppermute(value, ('tm', 'lat'), pairs)  7.33 us
    unnamed x10, local copies, waits for them, and re-layouts  1.64 us
  transfers between devices with their start and end apart: 7, of which 3 were waited for; matrix products, arithmetic and copies ran while one was open for 0% of the time, Pallas kernels for 26%

profile of v5, /device:TPU:102, one launch (start us, length us, event | category | flops | bytes accessed | tf_op | source)
XLA Modules:
  0.0 31.6 jit_solution(4413936221796543816)
XLA Ops:
  0.0 0.0 copy-start
  0.0 0.0 copy-start.2
  0.0 1.3 %shard_map.73 = (bf16[512,128]{1,0:T(8,128)(2,1)S(1)}, bf16[512,128]{1,0:T(8,128)(2,1)S(1)}, bf16[384,128]{1,0:T(8,128)(2,1)S(1)}, bf16[384,128]{1,0:T(8,128)(2,1)S(1)}) custom-call(bf16[64,8,128]{2,1,0:T(8,128)(2,1)} %bitcast.11, bf16[64,8,128]{2,1,0:T(8,128)(2,1)} %bg_hbm.1, bf16[64,256]{1,0:T(8,128)(2,1)} %bitcast.8, s32[1,256]{1,0:T(1,128)} %index_ref.1), custom_call_target="tpu_custom_call" | custom-call | bytes 1048576 | tf_op jit(solution)/shard_map/pallas_call | solution.py:28
  1.3 3.3 %collective-permute-start = (bf16[384,128]{1,0:T(8,128)(2,1)S(1)}, bf16[384,128]{1,0:T(8,128)(2,1)S(1)}, u32[]{:S(2)}, u32[]{:S(2)}) collective-permute-start(bf16[384,128]{1,0:T(8,128)(2,1)S(1)} %get-tuple-element.35), channel_id=1, source_target_pairs={{0,1},{1,0},{2,3},{3,2},{4,5},{5,4},{6,7},{7,6},{8,9},{9,8},{10,11... | collective-permute-start | bytes 294920 | tf_op jit(solution)/shard_map/ppermute | solution.py:450
  4.6 0.0 copy-start.4
  4.6 0.6 %collective-permute-start.1 = (bf16[384,128]{1,0:T(8,128)(2,1)S(1)}, bf16[384,128]{1,0:T(8,128)(2,1)S(1)}, u32[]{:S(2)}, u32[]{:S(2)}) collective-permute-start(bf16[384,128]{1,0:T(8,128)(2,1)S(1)} %get-tuple-element.36), channel_id=1, source_target_pairs={{0,8},{1,2},{2,1},{3,4},{4,3},{5,6},{6,5},{7,15},{8,0},{9,10},{10,... | collective-permute-start | bytes 294920 | tf_op jit(solution)/shard_map/ppermute | solution.py:450
  5.2 0.0 copy-start.3
  5.2 0.0 copy-done
  5.2 0.0 copy-done.2
  5.2 0.1 copy-done.4
  5.2 0.6 %copy-done.3 = s32[1,256]{1,0:T(1,128)S(1)} copy-done((s32[1,256]{1,0:T(1,128)S(1)}, s32[1,256]{1,0:T(1,128)}, u32[]{:S(2)}) %copy-start.3) | copy-done | bytes 1048
  5.8 0.0 copy-start.1
  5.9 1.0 %copy-done.1 = bf16[3,3,256,64]{2,3,1,0:T(8,128)(2,1)S(1)} copy-done((bf16[3,3,256,64]{2,3,1,0:T(8,128)(2,1)S(1)}, bf16[3,3,256,64]{2,3,1,0:T(8,128)(2,1)}, u32[]{:S(2)}) %copy-start.1) | copy-done | bytes 294936
  6.8 0.3 shard_map.74
  7.1 1.2 %shard_map.75 = (bf16[1536,128]{1,0:T(8,128)(2,1)S(1)}, bf16[384,128]{1,0:T(8,128)(2,1)S(1)}) custom-call(bf16[512,128]{1,0:T(8,128)(2,1)S(1)} %get-tuple-element.34.state_ref.own_ref, bf16[256,576]{1,0:T(8,128)(2,1)S(1)} %get-tuple-element.37.kernel_ref, f32[256,128]{1,0:T(8,128)S(1)} %get-tuple-element.38.bias_ref, bf16[64,256]{1,0:T(8,128)(2,1)S(1)} %copy-done), custom_call_target="tpu_custom_call" | custom-call | flops 251658240 | bytes 2097152 | tf_op jit(solution)/shard_map/pallas_call | solution.py:28
  8.4 0.0 collective-permute-done.first_ref
  8.4 3.2 %collective-permute-done.1.second_ref = bf16[384,128]{1,0:T(8,128)(2,1)S(1)} collective-permute-done((bf16[384,128]{1,0:T(8,128)(2,1)S(1)}, bf16[384,128]{1,0:T(8,128)(2,1)S(1)}, u32[]{:S(2)}, u32[]{:S(2)}) %collective-permute-start.1) | collective-permute-done | bytes 98336 | tf_op jit(solution)/shard_map/ppermute | solution.py:450
  11.6 0.1 shard_map.76
  11.7 0.1 collective-permute-start.4
  11.8 0.6 %collective-permute-start.3 = (bf16[512,128]{1,0:T(8,128)(2,1)S(1)}, bf16[512,128]{1,0:T(8,128)(2,1)S(1)}, u32[]{:S(2)}, u32[]{:S(2)}) collective-permute-start(bf16[512,128]{1,0:T(8,128)(2,1)S(1)} %get-tuple-element.34.state_ref.own_ref), channel_id=1, source_target_pairs={{0,2},{1,3},{2,0},{3,1},{4,6},{5,7},{6,4},{7,5},{8,16},{9,17},{10,... | collective-permute-start | bytes 393224 | tf_op jit(solution)/shard_map/ppermute | solution.py:450
  12.4 2.1 %collective-permute-start.2 = (bf16[384,128]{1,0:T(8,128)(2,1)S(1)}, bf16[384,128]{1,0:T(8,128)(2,1)S(1)}, u32[]{:S(2)}, u32[]{:S(2)}) collective-permute-start(bf16[384,128]{1,0:T(8,128)(2,1)S(1)} %get-tuple-element.44), channel_id=1, source_target_pairs={{0,2},{1,3},{2,0},{3,1},{4,6},{5,7},{6,4},{7,5},{8,16},{9,17},{10,... | collective-permute-start | bytes 294920 | tf_op jit(solution)/shard_map/ppermute | solution.py:450
  14.5 1.7 %shard_map.77 = (bf16[2048,128]{1,0:T(8,128)(2,1)S(1)}, bf16[512,128]{1,0:T(8,128)(2,1)S(1)}) custom-call(bf16[1024,128]{1,0:T(8,128)(2,1)S(1)} %get-tuple-element.46.state_ref.own_ref, bf16[256,576]{1,0:T(8,128)(2,1)S(1)} %get-tuple-element.37.kernel_ref, f32[256,128]{1,0:T(8,128)S(1)} %get-tuple-element.38.bias_ref, bf16[64,256]{1,0:T(8,128)(2,1)S(1)} %copy-done), custom_call_target="tpu_custom_call" | custom-call | flops 335544320 | bytes 2097152 | tf_op jit(solution)/shard_map/pallas_call | solution.py:28
  16.2 2.4 %collective-permute-done.3.far_own_ref = bf16[512,128]{1,0:T(8,128)(2,1)S(1)} collective-permute-done((bf16[512,128]{1,0:T(8,128)(2,1)S(1)}, bf16[512,128]{1,0:T(8,128)(2,1)S(1)}, u32[]{:S(2)}, u32[]{:S(2)}) %collective-permute-start.3) | collective-permute-done | bytes 131104 | tf_op jit(solution)/shard_map/ppermute | solution.py:450
  18.6 0.0 collective-permute-done.4.near_ref
  18.6 2.3 %shard_map.78 = (bf16[768,128]{1,0:T(8,128)(2,1)S(1)}, bf16[768,128]{1,0:T(8,128)(2,1)S(1)}) custom-call(bf16[896,128]{1,0:T(8,128)(2,1)S(1)} %collective-permute-done.4.near_ref, bf16[512,128]{1,0:T(8,128)(2,1)S(1)} %collective-permute-done.3.far_own_ref, bf16[1024,128]{1,0:T(8,128)(2,1)S(1)} %get-tuple-element.46.state_ref.own_ref, ...), custom_call_target="tpu_custom_call" | custom-call | flops 503316480 | bytes 2097152 | tf_op jit(solution)/shard_map/pallas_call | solution.py:28
  20.8 0.0 collective-permute-done.2.far_ref
  20.9 1.3 %shard_map.79 = (bf16[768,128]{1,0:T(8,128)(2,1)S(1)}, bf16[640,128]{1,0:T(8,128)(2,1)S(1)}) custom-call(bf16[384,128]{1,0:T(8,128)(2,1)S(1)} %collective-permute-done.2.far_ref, bf16[512,128]{1,0:T(8,128)(2,1)S(1)} %collective-permute-done.3.far_own_ref, bf16[768,128]{1,0:T(8,128)(2,1)S(1)} %get-tuple-element.53.part_ref, ...), custom_call_target="tpu_custom_call" | custom-call | flops 503316480 | bytes 2097152 | tf_op jit(solution)/shard_map/pallas_call | solution.py:28
  22.2 0.1 collective-permute-start.6
  22.2 0.6 %collective-permute-start.5 = (bf16[640,128]{1,0:T(8,128)(2,1)S(1)}, bf16[640,128]{1,0:T(8,128)(2,1)S(1)}, u32[]{:S(2)}, u32[]{:S(2)}) collective-permute-start(bf16[640,128]{1,0:T(8,128)(2,1)S(1)} %get-tuple-element.59), channel_id=1, source_target_pairs={{0,2},{1,3},{2,0},{3,1},{4,6},{5,7},{6,4},{7,5},{8,16},{9,17},{10,... | collective-permute-start | bytes 491528 | tf_op jit(solution)/shard_map/ppermute | solution.py:450
  22.8 2.0 %shard_map.80 = (bf16[2560,128]{1,0:T(8,128)(2,1)S(1)}, bf16[640,128]{1,0:T(8,128)(2,1)S(1)}) custom-call(bf16[768,128]{1,0:T(8,128)(2,1)S(1)} %get-tuple-element.60.state_ref.own_ref, bf16[256,576]{1,0:T(8,128)(2,1)S(1)} %get-tuple-element.37.kernel_ref, f32[256,128]{1,0:T(8,128)S(1)} %get-tuple-element.38.bias_ref, bf16[64,256]{1,0:T(8,128)(2,1)S(1)} %copy-done), custom_call_target="tpu_custom_call" | custom-call | flops 419430400 | bytes 2097152 | tf_op jit(solution)/shard_map/pallas_call | solution.py:28
  24.8 0.0 collective-permute-done.6.near_ref
  24.8 0.9 %shard_map.81.part_ref = bf16[512,128]{1,0:T(8,128)(2,1)S(1)} custom-call(bf16[640,128]{1,0:T(8,128)(2,1)S(1)} %collective-permute-done.6.near_ref, bf16[768,128]{1,0:T(8,128)(2,1)S(1)} %get-tuple-element.60.state_ref.own_ref, bf16[2560,128]{1,0:T(8,128)(2,1)S(1)} %get-tuple-element.61.active_ref, bf16[640,128]{1,0:T(8,128)(2,1)S(1)} %get-tuple-element.62.forecast_ref, ...), custom_call_target="tpu_custom_call" | custom-call | flops 335544320 | bytes 2097152 | tf_op jit(solution)/shard_map/pallas_call | solution.py:28
  25.6 3.6 %collective-permute-done.5.far_ref = bf16[640,128]{1,0:T(8,128)(2,1)S(1)} collective-permute-done((bf16[640,128]{1,0:T(8,128)(2,1)S(1)}, bf16[640,128]{1,0:T(8,128)(2,1)S(1)}, u32[]{:S(2)}, u32[]{:S(2)}) %collective-permute-start.5) | collective-permute-done | bytes 163872 | tf_op jit(solution)/shard_map/ppermute | solution.py:450
  29.3 2.4 %shard_map.82 = bf16[64,8,128]{2,1,0:T(8,128)(2,1)} custom-call(bf16[640,128]{1,0:T(8,128)(2,1)S(1)} %collective-permute-done.5.far_ref, bf16[512,128]{1,0:T(8,128)(2,1)S(1)} %shard_map.81.part_ref, bf16[768,128]{1,0:T(8,128)(2,1)S(1)} %get-tuple-element.60.state_ref.own_ref, bf16[512,128]{1,0:T(8,128)(2,1)S(1)} %get-tuple-element.55.bg_ref, ...), custom_call_target="tpu_custom_call" | custom-call | flops 335544320 | bytes 2097152 | tf_op jit(solution)/shard_map/pallas_call | solution.py:28
Async XLA Ops:
  0.0 5.2 %copy-start = (bf16[64,256]{1,0:T(8,128)(2,1)S(1)}, bf16[64,256]{1,0:T(8,128)(2,1)}, u32[]{:S(2)}) copy-start(bf16[64,256]{1,0:T(8,128)(2,1)} %out_weight_ref.15) | copy-start | bytes 98308
  0.0 5.2 %copy-start.2 = (bf16[1,64,256]{2,1,0:T(8,128)(2,1)S(1)}, bf16[1,64,256]{2,1,0:T(8,128)(2,1)}, u32[]{:S(2)}) copy-start(bf16[1,64,256]{2,1,0:T(8,128)(2,1)} %param.9) | copy-start | bytes 98308
  1.3 7.1 %collective-permute-start = (bf16[384,128]{1,0:T(8,128)(2,1)S(1)}, bf16[384,128]{1,0:T(8,128)(2,1)S(1)}, u32[]{:S(2)}, u32[]{:S(2)}) collective-permute-start(bf16[384,128]{1,0:T(8,128)(2,1)S(1)} %get-tuple-element.35), channel_id=1, source_target_pairs={{0,1},{1,0},{2,3},{3,2},{4,5},{5,4},{6,7},{7,6},{8,9},{9,8},{10,11... | collective-permute-start | bytes 294920 | tf_op jit(solution)/shard_map/ppermute | solution.py:450
  4.6 0.7 %copy-start.4 = (f32[256]{0:T(256)S(1)}, f32[256]{0:T(256)}, u32[]{:S(2)}) copy-start(f32[256]{0:T(256)} %param.12) | copy-start | bytes 3076
  4.6 7.0 %collective-permute-start.1 = (bf16[384,128]{1,0:T(8,128)(2,1)S(1)}, bf16[384,128]{1,0:T(8,128)(2,1)S(1)}, u32[]{:S(2)}, u32[]{:S(2)}) collective-permute-start(bf16[384,128]{1,0:T(8,128)(2,1)S(1)} %get-tuple-element.36), channel_id=1, source_target_pairs={{0,8},{1,2},{2,1},{3,4},{4,3},{5,6},{6,5},{7,15},{8,0},{9,10},{10,... | collective-permute-start | bytes 294920 | tf_op jit(solution)/shard_map/ppermute | solution.py:450
  5.2 0.7 %copy-start.3 = (s32[1,256]{1,0:T(1,128)S(1)}, s32[1,256]{1,0:T(1,128)}, u32[]{:S(2)}) copy-start(s32[1,256]{1,0:T(1,128)} %index_ref.1) | copy-start | bytes 3076
  5.8 1.0 %copy-start.1 = (bf16[3,3,256,64]{2,3,1,0:T(8,128)(2,1)S(1)}, bf16[3,3,256,64]{2,3,1,0:T(8,128)(2,1)}, u32[]{:S(2)}) copy-start(bf16[3,3,256,64]{2,3,1,0:T(8,128)(2,1)} %param.11) | copy-start | bytes 884740
  11.7 6.9 %collective-permute-start.4 = (bf16[896,128]{1,0:T(8,128)(2,1)S(1)}, bf16[896,128]{1,0:T(8,128)(2,1)S(1)}, u32[]{:S(2)}, u32[]{:S(2)}) collective-permute-start(bf16[896,128]{1,0:T(8,128)(2,1)S(1)} %get-tuple-element.45), channel_id=1, source_target_pairs={{0,8},{1,9},{2,10},{3,11},{4,12},{5,13},{6,14},{7,15},{8,0},{9,1},... | collective-permute-start | bytes 688136 | tf_op jit(solution)/shard_map/ppermute | solution.py:450
  11.8 6.8 %collective-permute-start.3 = (bf16[512,128]{1,0:T(8,128)(2,1)S(1)}, bf16[512,128]{1,0:T(8,128)(2,1)S(1)}, u32[]{:S(2)}, u32[]{:S(2)}) collective-permute-start(bf16[512,128]{1,0:T(8,128)(2,1)S(1)} %get-tuple-element.34.state_ref.own_ref), channel_id=1, source_target_pairs={{0,2},{1,3},{2,0},{3,1},{4,6},{5,7},{6,4},{7,5},{8,16},{9,17},{10,... | collective-permute-start | bytes 393224 | tf_op jit(solution)/shard_map/ppermute | solution.py:450
  12.4 8.4 %collective-permute-start.2 = (bf16[384,128]{1,0:T(8,128)(2,1)S(1)}, bf16[384,128]{1,0:T(8,128)(2,1)S(1)}, u32[]{:S(2)}, u32[]{:S(2)}) collective-permute-start(bf16[384,128]{1,0:T(8,128)(2,1)S(1)} %get-tuple-element.44), channel_id=1, source_target_pairs={{0,2},{1,3},{2,0},{3,1},{4,6},{5,7},{6,4},{7,5},{8,16},{9,17},{10,... | collective-permute-start | bytes 294920 | tf_op jit(solution)/shard_map/ppermute | solution.py:450
  22.2 2.6 %collective-permute-start.6 = (bf16[640,128]{1,0:T(8,128)(2,1)S(1)}, bf16[640,128]{1,0:T(8,128)(2,1)S(1)}, u32[]{:S(2)}, u32[]{:S(2)}) collective-permute-start(bf16[640,128]{1,0:T(8,128)(2,1)S(1)} %get-tuple-element.59), channel_id=1, source_target_pairs={{0,8},{1,9},{2,10},{3,11},{4,12},{5,13},{6,14},{7,15},{8,0},{9,1},... | collective-permute-start | bytes 491528 | tf_op jit(solution)/shard_map/ppermute | solution.py:450
  22.2 7.0 %collective-permute-start.5 = (bf16[640,128]{1,0:T(8,128)(2,1)S(1)}, bf16[640,128]{1,0:T(8,128)(2,1)S(1)}, u32[]{:S(2)}, u32[]{:S(2)}) collective-permute-start(bf16[640,128]{1,0:T(8,128)(2,1)S(1)} %get-tuple-element.59), channel_id=1, source_target_pairs={{0,2},{1,3},{2,0},{3,1},{4,6},{5,7},{6,4},{7,5},{8,16},{9,17},{10,... | collective-permute-start | bytes 491528 | tf_op jit(solution)/shard_map/ppermute | solution.py:450

commit v6 on v5

--- a/solution.py
+++ b/solution.py
@@ -84,13 +84,17 @@
 
 
 def pack_kernel(
-    x_hbm, bg_hbm, obs_hbm, index_hbm, own_ref, bg_rows_ref, first_ref, second_ref,
-    x_ref, bg_ref, obs_ref, index_ref, xs, bs, sems,
+    x_hbm, obs_hbm, index_hbm, bg_hbm, taps_hbm, out_weight_hbm, bias_hbm, own_ref, bg_rows_ref,
+    first_ref, second_ref, obs_ref, index_ref, taps_ref, out_weight_ref, bias_ref, x_ref, bg_ref,
+    xs, bs, sems,
 ):
     copies = [
         pltpu.make_async_copy(source, target, sems.at[place])
         for place, (source, target) in enumerate(
-            ((x_hbm, x_ref), (obs_hbm, obs_ref), (index_hbm, index_ref), (bg_hbm, bg_ref))
+            (
+                (x_hbm, x_ref), (obs_hbm, obs_ref), (index_hbm, index_ref), (bg_hbm, bg_ref),
+                (taps_hbm, taps_ref), (out_weight_hbm, out_weight_ref), (bias_hbm, bias_ref),
+            )
         )
     ]
     for copy in copies:
@@ -127,6 +131,8 @@
         send(4 + row, edge(row), edge(row + 6))
     for row in range(ROWS):
         bg_rows_ref[row * C : (row + 1) * C, :] = bs[latitude(row), :].astype(BF16)
+    for copy in copies[4:]:
+        copy.wait()
 
 
 def extend_kernel(
@@ -493,8 +499,6 @@
     window_snapshots, background, obs_values, obs_index, input_kernel_weight, hidden_bias_vector,
     output_pointwise_weight,
 ):
-    out_weight = output_pointwise_weight
-
     def forward(pairs, state):
         count = state.shape[0] // C - 2
         return call(
@@ -504,30 +508,38 @@
             row_flops(2 * len(pairs)), 2 << 20,
         )(state, forward_weight, bias, out_weight)
 
-    own, ground, first, second = call(
+    taps = jnp.transpose(input_kernel_weight, (0, 1, 3, 2)).reshape(9 * C, HID)
+    own, ground, first, second, observed, index, taps, out_weight, bias = call(
         pack_kernel,
-        (shape(ROWS * C), shape(ROWS * C), shape(PAYLOAD), shape(PAYLOAD)),
+        (
+            shape(ROWS * C), shape(ROWS * C), shape(PAYLOAD), shape(PAYLOAD),
+            jax.ShapeDtypeStruct((C, OBS), BF16),
+            jax.ShapeDtypeStruct((1, OBS), jnp.int32),
+            jax.ShapeDtypeStruct((9 * C, HID), BF16),
+            jax.ShapeDtypeStruct((C, HID), BF16),
+            jax.ShapeDtypeStruct((1, HID), F32),
+        ),
         [
             pltpu.VMEM((C, ROWS, LON), BF16),
             pltpu.VMEM((C, ROWS, LON), BF16),
-            pltpu.VMEM((C, OBS), BF16),
-            pltpu.VMEM((1, OBS), jnp.int32),
             pltpu.VMEM((C * ROWS, LON), F32),
             pltpu.VMEM((C * ROWS, LON), F32),
-            pltpu.SemaphoreType.DMA((4,)),
+            pltpu.SemaphoreType.DMA((7,)),
         ],
         0, 1 << 20, pl.BlockSpec(memory_space=pltpu.HBM),
     )(
         *(
             pltpu.with_memory_space_constraint(value, pltpu.HBM)
-            for value in (window_snapshots[0], background, obs_values[0], obs_index)
+            for value in (
+                window_snapshots[0], obs_values[0], obs_index, background, taps,
+                output_pointwise_weight, hidden_bias_vector[None, :],
+            )
         )
     )
+    second = exchange(second, far_strip)
     first = exchange(first, near_strip)
-    second = exchange(second, far_strip)
     far_own = exchange(own, far_window)
 
-    taps = jnp.transpose(input_kernel_weight, (0, 1, 3, 2)).reshape(9 * C, HID)
     sums, forward_weight, back_weight, bias, out_back = call(
         prepare_kernel,
         (
@@ -538,7 +550,7 @@
             jax.ShapeDtypeStruct((HID, C), BF16),
         ),
         [], ROWS * 2 * 80 * OBS * LON, 1 << 20,
-    )(obs_values[0], obs_index, taps, hidden_bias_vector[None, :], out_weight)
+    )(observed, index, taps, bias, out_weight)
     weights = (forward_weight, bias, out_weight, back_weight, out_back)
     inside = forward(in_order(6), own)
     first, second, inside, sums = lax.optimization_barrier((first, second, inside, sums))

time: 31.8 us -> 31.8 us (level)
  the two profiles are of different devices: /device:TPU:102 before, /device:TPU:98 now
where the time goes in v6:
time: 31.8 us; the launch traced here: 31.7 us
  Pallas kernels  13.4 us (42%)
  waiting for transfers between devices  11.2 us (35%)
  starting transfers between devices  7.04 us (22%)
    pallas_call x10, Pallas kernels, run(): pl.pallas_call(kernel, out_shape=outs, in_specs=[spec] * len(args), out_s...  13.4 us
    ppermute x7, waiting for transfers between devices, exchange(): return lax.ppermute(value, ('tm', 'lat'), pairs)  11.2 us
    ppermute x7, starting transfers between devices, exchange(): return lax.ppermute(value, ('tm', 'lat'), pairs)  7.04 us
  transfers between devices with their start and end apart: 7, of which 4 were waited for; matrix products, arithmetic and copies ran while one was open for 0% of the time, Pallas kernels for 26%

profile of v6, /device:TPU:98, one launch (start us, length us, event | category | flops | bytes accessed | tf_op | source)
XLA Modules:
  0.0 31.7 jit_solution(5591635127754941903)
XLA Ops:
  0.0 1.3 %shard_map.73 = (bf16[512,128]{1,0:T(8,128)(2,1)S(1)}, bf16[512,128]{1,0:T(8,128)(2,1)S(1)}, bf16[384,128]{1,0:T(8,128)(2,1)S(1)}, bf16[384,128]{1,0:T(8,128)(2,...) custom-call(bf16[64,8,128]{2,1,0:T(8,128)(2,1)} %bitcast.8, ...), custom_call_target="tpu_custom_call" | custom-call | bytes 1048576 | tf_op jit(solution)/shard_map/pallas_call | solution.py:28
  1.3 3.3 %collective-permute-start = (bf16[384,128]{1,0:T(8,128)(2,1)S(1)}, bf16[384,128]{1,0:T(8,128)(2,1)S(1)}, u32[]{:S(2)}, u32[]{:S(2)}) collective-permute-start(bf16[384,128]{1,0:T(8,128)(2,1)S(1)} %get-tuple-element.40), channel_id=1, source_target_pairs={{0,1},{1,0},{2,3},{3,2},{4,5},{5,4},{6,7},{7,6},{8,9},{9,8},{10,11... | collective-permute-start | bytes 294920 | tf_op jit(solution)/shard_map/ppermute | solution.py:456
  4.6 0.3 collective-permute-start.1
  4.9 0.3 shard_map.74
  5.2 1.2 %shard_map.75 = (bf16[1536,128]{1,0:T(8,128)(2,1)S(1)}, bf16[384,128]{1,0:T(8,128)(2,1)S(1)}) custom-call(bf16[512,128]{1,0:T(8,128)(2,1)S(1)} %get-tuple-element.39.state_ref.own_ref, bf16[256,576]{1,0:T(8,128)(2,1)S(1)} %get-tuple-element.47.kernel_ref, f32[256,128]{1,0:T(8,128)S(1)} %get-tuple-element.48.bias_ref, ...), custom_call_target="tpu_custom_call" | custom-call | flops 251658240 | bytes 2097152 | tf_op jit(solution)/shard_map/pallas_call | solution.py:28
  6.4 2.3 %collective-permute-done.first_ref = bf16[384,128]{1,0:T(8,128)(2,1)S(1)} collective-permute-done((bf16[384,128]{1,0:T(8,128)(2,1)S(1)}, bf16[384,128]{1,0:T(8,128)(2,1)S(1)}, u32[]{:S(2)}, u32[]{:S(2)}) %collective-permute-start) | collective-permute-done | bytes 98336 | tf_op jit(solution)/shard_map/ppermute | solution.py:456
  8.7 2.9 %collective-permute-done.1.second_ref = bf16[384,128]{1,0:T(8,128)(2,1)S(1)} collective-permute-done((bf16[384,128]{1,0:T(8,128)(2,1)S(1)}, bf16[384,128]{1,0:T(8,128)(2,1)S(1)}, u32[]{:S(2)}, u32[]{:S(2)}) %collective-permute-start.1) | collective-permute-done | bytes 98336 | tf_op jit(solution)/shard_map/ppermute | solution.py:456
  11.6 0.1 shard_map.76
  11.7 0.1 collective-permute-start.4
  11.8 0.6 %collective-permute-start.3 = (bf16[512,128]{1,0:T(8,128)(2,1)S(1)}, bf16[512,128]{1,0:T(8,128)(2,1)S(1)}, u32[]{:S(2)}, u32[]{:S(2)}) collective-permute-start(bf16[512,128]{1,0:T(8,128)(2,1)S(1)} %get-tuple-element.39.state_ref.own_ref), channel_id=1, source_target_pairs={{0,2},{1,3},{2,0},{3,1},{4,6},{5,7},{6,4},{7,5},{8,16},{9,17},{10,... | collective-permute-start | bytes 393224 | tf_op jit(solution)/shard_map/ppermute | solution.py:456
  12.4 2.1 %collective-permute-start.2 = (bf16[384,128]{1,0:T(8,128)(2,1)S(1)}, bf16[384,128]{1,0:T(8,128)(2,1)S(1)}, u32[]{:S(2)}, u32[]{:S(2)}) collective-permute-start(bf16[384,128]{1,0:T(8,128)(2,1)S(1)} %get-tuple-element.54), channel_id=1, source_target_pairs={{0,2},{1,3},{2,0},{3,1},{4,6},{5,7},{6,4},{7,5},{8,16},{9,17},{10,... | collective-permute-start | bytes 294920 | tf_op jit(solution)/shard_map/ppermute | solution.py:456
  14.5 1.7 %shard_map.77 = (bf16[2048,128]{1,0:T(8,128)(2,1)S(1)}, bf16[512,128]{1,0:T(8,128)(2,1)S(1)}) custom-call(bf16[1024,128]{1,0:T(8,128)(2,1)S(1)} %get-tuple-element.56.state_ref.own_ref, bf16[256,576]{1,0:T(8,128)(2,1)S(1)} %get-tuple-element.47.kernel_ref, f32[256,128]{1,0:T(8,128)S(1)} %get-tuple-element.48.bias_ref, ...), custom_call_target="tpu_custom_call" | custom-call | flops 335544320 | bytes 2097152 | tf_op jit(solution)/shard_map/pallas_call | solution.py:28
  16.2 2.4 %collective-permute-done.3.far_own_ref = bf16[512,128]{1,0:T(8,128)(2,1)S(1)} collective-permute-done((bf16[512,128]{1,0:T(8,128)(2,1)S(1)}, bf16[512,128]{1,0:T(8,128)(2,1)S(1)}, u32[]{:S(2)}, u32[]{:S(2)}) %collective-permute-start.3) | collective-permute-done | bytes 131104 | tf_op jit(solution)/shard_map/ppermute | solution.py:456
  18.6 0.0 collective-permute-done.4.near_ref
  18.6 2.3 %shard_map.78 = (bf16[768,128]{1,0:T(8,128)(2,1)S(1)}, bf16[768,128]{1,0:T(8,128)(2,1)S(1)}) custom-call(bf16[896,128]{1,0:T(8,128)(2,1)S(1)} %collective-permute-done.4.near_ref, bf16[512,128]{1,0:T(8,128)(2,1)S(1)} %collective-permute-done.3.far_own_ref, bf16[1024,128]{1,0:T(8,128)(2,1)S(1)} %get-tuple-element.56.state_ref.own_ref, ...), custom_call_target="tpu_custom_call" | custom-call | flops 503316480 | bytes 2097152 | tf_op jit(solution)/shard_map/pallas_call | solution.py:28
  20.9 0.0 collective-permute-done.2.far_ref
  20.9 1.3 %shard_map.79 = (bf16[768,128]{1,0:T(8,128)(2,1)S(1)}, bf16[640,128]{1,0:T(8,128)(2,1)S(1)}) custom-call(bf16[384,128]{1,0:T(8,128)(2,1)S(1)} %collective-permute-done.2.far_ref, bf16[512,128]{1,0:T(8,128)(2,1)S(1)} %collective-permute-done.3.far_own_ref, bf16[768,128]{1,0:T(8,128)(2,1)S(1)} %get-tuple-element.63.part_ref, ...), custom_call_target="tpu_custom_call" | custom-call | flops 503316480 | bytes 2097152 | tf_op jit(solution)/shard_map/pallas_call | solution.py:28
  22.2 0.1 collective-permute-start.6
  22.3 0.6 %collective-permute-start.5 = (bf16[640,128]{1,0:T(8,128)(2,1)S(1)}, bf16[640,128]{1,0:T(8,128)(2,1)S(1)}, u32[]{:S(2)}, u32[]{:S(2)}) collective-permute-start(bf16[640,128]{1,0:T(8,128)(2,1)S(1)} %get-tuple-element.69), channel_id=1, source_target_pairs={{0,2},{1,3},{2,0},{3,1},{4,6},{5,7},{6,4},{7,5},{8,16},{9,17},{10,... | collective-permute-start | bytes 491528 | tf_op jit(solution)/shard_map/ppermute | solution.py:456
  22.8 2.0 %shard_map.80 = (bf16[2560,128]{1,0:T(8,128)(2,1)S(1)}, bf16[640,128]{1,0:T(8,128)(2,1)S(1)}) custom-call(bf16[768,128]{1,0:T(8,128)(2,1)S(1)} %get-tuple-element.70.state_ref.own_ref, bf16[256,576]{1,0:T(8,128)(2,1)S(1)} %get-tuple-element.47.kernel_ref, f32[256,128]{1,0:T(8,128)S(1)} %get-tuple-element.48.bias_ref, ...), custom_call_target="tpu_custom_call" | custom-call | flops 419430400 | bytes 2097152 | tf_op jit(solution)/shard_map/pallas_call | solution.py:28
  24.8 0.0 collective-permute-done.6.near_ref
  24.8 0.9 %shard_map.81.part_ref = bf16[512,128]{1,0:T(8,128)(2,1)S(1)} custom-call(bf16[640,128]{1,0:T(8,128)(2,1)S(1)} %collective-permute-done.6.near_ref, bf16[768,128]{1,0:T(8,128)(2,1)S(1)} %get-tuple-element.70.state_ref.own_ref, bf16[2560,128]{1,0:T(8,128)(2,1)S(1)} %get-tuple-element.71.active_ref, bf16[640,128]{1,0:T(8,128)(2,1)S(1)} %get-tuple-element.72.forecast_ref, ...), custom_call_target="tpu_custom_call" | custom-call | flops 335544320 | bytes 2097152 | tf_op jit(solution)/shard_map/pallas_call | solution.py:28
  25.7 3.6 %collective-permute-done.5.far_ref = bf16[640,128]{1,0:T(8,128)(2,1)S(1)} collective-permute-done((bf16[640,128]{1,0:T(8,128)(2,1)S(1)}, bf16[640,128]{1,0:T(8,128)(2,1)S(1)}, u32[]{:S(2)}, u32[]{:S(2)}) %collective-permute-start.5) | collective-permute-done | bytes 163872 | tf_op jit(solution)/shard_map/ppermute | solution.py:456
  29.3 2.4 %shard_map.82 = bf16[64,8,128]{2,1,0:T(8,128)(2,1)} custom-call(bf16[640,128]{1,0:T(8,128)(2,1)S(1)} %collective-permute-done.5.far_ref, bf16[512,128]{1,0:T(8,128)(2,1)S(1)} %shard_map.81.part_ref, bf16[768,128]{1,0:T(8,128)(2,1)S(1)} %get-tuple-element.70.state_ref.own_ref, bf16[512,128]{1,0:T(8,128)(2,1)S(1)} %get-tuple-element.65.bg_ref, ...), custom_call_target="tpu_custom_call" | custom-call | flops 335544320 | bytes 2097152 | tf_op jit(solution)/shard_map/pallas_call | solution.py:28
Async XLA Ops:
  1.3 7.4 %collective-permute-start = (bf16[384,128]{1,0:T(8,128)(2,1)S(1)}, bf16[384,128]{1,0:T(8,128)(2,1)S(1)}, u32[]{:S(2)}, u32[]{:S(2)}) collective-permute-start(bf16[384,128]{1,0:T(8,128)(2,1)S(1)} %get-tuple-element.40), channel_id=1, source_target_pairs={{0,1},{1,0},{2,3},{3,2},{4,5},{5,4},{6,7},{7,6},{8,9},{9,8},{10,11... | collective-permute-start | bytes 294920 | tf_op jit(solution)/shard_map/ppermute | solution.py:456
  4.6 7.0 %collective-permute-start.1 = (bf16[384,128]{1,0:T(8,128)(2,1)S(1)}, bf16[384,128]{1,0:T(8,128)(2,1)S(1)}, u32[]{:S(2)}, u32[]{:S(2)}) collective-permute-start(bf16[384,128]{1,0:T(8,128)(2,1)S(1)} %get-tuple-element.41), channel_id=1, source_target_pairs={{0,8},{1,2},{2,1},{3,4},{4,3},{5,6},{6,5},{7,15},{8,0},{9,10},{10,... | collective-permute-start | bytes 294920 | tf_op jit(solution)/shard_map/ppermute | solution.py:456
  11.7 6.9 %collective-permute-start.4 = (bf16[896,128]{1,0:T(8,128)(2,1)S(1)}, bf16[896,128]{1,0:T(8,128)(2,1)S(1)}, u32[]{:S(2)}, u32[]{:S(2)}) collective-permute-start(bf16[896,128]{1,0:T(8,128)(2,1)S(1)} %get-tuple-element.55), channel_id=1, source_target_pairs={{0,8},{1,9},{2,10},{3,11},{4,12},{5,13},{6,14},{7,15},{8,0},{9,1},... | collective-permute-start | bytes 688136 | tf_op jit(solution)/shard_map/ppermute | solution.py:456
  11.8 6.8 %collective-permute-start.3 = (bf16[512,128]{1,0:T(8,128)(2,1)S(1)}, bf16[512,128]{1,0:T(8,128)(2,1)S(1)}, u32[]{:S(2)}, u32[]{:S(2)}) collective-permute-start(bf16[512,128]{1,0:T(8,128)(2,1)S(1)} %get-tuple-element.39.state_ref.own_ref), channel_id=1, source_target_pairs={{0,2},{1,3},{2,0},{3,1},{4,6},{5,7},{6,4},{7,5},{8,16},{9,17},{10,... | collective-permute-start | bytes 393224 | tf_op jit(solution)/shard_map/ppermute | solution.py:456
  12.4 8.4 %collective-permute-start.2 = (bf16[384,128]{1,0:T(8,128)(2,1)S(1)}, bf16[384,128]{1,0:T(8,128)(2,1)S(1)}, u32[]{:S(2)}, u32[]{:S(2)}) collective-permute-start(bf16[384,128]{1,0:T(8,128)(2,1)S(1)} %get-tuple-element.54), channel_id=1, source_target_pairs={{0,2},{1,3},{2,0},{3,1},{4,6},{5,7},{6,4},{7,5},{8,16},{9,17},{10,... | collective-permute-start | bytes 294920 | tf_op jit(solution)/shard_map/ppermute | solution.py:456
  22.2 2.6 %collective-permute-start.6 = (bf16[640,128]{1,0:T(8,128)(2,1)S(1)}, bf16[640,128]{1,0:T(8,128)(2,1)S(1)}, u32[]{:S(2)}, u32[]{:S(2)}) collective-permute-start(bf16[640,128]{1,0:T(8,128)(2,1)S(1)} %get-tuple-element.69), channel_id=1, source_target_pairs={{0,8},{1,9},{2,10},{3,11},{4,12},{5,13},{6,14},{7,15},{8,0},{9,1},... | collective-permute-start | bytes 491528 | tf_op jit(solution)/shard_map/ppermute | solution.py:456
  22.3 7.0 %collective-permute-start.5 = (bf16[640,128]{1,0:T(8,128)(2,1)S(1)}, bf16[640,128]{1,0:T(8,128)(2,1)S(1)}, u32[]{:S(2)}, u32[]{:S(2)}) collective-permute-start(bf16[640,128]{1,0:T(8,128)(2,1)S(1)} %get-tuple-element.69), channel_id=1, source_target_pairs={{0,2},{1,3},{2,0},{3,1},{4,6},{5,7},{6,4},{7,5},{8,16},{9,17},{10,... | collective-permute-start | bytes 491528 | tf_op jit(solution)/shard_map/ppermute | solution.py:456

commit v7 on v6

--- a/solution.py
+++ b/solution.py
@@ -157,17 +157,37 @@
     ext_ref[X_PART + ROWS * C :, :] = below
 
 
-def roll_rows(rows, shifted, pairs):
+def turn(value, b):
+    return value if b == 1 else pltpu.roll(value, 1 if b == 0 else LON - 1, 1)
+
+
+def actives(work, rows, kernel_ref, quad_ref, bias_ref, shifted, mixed):
+    quads, pairs = work
+    bias = jnp.concatenate([bias_ref[...], bias_ref[...]], axis=1)
+    for place, pair in enumerate(pair for quad in quads for pair in quad):
+        d = [at(rows, pair[0] + a).astype(F32) for a in range(4)]
+        for j, value in enumerate((d[0] - d[2], d[1] + d[2], d[2] - d[1], d[1] - d[3])):
+            for b in range(3):
+                start = (3 * place + b) * C
+                mixed[j, start : start + C, :] = turn(value, b).astype(BF16)
     for place in sorted({first + a for pair in pairs for first in pair for a in range(3)}):
-        into = slice(place * C, (place + 1) * C)
         value = at(rows, place)
-        wide = value.astype(F32)
-        shifted[0, into, :] = pltpu.roll(wide, 1, 1).astype(BF16)
-        shifted[1, into, :] = value
-        shifted[2, into, :] = pltpu.roll(wide, LON - 1, 1).astype(BF16)
-
-
-def hidden(shifted, kernel_ref, bias, pair):
+        for b in range(3):
+            moved = value if b == 1 else turn(value.astype(F32), b).astype(BF16)
+            shifted[b, place * C : (place + 1) * C, :] = moved
+    for place, (first, second) in enumerate(quads):
+        start, middle, end = (3 * C * (2 * place + n) for n in range(3))
+        m = [
+            jnp.dot(
+                quad_ref[j * HID : (j + 1) * HID, :],
+                jnp.concatenate([mixed[j, start:middle, :], mixed[j, middle:end, :]], axis=1),
+                preferred_element_type=F32,
+            )
+            for j in range(4)
+        ]
+        yield (first[0], second[0]), jnp.tanh(m[0] + m[1] + m[2] + bias).astype(BF16)
+        yield (first[1], second[1]), jnp.tanh(m[1] - m[2] - m[3] + bias).astype(BF16)
+
     def stack(first):
         return jnp.concatenate(
             [
@@ -178,9 +198,15 @@
             axis=0,
         )
 
-    cells = jnp.concatenate([stack(row) for row in pair], axis=1)
-    before = jnp.dot(kernel_ref[...], cells, preferred_element_type=F32) + bias
-    return jnp.tanh(before).astype(BF16)
+    for pair in pairs:
+        cells = jnp.concatenate([stack(row) for row in pair], axis=1)
+        before = jnp.dot(kernel_ref[...], cells, preferred_element_type=F32) + bias
+        yield pair, jnp.tanh(before).astype(BF16)
+
+
+def rows_of_work(work):
+    quads, pairs = work
+    return sorted([row for quad in quads for pair in quad for row in pair] + [r for p in pairs for r in p])
 
 
 def store_pair(ref, first, value, width=C):
@@ -188,33 +214,36 @@
     ref[(first + 1) * width : (first + 2) * width, :] = value[:, LON:]
 
 
-def wide_bias(bias_ref):
-    return jnp.concatenate([bias_ref[...], bias_ref[...]], axis=1)
-
-
 def forward_kernel(
-    pairs, state_ref, kernel_ref, bias_ref, out_weight_ref, active_ref, forecast_ref, shifted
+    work, state_ref, kernel_ref, quad_ref, bias_ref, out_weight_ref, active_ref, forecast_ref,
+    shifted, mixed,
 ):
     rows = rows_in(state_ref, 0, state_ref.shape[0] // C)
-    roll_rows(rows, shifted, pairs)
-    bias = wide_bias(bias_ref)
-    for place, (a, b) in enumerate(pairs):
-        active = hidden(shifted, kernel_ref, bias, (a, b))
-        store_pair(active_ref, 2 * place, active, HID)
+    places = {row: place for place, row in enumerate(rows_of_work(work))}
+    for pair, active in actives(work, rows, kernel_ref, quad_ref, bias_ref, shifted, mixed):
         step = jnp.dot(out_weight_ref[...], active, preferred_element_type=F32)
-        centre = beside(rows, a + 1, b + 1).astype(F32)
-        store_pair(forecast_ref, 2 * place, (centre + step).astype(BF16))
+        centre = beside(rows, pair[0] + 1, pair[1] + 1).astype(F32)
+        forecast = (centre + step).astype(BF16)
+        for half, row in enumerate(pair):
+            lanes = slice(half * LON, (half + 1) * LON)
+            place = places[row]
+            active_ref[place * HID : (place + 1) * HID, :] = active[:, lanes]
+            forecast_ref[place * C : (place + 1) * C, :] = forecast[:, lanes]
 
 
 def prepare_kernel(
-    obs_ref, index_ref, kernel_ref, bias_ref, out_weight_ref, sums_ref, forward_ref, back_ref,
-    wide_bias_ref, out_back_ref,
+    obs_ref, index_ref, kernel_ref, bias_ref, out_weight_ref, sums_ref, forward_ref, quad_ref,
+    back_ref, wide_bias_ref, out_back_ref,
 ):
     low, high = local_cells(index_ref[...])
     values = with_ones(obs_ref[...])
     for row in range(ROWS):
         sums_ref[row] = observation_sums(values, low, high, row)[:72, :]
     forward_ref[...] = kernel_ref[...].T
+    g = [kernel_ref[a * 3 * C : (a + 1) * 3 * C, :].astype(F32) for a in range(3)]
+    ends = g[0] + g[2]
+    for j, value in enumerate((g[0], 0.5 * (ends + g[1]), 0.5 * (ends - g[1]), g[2])):
+        quad_ref[j * HID : (j + 1) * HID, :] = value.astype(BF16).T
     out_back_ref[...] = out_weight_ref[...].T
     wide_bias_ref[...] = jnp.broadcast_to(bias_ref[...], (LON, HID)).T
     for a in range(3):
@@ -222,13 +251,10 @@
 
 
 def residual_part(
-    pairs, prev, own_ref, kernel_ref, bias_ref, out_weight_ref, shifted, take
-):
-    roll_rows(prev, shifted, pairs)
-    bias = wide_bias(bias_ref)
-    own_rows = rows_in(own_ref, 2, max(b for _, b in pairs) + 1)
-    for a, b in pairs:
-        active = hidden(shifted, kernel_ref, bias, (a, b))
+    work, prev, own_ref, kernel_ref, quad_ref, bias_ref, out_weight_ref, shifted, mixed, take
+):
+    own_rows = rows_in(own_ref, 2, max(rows_of_work(work)) + 1)
+    for (a, b), active in actives(work, prev, kernel_ref, quad_ref, bias_ref, shifted, mixed):
         step = jnp.dot(out_weight_ref[...], active, preferred_element_type=F32)
         centre = beside(prev, a + 1, b + 1).astype(F32)
         guess = (centre + step).astype(BF16).astype(F32)
@@ -282,18 +308,23 @@
     return even & jnp.logical_not(opening), opening, jnp.logical_not(even)
 
 
-def in_order(count):
-    return tuple((row, row + 1) for row in range(0, count, 2))
-
-
-INNER = ((3, 4), (5, 6), (7, 8))
-OUTER = ((0, 1), (2, 9), (10, 11))
+def quads_of(count):
+    return tuple(((row, row + 1), (row + 2, row + 3)) for row in range(0, count - 3, 4))
+
+
+INSIDE = (quads_of(4), ((4, 5),))
+OUTSIDE = ((((0, 1), (2, 3)), ((10, 11), (12, 13))), ())
+INNER = ((((3, 4), (5, 6)),), ((7, 8),))
+OUTER = ((((0, 1), (10, 11)),), ((2, 9),))
+TWELVE = (quads_of(12), ())
+TEN = (quads_of(8), ((8, 9),))
+EIGHT = (quads_of(8), ())
 
 
 def first_near_kernel(
     near_ref, far_own_ref, own_ref, active_in_ref, forecast_in_ref, active_out_ref, forecast_out_ref,
-    kernel_ref, bias_ref, out_weight_ref, back_ref, out_back_ref, part_ref, inner_ref, shifted, cot,
-    target,
+    kernel_ref, quad_ref, bias_ref, out_weight_ref, back_ref, out_back_ref, part_ref, inner_ref, shifted, mixed,
+    cot, target,
 ):
     def put(ref):
         def take(row, value):
@@ -315,14 +346,15 @@
     def _():
         prev = [None] * 3 + rows_in(far_own_ref, 0, ROWS)
         residual_part(
-            INNER, prev, own_ref, kernel_ref, bias_ref, out_weight_ref, shifted, put(inner_ref)
+            INNER, prev, own_ref, kernel_ref, quad_ref, bias_ref, out_weight_ref,
+            shifted, mixed, put(inner_ref)
         )
 
     @pl.when(odd)
     def _():
         residual_part(
-            in_order(12), rows_in(near_ref, 0, 14), own_ref, kernel_ref, bias_ref, out_weight_ref,
-            shifted, put(part_ref),
+            TWELVE, rows_in(near_ref, 0, 14), own_ref, kernel_ref, quad_ref, bias_ref, out_weight_ref,
+            shifted, mixed, put(part_ref),
         )
 
 
@@ -332,8 +364,8 @@
 
 def first_kernel(
     far_ref, far_own_ref, part_ref, inner_ref, own_ref, bg_ref, active_in_ref, forecast_in_ref,
-    active_out_ref, forecast_out_ref, kernel_ref, bias_ref, out_weight_ref, back_ref, out_back_ref,
-    sums_ref, above_ref, below_ref, state_ref, sent_ref, shifted, cot, target,
+    active_out_ref, forecast_out_ref, kernel_ref, quad_ref, bias_ref, out_weight_ref, back_ref, out_back_ref,
+    sums_ref, above_ref, below_ref, state_ref, sent_ref, shifted, mixed, cot, target,
 ):
     top, bottom = strip_ends()
 
@@ -360,8 +392,8 @@
     @pl.when(even)
     def _():
         residual_part(
-            OUTER, far, own_ref, kernel_ref, bias_ref, out_weight_ref, shifted,
-            lambda row, resid: step(row, resid, rows_of(part_ref, row)),
+            OUTER, far, own_ref, kernel_ref, quad_ref, bias_ref, out_weight_ref, shifted,
+            mixed, lambda row, resid: step(row, resid, rows_of(part_ref, row)),
         )
         for row in range(3, 9):
             step(row, rows_of(inner_ref, row), rows_of(part_ref, row))
@@ -386,8 +418,8 @@
 
 
 def second_near_kernel(
-    near_ref, own_ref, active_ref, forecast_ref, kernel_ref, bias_ref, out_weight_ref, back_ref,
-    out_back_ref, part_ref, shifted, cot, target,
+    near_ref, own_ref, active_ref, forecast_ref, kernel_ref, quad_ref, bias_ref, out_weight_ref,
+    back_ref, out_back_ref, part_ref, shifted, mixed, cot, target,
 ):
     def take(row, value):
         part_ref[row * C : (row + 1) * C, :] = value
@@ -405,13 +437,14 @@
     @pl.when(odd)
     def _():
         residual_part(
-            in_order(8), near, own_ref, kernel_ref, bias_ref, out_weight_ref, shifted, take
+            EIGHT, near, own_ref, kernel_ref, quad_ref, bias_ref, out_weight_ref,
+            shifted, mixed, take
         )
 
 
 def second_kernel(
-    far_ref, part_ref, own_ref, bg_ref, active_ref, forecast_ref, kernel_ref, bias_ref,
-    out_weight_ref, back_ref, out_back_ref, sums_ref, out_ref, shifted, cot, target, wide,
+    far_ref, part_ref, own_ref, bg_ref, active_ref, forecast_ref, kernel_ref, quad_ref, bias_ref,
+    out_weight_ref, back_ref, out_back_ref, sums_ref, out_ref, shifted, mixed, cot, target, wide,
 ):
     def step(row, resid, adjoint):
         own = rows_of(own_ref, row + 2).astype(F32)
@@ -425,8 +458,8 @@
     @pl.when(even)
     def _():
         residual_part(
-            in_order(8), far, own_ref, kernel_ref, bias_ref, out_weight_ref, shifted,
-            lambda row, resid: step(row, resid, rows_of(part_ref, row)),
+            EIGHT, far, own_ref, kernel_ref, quad_ref, bias_ref, out_weight_ref, shifted,
+            mixed, lambda row, resid: step(row, resid, rows_of(part_ref, row)),
         )
 
     @pl.when(opening)
@@ -480,12 +513,15 @@
     return jax.ShapeDtypeStruct((rows, LON), dtype)
 
 
-def shifted_scratch(count):
-    return [pltpu.VMEM((3, (count + 2) * C, LON), BF16)]
+def conv_scratch(count):
+    return [
+        pltpu.VMEM((3, (count + 2) * C, LON), BF16),
+        pltpu.VMEM((4, (count // 2) * 3 * C, LON), BF16),
+    ]
 
 
 def gradient_scratch(count):
-    return shifted_scratch(count) + [
+    return conv_scratch(count) + [
         pltpu.VMEM(((count + 2) * HID, LON), BF16),
         pltpu.VMEM(((count + 2) * C, LON), BF16),
     ]
@@ -499,14 +535,14 @@
     window_snapshots, background, obs_values, obs_index, input_kernel_weight, hidden_bias_vector,
     output_pointwise_weight,
 ):
-    def forward(pairs, state):
-        count = state.shape[0] // C - 2
+    def forward(work, state):
+        count = len(rows_of_work(work))
         return call(
-            functools.partial(forward_kernel, pairs),
-            (shape(2 * len(pairs) * HID), shape(2 * len(pairs) * C)),
-            shifted_scratch(count),
-            row_flops(2 * len(pairs)), 2 << 20,
-        )(state, forward_weight, bias, out_weight)
+            functools.partial(forward_kernel, work),
+            (shape(count * HID), shape(count * C)),
+            conv_scratch(state.shape[0] // C - 2),
+            row_flops(count), 2 << 20,
+        )(state, forward_weight, quad_weight, bias, out_weight)
 
     taps = jnp.transpose(input_kernel_weight, (0, 1, 3, 2)).reshape(9 * C, HID)
     own, ground, first, second, observed, index, taps, out_weight, bias = call(
@@ -540,19 +576,20 @@
     first = exchange(first, near_strip)
     far_own = exchange(own, far_window)
 
-    sums, forward_weight, back_weight, bias, out_back = call(
+    sums, forward_weight, quad_weight, back_weight, bias, out_back = call(
         prepare_kernel,
         (
             jax.ShapeDtypeStruct((ROWS, 72, LON), F32),
             jax.ShapeDtypeStruct((HID, 9 * C), BF16),
+            jax.ShapeDtypeStruct((4 * HID, 3 * C), BF16),
             jax.ShapeDtypeStruct((3 * C, 3 * HID), BF16),
             jax.ShapeDtypeStruct((HID, LON), F32),
             jax.ShapeDtypeStruct((HID, C), BF16),
         ),
         [], ROWS * 2 * 80 * OBS * LON, 1 << 20,
     )(observed, index, taps, bias, out_weight)
-    weights = (forward_weight, bias, out_weight, back_weight, out_back)
-    inside = forward(in_order(6), own)
+    weights = (forward_weight, quad_weight, bias, out_weight, back_weight, out_back)
+    inside = forward(INSIDE, own)
     first, second, inside, sums = lax.optimization_barrier((first, second, inside, sums))
 
     ext, sent, halo, above, below = call(
@@ -562,7 +599,7 @@
     )(own, first, second)
     far = exchange(halo, far_window)
     near = exchange(sent, near_window)
-    outside = forward(((0, 1), (2, 3), (10, 11), (12, 13)), ext)
+    outside = forward(OUTSIDE, ext)
     part, inner = call(
         first_near_kernel, (shape(12 * C), shape(12 * C)), gradient_scratch(12),
         row_flops(12), 2 << 20,
@@ -575,7 +612,7 @@
     )
     far = exchange(sent, far_window)
     near = exchange(sent, near_window)
-    given = (state, ground, *forward(in_order(10), state), *weights)
+    given = (state, ground, *forward(TEN, state), *weights)
     part = call(
         second_near_kernel, shape(8 * C), gradient_scratch(8), row_flops(8), 2 << 20
     )(near, state, *given[2:])

time: 31.8 us -> 30.4 us (0.956)
  Pallas kernels: 13.4 us -> 10.3 us
  waiting for transfers between devices: 11.2 us -> 13.1 us
    pallas_call x10, Pallas kernels: 13.4 us -> 10.3 us  [run(): pl.pallas_call(kernel, out_shape=outs, in_specs=[spec] * len(args), out_s...]
    ppermute x7, waiting for transfers between devices: 11.2 us -> 13.1 us  [exchange(): return lax.ppermute(value, ('tm', 'lat'), pairs)]
  transfers between devices with their start and end apart: 7 -> 7, of which waited for: 4 -> 4; matrix products, arithmetic and copies ran while one was open for 0% -> 0% of each run, Pallas kernels for 26% -> 21%
where the time goes in v7:
time: 30.4 us; the launch traced here: 30.3 us
  waiting for transfers between devices  13.1 us (43%)
  Pallas kernels  10.3 us (34%)
  starting transfers between devices  6.83 us (22%)
    ppermute x7, waiting for transfers between devices, exchange(): return lax.ppermute(value, ('tm', 'lat'), pairs)  13.1 us
    pallas_call x10, Pallas kernels, run(): pl.pallas_call(kernel, out_shape=outs, in_specs=[spec] * len(args), out_s...  10.3 us
    ppermute x7, starting transfers between devices, exchange(): return lax.ppermute(value, ('tm', 'lat'), pairs)  6.83 us
  transfers between devices with their start and end apart: 7, of which 4 were waited for; matrix products, arithmetic and copies ran while one was open for 0% of the time, Pallas kernels for 21%

profile of v7, /device:TPU:98, one launch (start us, length us, event | category | flops | bytes accessed | tf_op | source)
XLA Modules:
  0.0 30.3 jit_solution(14939707114761870124)
XLA Ops:
  0.0 1.3 %shard_map.73 = (bf16[512,128]{1,0:T(8,128)(2,1)S(1)}, bf16[512,128]{1,0:T(8,128)(2,1)S(1)}, bf16[384,128]{1,0:T(8,128)(2,1)S(1)}, bf16[384,128]{1,0:T(8,128)(2,...) custom-call(bf16[64,8,128]{2,1,0:T(8,128)(2,1)} %bitcast.8, ...), custom_call_target="tpu_custom_call" | custom-call | bytes 1048576 | tf_op jit(solution)/shard_map/pallas_call | solution.py:28
  1.3 3.3 %collective-permute-start = (bf16[384,128]{1,0:T(8,128)(2,1)S(1)}, bf16[384,128]{1,0:T(8,128)(2,1)S(1)}, u32[]{:S(2)}, u32[]{:S(2)}) collective-permute-start(bf16[384,128]{1,0:T(8,128)(2,1)S(1)} %get-tuple-element.41), channel_id=1, source_target_pairs={{0,1},{1,0},{2,3},{3,2},{4,5},{5,4},{6,7},{7,6},{8,9},{9,8},{10,11... | collective-permute-start | bytes 294920 | tf_op jit(solution)/shard_map/ppermute | solution.py:489
  4.6 0.3 %collective-permute-start.1 = (bf16[384,128]{1,0:T(8,128)(2,1)S(1)}, bf16[384,128]{1,0:T(8,128)(2,1)S(1)}, u32[]{:S(2)}, u32[]{:S(2)}) collective-permute-start(bf16[384,128]{1,0:T(8,128)(2,1)S(1)} %get-tuple-element.42), channel_id=1, source_target_pairs={{0,8},{1,2},{2,1},{3,4},{4,3},{5,6},{6,5},{7,15},{8,0},{9,10},{10,... | collective-permute-start | bytes 294920 | tf_op jit(solution)/shard_map/ppermute | solution.py:489
  4.9 0.4 %shard_map.74 = (f32[8,72,128]{2,1,0:T(8,128)S(1)}, bf16[256,576]{1,0:T(8,128)(2,1)S(1)}, bf16[1024,192]{1,0:T(8,128)(2,1)S(1)}, bf16[192,768]{1,0:T(8,128)(2,1)...) custom-call(bf16[64,256]{1,0:T(8,128)(2,1)S(1)} %get-tuple-element.43.obs_ref, ...), custom_call_target="tpu_custom_call" | custom-call | flops 41943040 | bytes 1048576 | tf_op jit(solution)/shard_map/pallas_call | solution.py:28
  5.3 0.9 %shard_map.75 = (bf16[1536,128]{1,0:T(8,128)(2,1)S(1)}, bf16[384,128]{1,0:T(8,128)(2,1)S(1)}) custom-call(bf16[512,128]{1,0:T(8,128)(2,1)S(1)} %get-tuple-element.40.state_ref.own_ref, bf16[256,576]{1,0:T(8,128)(2,1)S(1)} %get-tuple-element.48.kernel_ref, bf16[1024,192]{1,0:T(8,128)(2,1)S(1)} %get-tuple-element.49.quad_ref, ...), custom_call_target="tpu_custom_call" | custom-call | flops 251658240 | bytes 2097152 | tf_op jit(solution)/shard_map/pallas_call | solution.py:28
  6.2 2.5 %collective-permute-done.first_ref = bf16[384,128]{1,0:T(8,128)(2,1)S(1)} collective-permute-done((bf16[384,128]{1,0:T(8,128)(2,1)S(1)}, bf16[384,128]{1,0:T(8,128)(2,1)S(1)}, u32[]{:S(2)}, u32[]{:S(2)}) %collective-permute-start) | collective-permute-done | bytes 98336 | tf_op jit(solution)/shard_map/ppermute | solution.py:489
  8.7 2.9 %collective-permute-done.1.second_ref = bf16[384,128]{1,0:T(8,128)(2,1)S(1)} collective-permute-done((bf16[384,128]{1,0:T(8,128)(2,1)S(1)}, bf16[384,128]{1,0:T(8,128)(2,1)S(1)}, u32[]{:S(2)}, u32[]{:S(2)}) %collective-permute-start.1) | collective-permute-done | bytes 98336 | tf_op jit(solution)/shard_map/ppermute | solution.py:489
  11.6 0.1 shard_map.76
  11.7 0.1 collective-permute-start.4
  11.8 0.6 %collective-permute-start.3 = (bf16[512,128]{1,0:T(8,128)(2,1)S(1)}, bf16[512,128]{1,0:T(8,128)(2,1)S(1)}, u32[]{:S(2)}, u32[]{:S(2)}) collective-permute-start(bf16[512,128]{1,0:T(8,128)(2,1)S(1)} %get-tuple-element.40.state_ref.own_ref), channel_id=1, source_target_pairs={{0,2},{1,3},{2,0},{3,1},{4,6},{5,7},{6,4},{7,5},{8,16},{9,17},{10,... | collective-permute-start | bytes 393224 | tf_op jit(solution)/shard_map/ppermute | solution.py:489
  12.4 2.1 %collective-permute-start.2 = (bf16[384,128]{1,0:T(8,128)(2,1)S(1)}, bf16[384,128]{1,0:T(8,128)(2,1)S(1)}, u32[]{:S(2)}, u32[]{:S(2)}) collective-permute-start(bf16[384,128]{1,0:T(8,128)(2,1)S(1)} %get-tuple-element.56), channel_id=1, source_target_pairs={{0,2},{1,3},{2,0},{3,1},{4,6},{5,7},{6,4},{7,5},{8,16},{9,17},{10,... | collective-permute-start | bytes 294920 | tf_op jit(solution)/shard_map/ppermute | solution.py:489
  14.5 0.9 %shard_map.77 = (bf16[2048,128]{1,0:T(8,128)(2,1)S(1)}, bf16[512,128]{1,0:T(8,128)(2,1)S(1)}) custom-call(bf16[1024,128]{1,0:T(8,128)(2,1)S(1)} %get-tuple-element.58.state_ref.own_ref, bf16[256,576]{1,0:T(8,128)(2,1)S(1)} %get-tuple-element.48.kernel_ref, bf16[1024,192]{1,0:T(8,128)(2,1)S(1)} %get-tuple-element.49.quad_ref, ...), custom_call_target="tpu_custom_call" | custom-call | flops 335544320 | bytes 2097152 | tf_op jit(solution)/shard_map/pallas_call | solution.py:28
  15.4 3.2 %collective-permute-done.3.far_own_ref = bf16[512,128]{1,0:T(8,128)(2,1)S(1)} collective-permute-done((bf16[512,128]{1,0:T(8,128)(2,1)S(1)}, bf16[512,128]{1,0:T(8,128)(2,1)S(1)}, u32[]{:S(2)}, u32[]{:S(2)}) %collective-permute-start.3) | collective-permute-done | bytes 131104 | tf_op jit(solution)/shard_map/ppermute | solution.py:489
  18.6 0.0 collective-permute-done.4.near_ref
  18.6 2.0 %shard_map.78 = (bf16[768,128]{1,0:T(8,128)(2,1)S(1)}, bf16[768,128]{1,0:T(8,128)(2,1)S(1)}) custom-call(bf16[896,128]{1,0:T(8,128)(2,1)S(1)} %collective-permute-done.4.near_ref, bf16[512,128]{1,0:T(8,128)(2,1)S(1)} %collective-permute-done.3.far_own_ref, bf16[1024,128]{1,0:T(8,128)(2,1)S(1)} %get-tuple-element.58.state_ref.own_ref, ...), custom_call_target="tpu_custom_call" | custom-call | flops 503316480 | bytes 2097152 | tf_op jit(solution)/shard_map/pallas_call | solution.py:28
  20.6 0.0 collective-permute-done.2.far_ref
  20.6 1.0 %shard_map.79 = (bf16[768,128]{1,0:T(8,128)(2,1)S(1)}, bf16[640,128]{1,0:T(8,128)(2,1)S(1)}) custom-call(bf16[384,128]{1,0:T(8,128)(2,1)S(1)} %collective-permute-done.2.far_ref, bf16[512,128]{1,0:T(8,128)(2,1)S(1)} %collective-permute-done.3.far_own_ref, bf16[768,128]{1,0:T(8,128)(2,1)S(1)} %get-tuple-element.65.part_ref, ...), custom_call_target="tpu_custom_call" | custom-call | flops 503316480 | bytes 2097152 | tf_op jit(solution)/shard_map/pallas_call | solution.py:28
  21.6 0.1 collective-permute-start.6
  21.7 0.4 %collective-permute-start.5 = (bf16[640,128]{1,0:T(8,128)(2,1)S(1)}, bf16[640,128]{1,0:T(8,128)(2,1)S(1)}, u32[]{:S(2)}, u32[]{:S(2)}) collective-permute-start(bf16[640,128]{1,0:T(8,128)(2,1)S(1)} %get-tuple-element.71), channel_id=1, source_target_pairs={{0,2},{1,3},{2,0},{3,1},{4,6},{5,7},{6,4},{7,5},{8,16},{9,17},{10,... | collective-permute-start | bytes 491528 | tf_op jit(solution)/shard_map/ppermute | solution.py:489
  22.0 1.2 %shard_map.80 = (bf16[2560,128]{1,0:T(8,128)(2,1)S(1)}, bf16[640,128]{1,0:T(8,128)(2,1)S(1)}) custom-call(bf16[768,128]{1,0:T(8,128)(2,1)S(1)} %get-tuple-element.72.state_ref.own_ref, bf16[256,576]{1,0:T(8,128)(2,1)S(1)} %get-tuple-element.48.kernel_ref, bf16[1024,192]{1,0:T(8,128)(2,1)S(1)} %get-tuple-element.49.quad_ref, ...), custom_call_target="tpu_custom_call" | custom-call | flops 419430400 | bytes 2097152 | tf_op jit(solution)/shard_map/pallas_call | solution.py:28
  23.2 0.0 collective-permute-done.6.near_ref
  23.2 0.8 %shard_map.81.part_ref = bf16[512,128]{1,0:T(8,128)(2,1)S(1)} custom-call(bf16[640,128]{1,0:T(8,128)(2,1)S(1)} %collective-permute-done.6.near_ref, bf16[768,128]{1,0:T(8,128)(2,1)S(1)} %get-tuple-element.72.state_ref.own_ref, bf16[2560,128]{1,0:T(8,128)(2,1)S(1)} %get-tuple-element.73.active_ref, bf16[640,128]{1,0:T(8,128)(2,1)S(1)} %get-tuple-element.74.forecast_ref, ...), custom_call_target="tpu_custom_call" | custom-call | flops 335544320 | bytes 2097152 | tf_op jit(solution)/shard_map/pallas_call | solution.py:28
  24.1 4.6 %collective-permute-done.5.far_ref = bf16[640,128]{1,0:T(8,128)(2,1)S(1)} collective-permute-done((bf16[640,128]{1,0:T(8,128)(2,1)S(1)}, bf16[640,128]{1,0:T(8,128)(2,1)S(1)}, u32[]{:S(2)}, u32[]{:S(2)}) %collective-permute-start.5) | collective-permute-done | bytes 163872 | tf_op jit(solution)/shard_map/ppermute | solution.py:489
  28.7 1.6 %shard_map.82 = bf16[64,8,128]{2,1,0:T(8,128)(2,1)} custom-call(bf16[640,128]{1,0:T(8,128)(2,1)S(1)} %collective-permute-done.5.far_ref, bf16[512,128]{1,0:T(8,128)(2,1)S(1)} %shard_map.81.part_ref, bf16[768,128]{1,0:T(8,128)(2,1)S(1)} %get-tuple-element.72.state_ref.own_ref, bf16[512,128]{1,0:T(8,128)(2,1)S(1)} %get-tuple-element.67.bg_ref, ...), custom_call_target="tpu_custom_call" | custom-call | flops 335544320 | bytes 2097152 | tf_op jit(solution)/shard_map/pallas_call | solution.py:28
Async XLA Ops:
  1.3 7.4 %collective-permute-start = (bf16[384,128]{1,0:T(8,128)(2,1)S(1)}, bf16[384,128]{1,0:T(8,128)(2,1)S(1)}, u32[]{:S(2)}, u32[]{:S(2)}) collective-permute-start(bf16[384,128]{1,0:T(8,128)(2,1)S(1)} %get-tuple-element.41), channel_id=1, source_target_pairs={{0,1},{1,0},{2,3},{3,2},{4,5},{5,4},{6,7},{7,6},{8,9},{9,8},{10,11... | collective-permute-start | bytes 294920 | tf_op jit(solution)/shard_map/ppermute | solution.py:489
  4.6 7.0 %collective-permute-start.1 = (bf16[384,128]{1,0:T(8,128)(2,1)S(1)}, bf16[384,128]{1,0:T(8,128)(2,1)S(1)}, u32[]{:S(2)}, u32[]{:S(2)}) collective-permute-start(bf16[384,128]{1,0:T(8,128)(2,1)S(1)} %get-tuple-element.42), channel_id=1, source_target_pairs={{0,8},{1,2},{2,1},{3,4},{4,3},{5,6},{6,5},{7,15},{8,0},{9,10},{10,... | collective-permute-start | bytes 294920 | tf_op jit(solution)/shard_map/ppermute | solution.py:489
  11.7 6.9 %collective-permute-start.4 = (bf16[896,128]{1,0:T(8,128)(2,1)S(1)}, bf16[896,128]{1,0:T(8,128)(2,1)S(1)}, u32[]{:S(2)}, u32[]{:S(2)}) collective-permute-start(bf16[896,128]{1,0:T(8,128)(2,1)S(1)} %get-tuple-element.57), channel_id=1, source_target_pairs={{0,8},{1,9},{2,10},{3,11},{4,12},{5,13},{6,14},{7,15},{8,0},{9,1},... | collective-permute-start | bytes 688136 | tf_op jit(solution)/shard_map/ppermute | solution.py:489
  11.8 6.8 %collective-permute-start.3 = (bf16[512,128]{1,0:T(8,128)(2,1)S(1)}, bf16[512,128]{1,0:T(8,128)(2,1)S(1)}, u32[]{:S(2)}, u32[]{:S(2)}) collective-permute-start(bf16[512,128]{1,0:T(8,128)(2,1)S(1)} %get-tuple-element.40.state_ref.own_ref), channel_id=1, source_target_pairs={{0,2},{1,3},{2,0},{3,1},{4,6},{5,7},{6,4},{7,5},{8,16},{9,17},{10,... | collective-permute-start | bytes 393224 | tf_op jit(solution)/shard_map/ppermute | solution.py:489
  12.4 8.1 %collective-permute-start.2 = (bf16[384,128]{1,0:T(8,128)(2,1)S(1)}, bf16[384,128]{1,0:T(8,128)(2,1)S(1)}, u32[]{:S(2)}, u32[]{:S(2)}) collective-permute-start(bf16[384,128]{1,0:T(8,128)(2,1)S(1)} %get-tuple-element.56), channel_id=1, source_target_pairs={{0,2},{1,3},{2,0},{3,1},{4,6},{5,7},{6,4},{7,5},{8,16},{9,17},{10,... | collective-permute-start | bytes 294920 | tf_op jit(solution)/shard_map/ppermute | solution.py:489
  21.6 1.6 %collective-permute-start.6 = (bf16[640,128]{1,0:T(8,128)(2,1)S(1)}, bf16[640,128]{1,0:T(8,128)(2,1)S(1)}, u32[]{:S(2)}, u32[]{:S(2)}) collective-permute-start(bf16[640,128]{1,0:T(8,128)(2,1)S(1)} %get-tuple-element.71), channel_id=1, source_target_pairs={{0,8},{1,9},{2,10},{3,11},{4,12},{5,13},{6,14},{7,15},{8,0},{9,1},... | collective-permute-start | bytes 491528 | tf_op jit(solution)/shard_map/ppermute | solution.py:489
  21.7 7.0 %collective-permute-start.5 = (bf16[640,128]{1,0:T(8,128)(2,1)S(1)}, bf16[640,128]{1,0:T(8,128)(2,1)S(1)}, u32[]{:S(2)}, u32[]{:S(2)}) collective-permute-start(bf16[640,128]{1,0:T(8,128)(2,1)S(1)} %get-tuple-element.71), channel_id=1, source_target_pairs={{0,2},{1,3},{2,0},{3,1},{4,6},{5,7},{6,4},{7,5},{8,16},{9,17},{10,... | collective-permute-start | bytes 491528 | tf_op jit(solution)/shard_map/ppermute | solution.py:489

commit v8 on v7

--- a/solution.py
+++ b/solution.py
@@ -53,8 +53,8 @@
     return rows_of(ref, row, width)
 
 
-def beside(rows, a, b):
-    return jnp.concatenate([at(rows, a), at(rows, b)], axis=1)
+def beside(rows, *places):
+    return jnp.concatenate([at(rows, place) for place in places], axis=1)
 
 
 def latitude(row):
@@ -85,7 +85,7 @@
 
 def pack_kernel(
     x_hbm, obs_hbm, index_hbm, bg_hbm, taps_hbm, out_weight_hbm, bias_hbm, own_ref, bg_rows_ref,
-    first_ref, second_ref, obs_ref, index_ref, taps_ref, out_weight_ref, bias_ref, x_ref, bg_ref,
+    up_ref, down_ref, obs_ref, index_ref, taps_ref, out_weight_ref, bias_ref, x_ref, bg_ref,
     xs, bs, sems,
 ):
     copies = [
@@ -100,12 +100,10 @@
     for copy in copies:
         copy.start()
     copies[0].wait()
-    even = lax.rem(lax.axis_index("lat"), 2) == 0
 
     def send(place, up, down):
-        at = slice(place * C, (place + 1) * C)
-        first_ref[at, :] = jnp.where(even, down, up).astype(BF16)
-        second_ref[at, :] = jnp.where(even, up, down).astype(BF16)
+        up_ref[place * C : (place + 1) * C, :] = up.astype(BF16)
+        down_ref[place * C : (place + 1) * C, :] = down.astype(BF16)
 
     xs[...] = x_ref[...].astype(F32).reshape(ROWS * C, LON)
     for row in range(4):
@@ -136,17 +134,14 @@
 
 
 def extend_kernel(
-    own_ref, first_ref, second_ref, ext_ref, near_ref, far_ref, above_edge_ref, below_edge_ref
+    own_ref, above_ref, below_ref, ext_ref, near_ref, far_ref, above_edge_ref, below_edge_ref
 ):
     strip = lax.axis_index("lat")
-    even = lax.rem(strip, 2) == 0
     zero = jnp.zeros((X_PART, LON), BF16)
-    above = jnp.where(even, second_ref[...], first_ref[...])
-    below = jnp.where(even, first_ref[...], second_ref[...])
-    above_edge_ref[...] = above[X_PART:, :]
-    below_edge_ref[...] = below[X_PART:, :]
-    above = jnp.where(strip > 0, above[:X_PART, :], zero)
-    below = jnp.where(strip < lax.axis_size("lat") - 1, below[:X_PART, :], zero)
+    above_edge_ref[...] = above_ref[X_PART:, :]
+    below_edge_ref[...] = below_ref[X_PART:, :]
+    above = jnp.where(strip > 0, above_ref[:X_PART, :], zero)
+    below = jnp.where(strip < lax.axis_size("lat") - 1, below_ref[:X_PART, :], zero)
     far_ref[: 3 * C, :] = above[C:, :]
     far_ref[3 * C :, :] = below[: 3 * C, :]
     near_ref[: 3 * C, :] = above[C:, :]
@@ -161,52 +156,37 @@
     return value if b == 1 else pltpu.roll(value, 1 if b == 0 else LON - 1, 1)
 
 
-def actives(work, rows, kernel_ref, quad_ref, bias_ref, shifted, mixed):
-    quads, pairs = work
-    bias = jnp.concatenate([bias_ref[...], bias_ref[...]], axis=1)
-    for place, pair in enumerate(pair for quad in quads for pair in quad):
+def actives(work, rows, conv_ref, bias_ref, mixed):
+    for place, pair in enumerate(pair for group in work for pair in group):
         d = [at(rows, pair[0] + a).astype(F32) for a in range(4)]
         for j, value in enumerate((d[0] - d[2], d[1] + d[2], d[2] - d[1], d[1] - d[3])):
             for b in range(3):
                 start = (3 * place + b) * C
                 mixed[j, start : start + C, :] = turn(value, b).astype(BF16)
-    for place in sorted({first + a for pair in pairs for first in pair for a in range(3)}):
-        value = at(rows, place)
-        for b in range(3):
-            moved = value if b == 1 else turn(value.astype(F32), b).astype(BF16)
-            shifted[b, place * C : (place + 1) * C, :] = moved
-    for place, (first, second) in enumerate(quads):
-        start, middle, end = (3 * C * (2 * place + n) for n in range(3))
+    place = 0
+    for group in work:
+        bias = jnp.concatenate([bias_ref[...]] * len(group), axis=1)
+        spans = [slice(3 * C * (place + n), 3 * C * (place + n + 1)) for n in range(len(group))]
+        place += len(group)
         m = [
             jnp.dot(
-                quad_ref[j * HID : (j + 1) * HID, :],
-                jnp.concatenate([mixed[j, start:middle, :], mixed[j, middle:end, :]], axis=1),
+                conv_ref[j * HID : (j + 1) * HID, :],
+                jnp.concatenate([mixed[j, span, :] for span in spans], axis=1),
                 preferred_element_type=F32,
             )
             for j in range(4)
         ]
-        yield (first[0], second[0]), jnp.tanh(m[0] + m[1] + m[2] + bias).astype(BF16)
-        yield (first[1], second[1]), jnp.tanh(m[1] - m[2] - m[3] + bias).astype(BF16)
-
-    def stack(first):
-        return jnp.concatenate(
-            [
-                shifted[b, (first + a) * C : (first + a + 1) * C, :]
-                for a in range(3)
-                for b in range(3)
-            ],
-            axis=0,
-        )
-
-    for pair in pairs:
-        cells = jnp.concatenate([stack(row) for row in pair], axis=1)
-        before = jnp.dot(kernel_ref[...], cells, preferred_element_type=F32) + bias
-        yield pair, jnp.tanh(before).astype(BF16)
+        upper, lower = zip(*group)
+        yield upper, jnp.tanh(m[0] + m[1] + m[2] + bias).astype(BF16)
+        yield lower, jnp.tanh(m[1] - m[2] - m[3] + bias).astype(BF16)
 
 
 def rows_of_work(work):
-    quads, pairs = work
-    return sorted([row for quad in quads for pair in quad for row in pair] + [r for p in pairs for r in p])
+    return sorted(row for group in work for pair in group for row in pair)
+
+
+def lanes_of(half):
+    return slice(half * LON, (half + 1) * LON)
 
 
 def store_pair(ref, first, value, width=C):
@@ -215,35 +195,32 @@
 
 
 def forward_kernel(
-    work, state_ref, kernel_ref, quad_ref, bias_ref, out_weight_ref, active_ref, forecast_ref,
-    shifted, mixed,
+    work, state_ref, conv_ref, bias_ref, out_weight_ref, active_ref, forecast_ref, mixed
 ):
     rows = rows_in(state_ref, 0, state_ref.shape[0] // C)
-    places = {row: place for place, row in enumerate(rows_of_work(work))}
-    for pair, active in actives(work, rows, kernel_ref, quad_ref, bias_ref, shifted, mixed):
+    order = {row: place for place, row in enumerate(rows_of_work(work))}
+    for some, active in actives(work, rows, conv_ref, bias_ref, mixed):
         step = jnp.dot(out_weight_ref[...], active, preferred_element_type=F32)
-        centre = beside(rows, pair[0] + 1, pair[1] + 1).astype(F32)
+        centre = beside(rows, *(row + 1 for row in some)).astype(F32)
         forecast = (centre + step).astype(BF16)
-        for half, row in enumerate(pair):
-            lanes = slice(half * LON, (half + 1) * LON)
-            place = places[row]
-            active_ref[place * HID : (place + 1) * HID, :] = active[:, lanes]
-            forecast_ref[place * C : (place + 1) * C, :] = forecast[:, lanes]
+        for half, row in enumerate(some):
+            place = order[row]
+            active_ref[place * HID : (place + 1) * HID, :] = active[:, lanes_of(half)]
+            forecast_ref[place * C : (place + 1) * C, :] = forecast[:, lanes_of(half)]
 
 
 def prepare_kernel(
-    obs_ref, index_ref, kernel_ref, bias_ref, out_weight_ref, sums_ref, forward_ref, quad_ref,
-    back_ref, wide_bias_ref, out_back_ref,
+    obs_ref, index_ref, kernel_ref, bias_ref, out_weight_ref, sums_ref, conv_ref, back_ref,
+    wide_bias_ref, out_back_ref,
 ):
     low, high = local_cells(index_ref[...])
     values = with_ones(obs_ref[...])
     for row in range(ROWS):
         sums_ref[row] = observation_sums(values, low, high, row)[:72, :]
-    forward_ref[...] = kernel_ref[...].T
     g = [kernel_ref[a * 3 * C : (a + 1) * 3 * C, :].astype(F32) for a in range(3)]
     ends = g[0] + g[2]
     for j, value in enumerate((g[0], 0.5 * (ends + g[1]), 0.5 * (ends - g[1]), g[2])):
-        quad_ref[j * HID : (j + 1) * HID, :] = value.astype(BF16).T
+        conv_ref[j * HID : (j + 1) * HID, :] = value.astype(BF16).T
     out_back_ref[...] = out_weight_ref[...].T
     wide_bias_ref[...] = jnp.broadcast_to(bias_ref[...], (LON, HID)).T
     for a in range(3):
@@ -251,16 +228,16 @@
 
 
 def residual_part(
-    work, prev, own_ref, kernel_ref, quad_ref, bias_ref, out_weight_ref, shifted, mixed, take
+    work, prev, own_ref, conv_ref, bias_ref, out_weight_ref, mixed, take
 ):
     own_rows = rows_in(own_ref, 2, max(rows_of_work(work)) + 1)
-    for (a, b), active in actives(work, prev, kernel_ref, quad_ref, bias_ref, shifted, mixed):
+    for some, active in actives(work, prev, conv_ref, bias_ref, mixed):
         step = jnp.dot(out_weight_ref[...], active, preferred_element_type=F32)
-        centre = beside(prev, a + 1, b + 1).astype(F32)
+        centre = beside(prev, *(row + 1 for row in some)).astype(F32)
         guess = (centre + step).astype(BF16).astype(F32)
-        resid = (beside(own_rows, a, b).astype(F32) - guess).astype(BF16)
-        take(a, resid[:, :LON])
-        take(b, resid[:, LON:])
+        resid = (beside(own_rows, *some).astype(F32) - guess).astype(BF16)
+        for half, row in enumerate(some):
+            take(row, resid[:, lanes_of(half)])
 
 
 def strip_ends():
@@ -312,18 +289,18 @@
     return tuple(((row, row + 1), (row + 2, row + 3)) for row in range(0, count - 3, 4))
 
 
-INSIDE = (quads_of(4), ((4, 5),))
-OUTSIDE = ((((0, 1), (2, 3)), ((10, 11), (12, 13))), ())
-INNER = ((((3, 4), (5, 6)),), ((7, 8),))
-OUTER = ((((0, 1), (10, 11)),), ((2, 9),))
-TWELVE = (quads_of(12), ())
-TEN = (quads_of(8), ((8, 9),))
-EIGHT = (quads_of(8), ())
+INSIDE = (((0, 1), (2, 3)), ((4, 5),))
+OUTSIDE = (((0, 1), (2, 3)), ((10, 11), (12, 13)))
+INNER = (((4, 5), (6, 7)),)
+OUTER = (((0, 1), (2, 3)), ((8, 9), (10, 11)))
+TWELVE = quads_of(12)
+TEN = quads_of(8) + (((8, 9),),)
+EIGHT = quads_of(8)
 
 
 def first_near_kernel(
     near_ref, far_own_ref, own_ref, active_in_ref, forecast_in_ref, active_out_ref, forecast_out_ref,
-    kernel_ref, quad_ref, bias_ref, out_weight_ref, back_ref, out_back_ref, part_ref, inner_ref, shifted, mixed,
+    conv_ref, bias_ref, out_weight_ref, back_ref, out_back_ref, part_ref, inner_ref, mixed,
     cot, target,
 ):
     def put(ref):
@@ -346,15 +323,15 @@
     def _():
         prev = [None] * 3 + rows_in(far_own_ref, 0, ROWS)
         residual_part(
-            INNER, prev, own_ref, kernel_ref, quad_ref, bias_ref, out_weight_ref,
-            shifted, mixed, put(inner_ref)
+            INNER, prev, own_ref, conv_ref, bias_ref, out_weight_ref,
+            mixed, put(inner_ref)
         )
 
     @pl.when(odd)
     def _():
         residual_part(
-            TWELVE, rows_in(near_ref, 0, 14), own_ref, kernel_ref, quad_ref, bias_ref, out_weight_ref,
-            shifted, mixed, put(part_ref),
+            TWELVE, rows_in(near_ref, 0, 14), own_ref, conv_ref, bias_ref, out_weight_ref,
+            mixed, put(part_ref),
         )
 
 
@@ -364,8 +341,8 @@
 
 def first_kernel(
     far_ref, far_own_ref, part_ref, inner_ref, own_ref, bg_ref, active_in_ref, forecast_in_ref,
-    active_out_ref, forecast_out_ref, kernel_ref, quad_ref, bias_ref, out_weight_ref, back_ref, out_back_ref,
-    sums_ref, above_ref, below_ref, state_ref, sent_ref, shifted, mixed, cot, target,
+    active_out_ref, forecast_out_ref, conv_ref, bias_ref, out_weight_ref, back_ref, out_back_ref,
+    sums_ref, above_ref, below_ref, state_ref, sent_ref, mixed, cot, target,
 ):
     top, bottom = strip_ends()
 
@@ -392,10 +369,10 @@
     @pl.when(even)
     def _():
         residual_part(
-            OUTER, far, own_ref, kernel_ref, quad_ref, bias_ref, out_weight_ref, shifted,
+            OUTER, far, own_ref, conv_ref, bias_ref, out_weight_ref,
             mixed, lambda row, resid: step(row, resid, rows_of(part_ref, row)),
         )
-        for row in range(3, 9):
+        for row in range(4, 8):
             step(row, rows_of(inner_ref, row), rows_of(part_ref, row))
 
     @pl.when(opening)
@@ -418,8 +395,8 @@
 
 
 def second_near_kernel(
-    near_ref, own_ref, active_ref, forecast_ref, kernel_ref, quad_ref, bias_ref, out_weight_ref,
-    back_ref, out_back_ref, part_ref, shifted, mixed, cot, target,
+    near_ref, own_ref, active_ref, forecast_ref, conv_ref, bias_ref, out_weight_ref,
+    back_ref, out_back_ref, part_ref, mixed, cot, target,
 ):
     def take(row, value):
         part_ref[row * C : (row + 1) * C, :] = value
@@ -437,14 +414,14 @@
     @pl.when(odd)
     def _():
         residual_part(
-            EIGHT, near, own_ref, kernel_ref, quad_ref, bias_ref, out_weight_ref,
-            shifted, mixed, take
+            EIGHT, near, own_ref, conv_ref, bias_ref, out_weight_ref,
+            mixed, take
         )
 
 
 def second_kernel(
-    far_ref, part_ref, own_ref, bg_ref, active_ref, forecast_ref, kernel_ref, quad_ref, bias_ref,
-    out_weight_ref, back_ref, out_back_ref, sums_ref, out_ref, shifted, mixed, cot, target, wide,
+    far_ref, part_ref, own_ref, bg_ref, active_ref, forecast_ref, conv_ref, bias_ref,
+    out_weight_ref, back_ref, out_back_ref, sums_ref, out_ref, mixed, cot, target, wide,
 ):
     def step(row, resid, adjoint):
         own = rows_of(own_ref, row + 2).astype(F32)
@@ -458,7 +435,7 @@
     @pl.when(even)
     def _():
         residual_part(
-            EIGHT, far, own_ref, kernel_ref, quad_ref, bias_ref, out_weight_ref, shifted,
+            EIGHT, far, own_ref, conv_ref, bias_ref, out_weight_ref,
             mixed, lambda row, resid: step(row, resid, rows_of(part_ref, row)),
         )
 
@@ -489,14 +466,12 @@
     return lax.ppermute(value, ("tm", "lat"), pairs)
 
 
-def near_strip(window, strip, last_window, last_strip):
-    return window, strip ^ 1
-
-
-def far_strip(window, strip, last_window, last_strip):
-    if strip in (0, last_strip):
-        return window ^ 1, strip
-    return window, ((strip + 1) ^ 1) - 1
+def strip_below(window, strip, last_window, last_strip):
+    return window, (strip + 1) % (last_strip + 1)
+
+
+def strip_above(window, strip, last_window, last_strip):
+    return window, (strip - 1) % (last_strip + 1)
 
 
 def near_window(window, strip, last_window, last_strip):
@@ -515,7 +490,6 @@
 
 def conv_scratch(count):
     return [
-        pltpu.VMEM((3, (count + 2) * C, LON), BF16),
         pltpu.VMEM((4, (count // 2) * 3 * C, LON), BF16),
     ]
 
@@ -542,10 +516,10 @@
             (shape(count * HID), shape(count * C)),
             conv_scratch(state.shape[0] // C - 2),
             row_flops(count), 2 << 20,
-        )(state, forward_weight, quad_weight, bias, out_weight)
+        )(state, conv_weight, bias, out_weight)
 
     taps = jnp.transpose(input_kernel_weight, (0, 1, 3, 2)).reshape(9 * C, HID)
-    own, ground, first, second, observed, index, taps, out_weight, bias = call(
+    own, ground, up, down, observed, index, taps, out_weight, bias = call(
         pack_kernel,
         (
             shape(ROWS * C), shape(ROWS * C), shape(PAYLOAD), shape(PAYLOAD),
@@ -572,15 +546,14 @@
             )
         )
     )
-    second = exchange(second, far_strip)
-    first = exchange(first, near_strip)
+    above = exchange(down, strip_below)
+    below = exchange(up, strip_above)
     far_own = exchange(own, far_window)
 
-    sums, forward_weight, quad_weight, back_weight, bias, out_back = call(
+    sums, conv_weight, back_weight, bias, out_back = call(
         prepare_kernel,
         (
             jax.ShapeDtypeStruct((ROWS, 72, LON), F32),
-            jax.ShapeDtypeStruct((HID, 9 * C), BF16),
             jax.ShapeDtypeStruct((4 * HID, 3 * C), BF16),
             jax.ShapeDtypeStruct((3 * C, 3 * HID), BF16),
             jax.ShapeDtypeStruct((HID, LON), F32),
@@ -588,15 +561,15 @@
         ),
         [], ROWS * 2 * 80 * OBS * LON, 1 << 20,
     )(observed, index, taps, bias, out_weight)
-    weights = (forward_weight, quad_weight, bias, out_weight, back_weight, out_back)
+    weights = (conv_weight, bias, out_weight, back_weight, out_back)
     inside = forward(INSIDE, own)
-    first, second, inside, sums = lax.optimization_barrier((first, second, inside, sums))
-
-    ext, sent, halo, above, below = call(
+    above, below, inside, sums = lax.optimization_barrier((above, below, inside, sums))
+
+    ext, sent, halo, above_edge, below_edge = call(
         extend_kernel,
         (shape(16 * C), shape(14 * C), shape(6 * C), shape(2 * C), shape(2 * C)),
         [], 0, 1 << 20,
-    )(own, first, second)
+    )(own, above, below)
     far = exchange(halo, far_window)
     near = exchange(sent, near_window)
     outside = forward(OUTSIDE, ext)
@@ -608,7 +581,8 @@
         first_kernel, (shape(12 * C), shape(10 * C)), gradient_scratch(12), row_flops(12),
         2 << 20,
     )(
-        far, far_own, part, inner, ext, ground, *inside, *outside, *weights, sums, above, below
+        far, far_own, part, inner, ext, ground, *inside, *outside, *weights, sums,
+        above_edge, below_edge,
     )
     far = exchange(sent, far_window)
     near = exchange(sent, near_window)

time: 30.4 us -> 31.2 us (1.026)
  the two profiles are of different devices: /device:TPU:98 before, /device:TPU:41 now
where the time goes in v8:
time: 31.2 us; the launch traced here: 31.1 us
  waiting for transfers between devices  11.8 us (38%)
  starting transfers between devices  9.82 us (31%)
  Pallas kernels  9.43 us (30%)
    ppermute x7, waiting for transfers between devices, exchange(): return lax.ppermute(value, ('tm', 'lat'), pairs)  11.8 us
    ppermute x7, starting transfers between devices, exchange(): return lax.ppermute(value, ('tm', 'lat'), pairs)  9.82 us
    pallas_call x10, Pallas kernels, run(): pl.pallas_call(kernel, out_shape=outs, in_specs=[spec] * len(args), out_s...  9.43 us
  transfers between devices with their start and end apart: 7, of which 5 were waited for; matrix products, arithmetic and copies ran while one was open for 0% of the time, Pallas kernels for 18%

profile of v8, /device:TPU:41, one launch (start us, length us, event | category | flops | bytes accessed | tf_op | source)
XLA Modules:
  0.0 31.1 jit_solution(11491083242463484146)
XLA Ops:
  0.0 1.3 %shard_map.73 = (bf16[512,128]{1,0:T(8,128)(2,1)S(1)}, bf16[512,128]{1,0:T(8,128)(2,1)S(1)}, bf16[384,128]{1,0:T(8,128)(2,1)S(1)}, bf16[384,128]{1,0:T(8,128)(2,...) custom-call(bf16[64,8,128]{2,1,0:T(8,128)(2,1)} %bitcast.8, ...), custom_call_target="tpu_custom_call" | custom-call | bytes 1048576 | tf_op jit(solution)/shard_map/pallas_call | solution.py:28
  1.3 2.1 %collective-permute-start = (bf16[384,128]{1,0:T(8,128)(2,1)S(1)}, bf16[384,128]{1,0:T(8,128)(2,1)S(1)}, u32[]{:S(2)}, u32[]{:S(2)}) collective-permute-start(bf16[384,128]{1,0:T(8,128)(2,1)S(1)} %get-tuple-element.40), channel_id=1, source_target_pairs={{0,1},{1,2},{2,3},{3,4},{4,5},{5,6},{6,7},{7,0},{8,9},{9,10},{10,1... | collective-permute-start | bytes 294920 | tf_op jit(solution)/shard_map/ppermute | solution.py:466
  3.4 3.1 %collective-permute-start.1 = (bf16[384,128]{1,0:T(8,128)(2,1)S(1)}, bf16[384,128]{1,0:T(8,128)(2,1)S(1)}, u32[]{:S(2)}, u32[]{:S(2)}) collective-permute-start(bf16[384,128]{1,0:T(8,128)(2,1)S(1)} %get-tuple-element.41), channel_id=1, source_target_pairs={{0,7},{1,0},{2,1},{3,2},{4,3},{5,4},{6,5},{7,6},{8,15},{9,8},{10,9... | collective-permute-start | bytes 294920 | tf_op jit(solution)/shard_map/ppermute | solution.py:466
  6.5 0.3 %shard_map.74 = (f32[8,72,128]{2,1,0:T(8,128)S(1)}, bf16[1024,192]{1,0:T(8,128)(2,1)S(1)}, bf16[192,768]{1,0:T(8,128)(2,1)S(1)}, f32[256,128]{1,0:T(8,128)S(1)}, bf16[256,64]{1,0:T(8,128)(2,1)S(1)}) custom-call(bf16[64,256]{1,0:T(8,128)(2,1)S(1)} %get-tuple-element.42.obs_ref, s32[1,256]{1,0:T(1,128)S(1)} %get-tuple-element.43.index_ref, ...), custom_call_target="tpu_custom_call" | custom-call | flops 41943040 | bytes 1048576 | tf_op jit(solution)/shard_map/pallas_call | solution.py:28
  6.8 0.9 %shard_map.75 = (bf16[1536,128]{1,0:T(8,128)(2,1)S(1)}, bf16[384,128]{1,0:T(8,128)(2,1)S(1)}) custom-call(bf16[512,128]{1,0:T(8,128)(2,1)S(1)} %get-tuple-element.39.state_ref.own_ref, bf16[1024,192]{1,0:T(8,128)(2,1)S(1)} %get-tuple-element.47.conv_ref, f32[256,128]{1,0:T(8,128)S(1)} %get-tuple-element.48.bias_ref, ...), custom_call_target="tpu_custom_call" | custom-call | flops 251658240 | bytes 2097152 | tf_op jit(solution)/shard_map/pallas_call | solution.py:28
  7.7 0.9 %collective-permute-done.above_ref = bf16[384,128]{1,0:T(8,128)(2,1)S(1)} collective-permute-done((bf16[384,128]{1,0:T(8,128)(2,1)S(1)}, bf16[384,128]{1,0:T(8,128)(2,1)S(1)}, u32[]{:S(2)}, u32[]{:S(2)}) %collective-permute-start) | collective-permute-done | bytes 98336 | tf_op jit(solution)/shard_map/ppermute | solution.py:466
  8.6 3.1 %collective-permute-done.1.below_ref = bf16[384,128]{1,0:T(8,128)(2,1)S(1)} collective-permute-done((bf16[384,128]{1,0:T(8,128)(2,1)S(1)}, bf16[384,128]{1,0:T(8,128)(2,1)S(1)}, u32[]{:S(2)}, u32[]{:S(2)}) %collective-permute-start.1) | collective-permute-done | bytes 98336 | tf_op jit(solution)/shard_map/ppermute | solution.py:466
  11.6 0.1 shard_map.76
  11.7 0.7 %collective-permute-start.4 = (bf16[896,128]{1,0:T(8,128)(2,1)S(1)}, bf16[896,128]{1,0:T(8,128)(2,1)S(1)}, u32[]{:S(2)}, u32[]{:S(2)}) collective-permute-start(bf16[896,128]{1,0:T(8,128)(2,1)S(1)} %get-tuple-element.55), channel_id=1, source_target_pairs={{0,8},{1,9},{2,10},{3,11},{4,12},{5,13},{6,14},{7,15},{8,0},{9,1},... | collective-permute-start | bytes 688136 | tf_op jit(solution)/shard_map/ppermute | solution.py:466
  12.4 1.6 %collective-permute-start.3 = (bf16[512,128]{1,0:T(8,128)(2,1)S(1)}, bf16[512,128]{1,0:T(8,128)(2,1)S(1)}, u32[]{:S(2)}, u32[]{:S(2)}) collective-permute-start(bf16[512,128]{1,0:T(8,128)(2,1)S(1)} %get-tuple-element.39.state_ref.own_ref), channel_id=1, source_target_pairs={{0,2},{1,3},{2,0},{3,1},{4,6},{5,7},{6,4},{7,5},{8,16},{9,17},{10,... | collective-permute-start | bytes 393224 | tf_op jit(solution)/shard_map/ppermute | solution.py:466
  14.0 1.0 %collective-permute-start.2 = (bf16[384,128]{1,0:T(8,128)(2,1)S(1)}, bf16[384,128]{1,0:T(8,128)(2,1)S(1)}, u32[]{:S(2)}, u32[]{:S(2)}) collective-permute-start(bf16[384,128]{1,0:T(8,128)(2,1)S(1)} %get-tuple-element.54), channel_id=1, source_target_pairs={{0,2},{1,3},{2,0},{3,1},{4,6},{5,7},{6,4},{7,5},{8,16},{9,17},{10,... | collective-permute-start | bytes 294920 | tf_op jit(solution)/shard_map/ppermute | solution.py:466
  15.0 0.9 %shard_map.77 = (bf16[2048,128]{1,0:T(8,128)(2,1)S(1)}, bf16[512,128]{1,0:T(8,128)(2,1)S(1)}) custom-call(bf16[1024,128]{1,0:T(8,128)(2,1)S(1)} %get-tuple-element.56.state_ref.own_ref, bf16[1024,192]{1,0:T(8,128)(2,1)S(1)} %get-tuple-element.47.conv_ref, f32[256,128]{1,0:T(8,128)S(1)} %get-tuple-element.48.bias_ref, ...), custom_call_target="tpu_custom_call" | custom-call | flops 335544320 | bytes 2097152 | tf_op jit(solution)/shard_map/pallas_call | solution.py:28
  15.9 3.2 %collective-permute-done.3.far_own_ref = bf16[512,128]{1,0:T(8,128)(2,1)S(1)} collective-permute-done((bf16[512,128]{1,0:T(8,128)(2,1)S(1)}, bf16[512,128]{1,0:T(8,128)(2,1)S(1)}, u32[]{:S(2)}, u32[]{:S(2)}) %collective-permute-start.3) | collective-permute-done | bytes 131104 | tf_op jit(solution)/shard_map/ppermute | solution.py:466
  19.1 0.0 collective-permute-done.4.near_ref
  19.1 1.2 %shard_map.78 = (bf16[768,128]{1,0:T(8,128)(2,1)S(1)}, bf16[768,128]{1,0:T(8,128)(2,1)S(1)}) custom-call(bf16[896,128]{1,0:T(8,128)(2,1)S(1)} %collective-permute-done.4.near_ref, bf16[512,128]{1,0:T(8,128)(2,1)S(1)} %collective-permute-done.3.far_own_ref, bf16[1024,128]{1,0:T(8,128)(2,1)S(1)} %get-tuple-element.56.state_ref.own_ref, ...), custom_call_target="tpu_custom_call" | custom-call | flops 503316480 | bytes 2097152 | tf_op jit(solution)/shard_map/pallas_call | solution.py:28
  20.3 0.7 %collective-permute-done.2.far_ref = bf16[384,128]{1,0:T(8,128)(2,1)S(1)} collective-permute-done((bf16[384,128]{1,0:T(8,128)(2,1)S(1)}, bf16[384,128]{1,0:T(8,128)(2,1)S(1)}, u32[]{:S(2)}, u32[]{:S(2)}) %collective-permute-start.2) | collective-permute-done | bytes 98336 | tf_op jit(solution)/shard_map/ppermute | solution.py:466
  21.1 1.1 %shard_map.79 = (bf16[768,128]{1,0:T(8,128)(2,1)S(1)}, bf16[640,128]{1,0:T(8,128)(2,1)S(1)}) custom-call(bf16[384,128]{1,0:T(8,128)(2,1)S(1)} %collective-permute-done.2.far_ref, bf16[512,128]{1,0:T(8,128)(2,1)S(1)} %collective-permute-done.3.far_own_ref, bf16[768,128]{1,0:T(8,128)(2,1)S(1)} %get-tuple-element.63.part_ref, ...), custom_call_target="tpu_custom_call" | custom-call | flops 503316480 | bytes 2097152 | tf_op jit(solution)/shard_map/pallas_call | solution.py:28
  22.1 0.1 collective-permute-start.6
  22.2 1.3 %collective-permute-start.5 = (bf16[640,128]{1,0:T(8,128)(2,1)S(1)}, bf16[640,128]{1,0:T(8,128)(2,1)S(1)}, u32[]{:S(2)}, u32[]{:S(2)}) collective-permute-start(bf16[640,128]{1,0:T(8,128)(2,1)S(1)} %get-tuple-element.69), channel_id=1, source_target_pairs={{0,2},{1,3},{2,0},{3,1},{4,6},{5,7},{6,4},{7,5},{8,16},{9,17},{10,... | collective-permute-start | bytes 491528 | tf_op jit(solution)/shard_map/ppermute | solution.py:466
  23.5 1.2 %shard_map.80 = (bf16[2560,128]{1,0:T(8,128)(2,1)S(1)}, bf16[640,128]{1,0:T(8,128)(2,1)S(1)}) custom-call(bf16[768,128]{1,0:T(8,128)(2,1)S(1)} %get-tuple-element.70.state_ref.own_ref, bf16[1024,192]{1,0:T(8,128)(2,1)S(1)} %get-tuple-element.47.conv_ref, f32[256,128]{1,0:T(8,128)S(1)} %get-tuple-element.48.bias_ref, ...), custom_call_target="tpu_custom_call" | custom-call | flops 419430400 | bytes 2097152 | tf_op jit(solution)/shard_map/pallas_call | solution.py:28
  24.7 0.0 collective-permute-done.6.near_ref
  24.7 0.9 %shard_map.81.part_ref = bf16[512,128]{1,0:T(8,128)(2,1)S(1)} custom-call(bf16[640,128]{1,0:T(8,128)(2,1)S(1)} %collective-permute-done.6.near_ref, bf16[768,128]{1,0:T(8,128)(2,1)S(1)} %get-tuple-element.70.state_ref.own_ref, bf16[2560,128]{1,0:T(8,128)(2,1)S(1)} %get-tuple-element.71.active_ref, bf16[640,128]{1,0:T(8,128)(2,1)S(1)} %get-tuple-element.72.forecast_ref, ...), custom_call_target="tpu_custom_call" | custom-call | flops 335544320 | bytes 2097152 | tf_op jit(solution)/shard_map/pallas_call | solution.py:28
  25.6 4.0 %collective-permute-done.5.far_ref = bf16[640,128]{1,0:T(8,128)(2,1)S(1)} collective-permute-done((bf16[640,128]{1,0:T(8,128)(2,1)S(1)}, bf16[640,128]{1,0:T(8,128)(2,1)S(1)}, u32[]{:S(2)}, u32[]{:S(2)}) %collective-permute-start.5) | collective-permute-done | bytes 163872 | tf_op jit(solution)/shard_map/ppermute | solution.py:466
  29.6 1.5 %shard_map.82 = bf16[64,8,128]{2,1,0:T(8,128)(2,1)} custom-call(bf16[640,128]{1,0:T(8,128)(2,1)S(1)} %collective-permute-done.5.far_ref, bf16[512,128]{1,0:T(8,128)(2,1)S(1)} %shard_map.81.part_ref, bf16[768,128]{1,0:T(8,128)(2,1)S(1)} %get-tuple-element.70.state_ref.own_ref, bf16[512,128]{1,0:T(8,128)(2,1)S(1)} %get-tuple-element.65.bg_ref, ...), custom_call_target="tpu_custom_call" | custom-call | flops 335544320 | bytes 2097152 | tf_op jit(solution)/shard_map/pallas_call | solution.py:28
Async XLA Ops:
  1.3 7.3 %collective-permute-start = (bf16[384,128]{1,0:T(8,128)(2,1)S(1)}, bf16[384,128]{1,0:T(8,128)(2,1)S(1)}, u32[]{:S(2)}, u32[]{:S(2)}) collective-permute-start(bf16[384,128]{1,0:T(8,128)(2,1)S(1)} %get-tuple-element.40), channel_id=1, source_target_pairs={{0,1},{1,2},{2,3},{3,4},{4,5},{5,6},{6,7},{7,0},{8,9},{9,10},{10,1... | collective-permute-start | bytes 294920 | tf_op jit(solution)/shard_map/ppermute | solution.py:466
  3.4 8.2 %collective-permute-start.1 = (bf16[384,128]{1,0:T(8,128)(2,1)S(1)}, bf16[384,128]{1,0:T(8,128)(2,1)S(1)}, u32[]{:S(2)}, u32[]{:S(2)}) collective-permute-start(bf16[384,128]{1,0:T(8,128)(2,1)S(1)} %get-tuple-element.41), channel_id=1, source_target_pairs={{0,7},{1,0},{2,1},{3,2},{4,3},{5,4},{6,5},{7,6},{8,15},{9,8},{10,9... | collective-permute-start | bytes 294920 | tf_op jit(solution)/shard_map/ppermute | solution.py:466
  11.7 7.4 %collective-permute-start.4 = (bf16[896,128]{1,0:T(8,128)(2,1)S(1)}, bf16[896,128]{1,0:T(8,128)(2,1)S(1)}, u32[]{:S(2)}, u32[]{:S(2)}) collective-permute-start(bf16[896,128]{1,0:T(8,128)(2,1)S(1)} %get-tuple-element.55), channel_id=1, source_target_pairs={{0,8},{1,9},{2,10},{3,11},{4,12},{5,13},{6,14},{7,15},{8,0},{9,1},... | collective-permute-start | bytes 688136 | tf_op jit(solution)/shard_map/ppermute | solution.py:466
  12.4 6.7 %collective-permute-start.3 = (bf16[512,128]{1,0:T(8,128)(2,1)S(1)}, bf16[512,128]{1,0:T(8,128)(2,1)S(1)}, u32[]{:S(2)}, u32[]{:S(2)}) collective-permute-start(bf16[512,128]{1,0:T(8,128)(2,1)S(1)} %get-tuple-element.39.state_ref.own_ref), channel_id=1, source_target_pairs={{0,2},{1,3},{2,0},{3,1},{4,6},{5,7},{6,4},{7,5},{8,16},{9,17},{10,... | collective-permute-start | bytes 393224 | tf_op jit(solution)/shard_map/ppermute | solution.py:466
  14.0 7.0 %collective-permute-start.2 = (bf16[384,128]{1,0:T(8,128)(2,1)S(1)}, bf16[384,128]{1,0:T(8,128)(2,1)S(1)}, u32[]{:S(2)}, u32[]{:S(2)}) collective-permute-start(bf16[384,128]{1,0:T(8,128)(2,1)S(1)} %get-tuple-element.54), channel_id=1, source_target_pairs={{0,2},{1,3},{2,0},{3,1},{4,6},{5,7},{6,4},{7,5},{8,16},{9,17},{10,... | collective-permute-start | bytes 294920 | tf_op jit(solution)/shard_map/ppermute | solution.py:466
  22.1 2.6 %collective-permute-start.6 = (bf16[640,128]{1,0:T(8,128)(2,1)S(1)}, bf16[640,128]{1,0:T(8,128)(2,1)S(1)}, u32[]{:S(2)}, u32[]{:S(2)}) collective-permute-start(bf16[640,128]{1,0:T(8,128)(2,1)S(1)} %get-tuple-element.69), channel_id=1, source_target_pairs={{0,8},{1,9},{2,10},{3,11},{4,12},{5,13},{6,14},{7,15},{8,0},{9,1},... | collective-permute-start | bytes 491528 | tf_op jit(solution)/shard_map/ppermute | solution.py:466
  22.2 7.4 %collective-permute-start.5 = (bf16[640,128]{1,0:T(8,128)(2,1)S(1)}, bf16[640,128]{1,0:T(8,128)(2,1)S(1)}, u32[]{:S(2)}, u32[]{:S(2)}) collective-permute-start(bf16[640,128]{1,0:T(8,128)(2,1)S(1)} %get-tuple-element.69), channel_id=1, source_target_pairs={{0,2},{1,3},{2,0},{3,1},{4,6},{5,7},{6,4},{7,5},{8,16},{9,17},{10,... | collective-permute-start | bytes 491528 | tf_op jit(solution)/shard_map/ppermute | solution.py:466

commit v9 on v8

--- a/solution.py
+++ b/solution.py
@@ -85,7 +85,7 @@
 
 def pack_kernel(
     x_hbm, obs_hbm, index_hbm, bg_hbm, taps_hbm, out_weight_hbm, bias_hbm, own_ref, bg_rows_ref,
-    up_ref, down_ref, obs_ref, index_ref, taps_ref, out_weight_ref, bias_ref, x_ref, bg_ref,
+    first_ref, second_ref, obs_ref, index_ref, taps_ref, out_weight_ref, bias_ref, x_ref, bg_ref,
     xs, bs, sems,
 ):
     copies = [
@@ -100,10 +100,12 @@
     for copy in copies:
         copy.start()
     copies[0].wait()
+    even = lax.rem(lax.axis_index("lat"), 2) == 0
 
     def send(place, up, down):
-        up_ref[place * C : (place + 1) * C, :] = up.astype(BF16)
-        down_ref[place * C : (place + 1) * C, :] = down.astype(BF16)
+        at = slice(place * C, (place + 1) * C)
+        first_ref[at, :] = jnp.where(even, down, up).astype(BF16)
+        second_ref[at, :] = jnp.where(even, up, down).astype(BF16)
 
     xs[...] = x_ref[...].astype(F32).reshape(ROWS * C, LON)
     for row in range(4):
@@ -134,14 +136,17 @@
 
 
 def extend_kernel(
-    own_ref, above_ref, below_ref, ext_ref, near_ref, far_ref, above_edge_ref, below_edge_ref
+    own_ref, first_ref, second_ref, ext_ref, near_ref, far_ref, above_edge_ref, below_edge_ref
 ):
     strip = lax.axis_index("lat")
+    even = lax.rem(strip, 2) == 0
     zero = jnp.zeros((X_PART, LON), BF16)
-    above_edge_ref[...] = above_ref[X_PART:, :]
-    below_edge_ref[...] = below_ref[X_PART:, :]
-    above = jnp.where(strip > 0, above_ref[:X_PART, :], zero)
-    below = jnp.where(strip < lax.axis_size("lat") - 1, below_ref[:X_PART, :], zero)
+    above = jnp.where(even, second_ref[...], first_ref[...])
+    below = jnp.where(even, first_ref[...], second_ref[...])
+    above_edge_ref[...] = above[X_PART:, :]
+    below_edge_ref[...] = below[X_PART:, :]
+    above = jnp.where(strip > 0, above[:X_PART, :], zero)
+    below = jnp.where(strip < lax.axis_size("lat") - 1, below[:X_PART, :], zero)
     far_ref[: 3 * C, :] = above[C:, :]
     far_ref[3 * C :, :] = below[: 3 * C, :]
     near_ref[: 3 * C, :] = above[C:, :]
@@ -466,12 +471,14 @@
     return lax.ppermute(value, ("tm", "lat"), pairs)
 
 
-def strip_below(window, strip, last_window, last_strip):
-    return window, (strip + 1) % (last_strip + 1)
-
-
-def strip_above(window, strip, last_window, last_strip):
-    return window, (strip - 1) % (last_strip + 1)
+def near_strip(window, strip, last_window, last_strip):
+    return window, strip ^ 1
+
+
+def far_strip(window, strip, last_window, last_strip):
+    if strip in (0, last_strip):
+        return window ^ 1, strip
+    return window, ((strip + 1) ^ 1) - 1
 
 
 def near_window(window, strip, last_window, last_strip):
@@ -519,7 +526,7 @@
         )(state, conv_weight, bias, out_weight)
 
     taps = jnp.transpose(input_kernel_weight, (0, 1, 3, 2)).reshape(9 * C, HID)
-    own, ground, up, down, observed, index, taps, out_weight, bias = call(
+    own, ground, first, second, observed, index, taps, out_weight, bias = call(
         pack_kernel,
         (
             shape(ROWS * C), shape(ROWS * C), shape(PAYLOAD), shape(PAYLOAD),
@@ -546,8 +553,8 @@
             )
         )
     )
-    above = exchange(down, strip_below)
-    below = exchange(up, strip_above)
+    second = exchange(second, far_strip)
+    first = exchange(first, near_strip)
     far_own = exchange(own, far_window)
 
     sums, conv_weight, back_weight, bias, out_back = call(
@@ -563,13 +570,13 @@
     )(observed, index, taps, bias, out_weight)
     weights = (conv_weight, bias, out_weight, back_weight, out_back)
     inside = forward(INSIDE, own)
-    above, below, inside, sums = lax.optimization_barrier((above, below, inside, sums))
+    first, second, inside, sums = lax.optimization_barrier((first, second, inside, sums))
 
     ext, sent, halo, above_edge, below_edge = call(
         extend_kernel,
         (shape(16 * C), shape(14 * C), shape(6 * C), shape(2 * C), shape(2 * C)),
         [], 0, 1 << 20,
-    )(own, above, below)
+    )(own, first, second)
     far = exchange(halo, far_window)
     near = exchange(sent, near_window)
     outside = forward(OUTSIDE, ext)

time: 31.2 us -> 30.4 us (0.974)
  the two profiles are of different devices: /device:TPU:41 before, /device:TPU:43 now
where the time goes in v9:
time: 30.4 us; the launch traced here: 30.3 us
  waiting for transfers between devices  10.8 us (36%)
  starting transfers between devices  9.98 us (33%)
  Pallas kernels  9.44 us (31%)
    ppermute x7, waiting for transfers between devices, exchange(): return lax.ppermute(value, ('tm', 'lat'), pairs)  10.8 us
    ppermute x7, starting transfers between devices, exchange(): return lax.ppermute(value, ('tm', 'lat'), pairs)  9.98 us
    pallas_call x10, Pallas kernels, run(): pl.pallas_call(kernel, out_shape=outs, in_specs=[spec] * len(args), out_s...  9.44 us
  transfers between devices with their start and end apart: 7, of which 5 were waited for; matrix products, arithmetic and copies ran while one was open for 0% of the time, Pallas kernels for 18%

profile of v9, /device:TPU:43, one launch (start us, length us, event | category | flops | bytes accessed | tf_op | source)
XLA Modules:
  0.0 30.3 jit_solution(16402597013017204058)
XLA Ops:
  0.0 1.3 %shard_map.73 = (bf16[512,128]{1,0:T(8,128)(2,1)S(1)}, bf16[512,128]{1,0:T(8,128)(2,1)S(1)}, bf16[384,128]{1,0:T(8,128)(2,1)S(1)}, bf16[384,128]{1,0:T(8,128)(2,...) custom-call(bf16[64,8,128]{2,1,0:T(8,128)(2,1)} %bitcast.8, ...), custom_call_target="tpu_custom_call" | custom-call | bytes 1048576 | tf_op jit(solution)/shard_map/pallas_call | solution.py:28
  1.3 2.1 %collective-permute-start = (bf16[384,128]{1,0:T(8,128)(2,1)S(1)}, bf16[384,128]{1,0:T(8,128)(2,1)S(1)}, u32[]{:S(2)}, u32[]{:S(2)}) collective-permute-start(bf16[384,128]{1,0:T(8,128)(2,1)S(1)} %get-tuple-element.40), channel_id=1, source_target_pairs={{0,1},{1,0},{2,3},{3,2},{4,5},{5,4},{6,7},{7,6},{8,9},{9,8},{10,11... | collective-permute-start | bytes 294920 | tf_op jit(solution)/shard_map/ppermute | solution.py:471
  3.4 0.9 %collective-permute-start.1 = (bf16[384,128]{1,0:T(8,128)(2,1)S(1)}, bf16[384,128]{1,0:T(8,128)(2,1)S(1)}, u32[]{:S(2)}, u32[]{:S(2)}) collective-permute-start(bf16[384,128]{1,0:T(8,128)(2,1)S(1)} %get-tuple-element.41), channel_id=1, source_target_pairs={{0,8},{1,2},{2,1},{3,4},{4,3},{5,6},{6,5},{7,15},{8,0},{9,10},{10,... | collective-permute-start | bytes 294920 | tf_op jit(solution)/shard_map/ppermute | solution.py:471
  4.3 0.3 %shard_map.74 = (f32[8,72,128]{2,1,0:T(8,128)S(1)}, bf16[1024,192]{1,0:T(8,128)(2,1)S(1)}, bf16[192,768]{1,0:T(8,128)(2,1)S(1)}, f32[256,128]{1,0:T(8,128)S(1)}, bf16[256,64]{1,0:T(8,128)(2,1)S(1)}) custom-call(bf16[64,256]{1,0:T(8,128)(2,1)S(1)} %get-tuple-element.42.obs_ref, s32[1,256]{1,0:T(1,128)S(1)} %get-tuple-element.43.index_ref, ...), custom_call_target="tpu_custom_call" | custom-call | flops 41943040 | bytes 1048576 | tf_op jit(solution)/shard_map/pallas_call | solution.py:28
  4.7 0.9 %shard_map.75 = (bf16[1536,128]{1,0:T(8,128)(2,1)S(1)}, bf16[384,128]{1,0:T(8,128)(2,1)S(1)}) custom-call(bf16[512,128]{1,0:T(8,128)(2,1)S(1)} %get-tuple-element.39.state_ref.own_ref, bf16[1024,192]{1,0:T(8,128)(2,1)S(1)} %get-tuple-element.47.conv_ref, f32[256,128]{1,0:T(8,128)S(1)} %get-tuple-element.48.bias_ref, ...), custom_call_target="tpu_custom_call" | custom-call | flops 251658240 | bytes 2097152 | tf_op jit(solution)/shard_map/pallas_call | solution.py:28
  5.6 0.8 %collective-permute-done.first_ref = bf16[384,128]{1,0:T(8,128)(2,1)S(1)} collective-permute-done((bf16[384,128]{1,0:T(8,128)(2,1)S(1)}, bf16[384,128]{1,0:T(8,128)(2,1)S(1)}, u32[]{:S(2)}, u32[]{:S(2)}) %collective-permute-start) | collective-permute-done | bytes 98336 | tf_op jit(solution)/shard_map/ppermute | solution.py:471
  6.4 2.9 %collective-permute-done.1.second_ref = bf16[384,128]{1,0:T(8,128)(2,1)S(1)} collective-permute-done((bf16[384,128]{1,0:T(8,128)(2,1)S(1)}, bf16[384,128]{1,0:T(8,128)(2,1)S(1)}, u32[]{:S(2)}, u32[]{:S(2)}) %collective-permute-start.1) | collective-permute-done | bytes 98336 | tf_op jit(solution)/shard_map/ppermute | solution.py:471
  9.3 0.1 shard_map.76
  9.4 2.2 %collective-permute-start.4 = (bf16[896,128]{1,0:T(8,128)(2,1)S(1)}, bf16[896,128]{1,0:T(8,128)(2,1)S(1)}, u32[]{:S(2)}, u32[]{:S(2)}) collective-permute-start(bf16[896,128]{1,0:T(8,128)(2,1)S(1)} %get-tuple-element.55), channel_id=1, source_target_pairs={{0,8},{1,9},{2,10},{3,11},{4,12},{5,13},{6,14},{7,15},{8,0},{9,1},... | collective-permute-start | bytes 688136 | tf_op jit(solution)/shard_map/ppermute | solution.py:471
  11.6 2.4 %collective-permute-start.3 = (bf16[512,128]{1,0:T(8,128)(2,1)S(1)}, bf16[512,128]{1,0:T(8,128)(2,1)S(1)}, u32[]{:S(2)}, u32[]{:S(2)}) collective-permute-start(bf16[512,128]{1,0:T(8,128)(2,1)S(1)} %get-tuple-element.39.state_ref.own_ref), channel_id=1, source_target_pairs={{0,2},{1,3},{2,0},{3,1},{4,6},{5,7},{6,4},{7,5},{8,16},{9,17},{10,... | collective-permute-start | bytes 393224 | tf_op jit(solution)/shard_map/ppermute | solution.py:471
  14.0 0.2 collective-permute-start.2
  14.2 0.9 %shard_map.77 = (bf16[2048,128]{1,0:T(8,128)(2,1)S(1)}, bf16[512,128]{1,0:T(8,128)(2,1)S(1)}) custom-call(bf16[1024,128]{1,0:T(8,128)(2,1)S(1)} %get-tuple-element.56.state_ref.own_ref, bf16[1024,192]{1,0:T(8,128)(2,1)S(1)} %get-tuple-element.47.conv_ref, f32[256,128]{1,0:T(8,128)S(1)} %get-tuple-element.48.bias_ref, ...), custom_call_target="tpu_custom_call" | custom-call | flops 335544320 | bytes 2097152 | tf_op jit(solution)/shard_map/pallas_call | solution.py:28
  15.1 3.1 %collective-permute-done.3.far_own_ref = bf16[512,128]{1,0:T(8,128)(2,1)S(1)} collective-permute-done((bf16[512,128]{1,0:T(8,128)(2,1)S(1)}, bf16[512,128]{1,0:T(8,128)(2,1)S(1)}, u32[]{:S(2)}, u32[]{:S(2)}) %collective-permute-start.3) | collective-permute-done | bytes 131104 | tf_op jit(solution)/shard_map/ppermute | solution.py:471
  18.3 0.0 collective-permute-done.4.near_ref
  18.3 1.2 %shard_map.78 = (bf16[768,128]{1,0:T(8,128)(2,1)S(1)}, bf16[768,128]{1,0:T(8,128)(2,1)S(1)}) custom-call(bf16[896,128]{1,0:T(8,128)(2,1)S(1)} %collective-permute-done.4.near_ref, bf16[512,128]{1,0:T(8,128)(2,1)S(1)} %collective-permute-done.3.far_own_ref, bf16[1024,128]{1,0:T(8,128)(2,1)S(1)} %get-tuple-element.56.state_ref.own_ref, ...), custom_call_target="tpu_custom_call" | custom-call | flops 503316480 | bytes 2097152 | tf_op jit(solution)/shard_map/pallas_call | solution.py:28
  19.5 0.8 %collective-permute-done.2.far_ref = bf16[384,128]{1,0:T(8,128)(2,1)S(1)} collective-permute-done((bf16[384,128]{1,0:T(8,128)(2,1)S(1)}, bf16[384,128]{1,0:T(8,128)(2,1)S(1)}, u32[]{:S(2)}, u32[]{:S(2)}) %collective-permute-start.2) | collective-permute-done | bytes 98336 | tf_op jit(solution)/shard_map/ppermute | solution.py:471
  20.2 1.1 %shard_map.79 = (bf16[768,128]{1,0:T(8,128)(2,1)S(1)}, bf16[640,128]{1,0:T(8,128)(2,1)S(1)}) custom-call(bf16[384,128]{1,0:T(8,128)(2,1)S(1)} %collective-permute-done.2.far_ref, bf16[512,128]{1,0:T(8,128)(2,1)S(1)} %collective-permute-done.3.far_own_ref, bf16[768,128]{1,0:T(8,128)(2,1)S(1)} %get-tuple-element.63.part_ref, ...), custom_call_target="tpu_custom_call" | custom-call | flops 503316480 | bytes 2097152 | tf_op jit(solution)/shard_map/pallas_call | solution.py:28
  21.3 0.1 collective-permute-start.6
  21.4 2.0 %collective-permute-start.5 = (bf16[640,128]{1,0:T(8,128)(2,1)S(1)}, bf16[640,128]{1,0:T(8,128)(2,1)S(1)}, u32[]{:S(2)}, u32[]{:S(2)}) collective-permute-start(bf16[640,128]{1,0:T(8,128)(2,1)S(1)} %get-tuple-element.69), channel_id=1, source_target_pairs={{0,2},{1,3},{2,0},{3,1},{4,6},{5,7},{6,4},{7,5},{8,16},{9,17},{10,... | collective-permute-start | bytes 491528 | tf_op jit(solution)/shard_map/ppermute | solution.py:471
  23.4 1.2 %shard_map.80 = (bf16[2560,128]{1,0:T(8,128)(2,1)S(1)}, bf16[640,128]{1,0:T(8,128)(2,1)S(1)}) custom-call(bf16[768,128]{1,0:T(8,128)(2,1)S(1)} %get-tuple-element.70.state_ref.own_ref, bf16[1024,192]{1,0:T(8,128)(2,1)S(1)} %get-tuple-element.47.conv_ref, f32[256,128]{1,0:T(8,128)S(1)} %get-tuple-element.48.bias_ref, ...), custom_call_target="tpu_custom_call" | custom-call | flops 419430400 | bytes 2097152 | tf_op jit(solution)/shard_map/pallas_call | solution.py:28
  24.6 0.0 collective-permute-done.6.near_ref
  24.7 0.9 %shard_map.81.part_ref = bf16[512,128]{1,0:T(8,128)(2,1)S(1)} custom-call(bf16[640,128]{1,0:T(8,128)(2,1)S(1)} %collective-permute-done.6.near_ref, bf16[768,128]{1,0:T(8,128)(2,1)S(1)} %get-tuple-element.70.state_ref.own_ref, bf16[2560,128]{1,0:T(8,128)(2,1)S(1)} %get-tuple-element.71.active_ref, bf16[640,128]{1,0:T(8,128)(2,1)S(1)} %get-tuple-element.72.forecast_ref, ...), custom_call_target="tpu_custom_call" | custom-call | flops 335544320 | bytes 2097152 | tf_op jit(solution)/shard_map/pallas_call | solution.py:28
  25.6 3.2 %collective-permute-done.5.far_ref = bf16[640,128]{1,0:T(8,128)(2,1)S(1)} collective-permute-done((bf16[640,128]{1,0:T(8,128)(2,1)S(1)}, bf16[640,128]{1,0:T(8,128)(2,1)S(1)}, u32[]{:S(2)}, u32[]{:S(2)}) %collective-permute-start.5) | collective-permute-done | bytes 163872 | tf_op jit(solution)/shard_map/ppermute | solution.py:471
  28.8 1.5 %shard_map.82 = bf16[64,8,128]{2,1,0:T(8,128)(2,1)} custom-call(bf16[640,128]{1,0:T(8,128)(2,1)S(1)} %collective-permute-done.5.far_ref, bf16[512,128]{1,0:T(8,128)(2,1)S(1)} %shard_map.81.part_ref, bf16[768,128]{1,0:T(8,128)(2,1)S(1)} %get-tuple-element.70.state_ref.own_ref, bf16[512,128]{1,0:T(8,128)(2,1)S(1)} %get-tuple-element.65.bg_ref, ...), custom_call_target="tpu_custom_call" | custom-call | flops 335544320 | bytes 2097152 | tf_op jit(solution)/shard_map/pallas_call | solution.py:28
Async XLA Ops:
  1.3 5.1 %collective-permute-start = (bf16[384,128]{1,0:T(8,128)(2,1)S(1)}, bf16[384,128]{1,0:T(8,128)(2,1)S(1)}, u32[]{:S(2)}, u32[]{:S(2)}) collective-permute-start(bf16[384,128]{1,0:T(8,128)(2,1)S(1)} %get-tuple-element.40), channel_id=1, source_target_pairs={{0,1},{1,0},{2,3},{3,2},{4,5},{5,4},{6,7},{7,6},{8,9},{9,8},{10,11... | collective-permute-start | bytes 294920 | tf_op jit(solution)/shard_map/ppermute | solution.py:471
  3.4 5.9 %collective-permute-start.1 = (bf16[384,128]{1,0:T(8,128)(2,1)S(1)}, bf16[384,128]{1,0:T(8,128)(2,1)S(1)}, u32[]{:S(2)}, u32[]{:S(2)}) collective-permute-start(bf16[384,128]{1,0:T(8,128)(2,1)S(1)} %get-tuple-element.41), channel_id=1, source_target_pairs={{0,8},{1,2},{2,1},{3,4},{4,3},{5,6},{6,5},{7,15},{8,0},{9,10},{10,... | collective-permute-start | bytes 294920 | tf_op jit(solution)/shard_map/ppermute | solution.py:471
  9.4 8.9 %collective-permute-start.4 = (bf16[896,128]{1,0:T(8,128)(2,1)S(1)}, bf16[896,128]{1,0:T(8,128)(2,1)S(1)}, u32[]{:S(2)}, u32[]{:S(2)}) collective-permute-start(bf16[896,128]{1,0:T(8,128)(2,1)S(1)} %get-tuple-element.55), channel_id=1, source_target_pairs={{0,8},{1,9},{2,10},{3,11},{4,12},{5,13},{6,14},{7,15},{8,0},{9,1},... | collective-permute-start | bytes 688136 | tf_op jit(solution)/shard_map/ppermute | solution.py:471
  11.6 6.7 %collective-permute-start.3 = (bf16[512,128]{1,0:T(8,128)(2,1)S(1)}, bf16[512,128]{1,0:T(8,128)(2,1)S(1)}, u32[]{:S(2)}, u32[]{:S(2)}) collective-permute-start(bf16[512,128]{1,0:T(8,128)(2,1)S(1)} %get-tuple-element.39.state_ref.own_ref), channel_id=1, source_target_pairs={{0,2},{1,3},{2,0},{3,1},{4,6},{5,7},{6,4},{7,5},{8,16},{9,17},{10,... | collective-permute-start | bytes 393224 | tf_op jit(solution)/shard_map/ppermute | solution.py:471
  14.0 6.3 %collective-permute-start.2 = (bf16[384,128]{1,0:T(8,128)(2,1)S(1)}, bf16[384,128]{1,0:T(8,128)(2,1)S(1)}, u32[]{:S(2)}, u32[]{:S(2)}) collective-permute-start(bf16[384,128]{1,0:T(8,128)(2,1)S(1)} %get-tuple-element.54), channel_id=1, source_target_pairs={{0,2},{1,3},{2,0},{3,1},{4,6},{5,7},{6,4},{7,5},{8,16},{9,17},{10,... | collective-permute-start | bytes 294920 | tf_op jit(solution)/shard_map/ppermute | solution.py:471
  21.3 3.3 %collective-permute-start.6 = (bf16[640,128]{1,0:T(8,128)(2,1)S(1)}, bf16[640,128]{1,0:T(8,128)(2,1)S(1)}, u32[]{:S(2)}, u32[]{:S(2)}) collective-permute-start(bf16[640,128]{1,0:T(8,128)(2,1)S(1)} %get-tuple-element.69), channel_id=1, source_target_pairs={{0,8},{1,9},{2,10},{3,11},{4,12},{5,13},{6,14},{7,15},{8,0},{9,1},... | collective-permute-start | bytes 491528 | tf_op jit(solution)/shard_map/ppermute | solution.py:471
  21.4 7.4 %collective-permute-start.5 = (bf16[640,128]{1,0:T(8,128)(2,1)S(1)}, bf16[640,128]{1,0:T(8,128)(2,1)S(1)}, u32[]{:S(2)}, u32[]{:S(2)}) collective-permute-start(bf16[640,128]{1,0:T(8,128)(2,1)S(1)} %get-tuple-element.69), channel_id=1, source_target_pairs={{0,2},{1,3},{2,0},{3,1},{4,6},{5,7},{6,4},{7,5},{8,16},{9,17},{10,... | collective-permute-start | bytes 491528 | tf_op jit(solution)/shard_map/ppermute | solution.py:471

commit v10 on v9

--- a/solution.py
+++ b/solution.py
@@ -84,9 +84,8 @@
 
 
 def pack_kernel(
-    x_hbm, obs_hbm, index_hbm, bg_hbm, taps_hbm, out_weight_hbm, bias_hbm, own_ref, bg_rows_ref,
-    first_ref, second_ref, obs_ref, index_ref, taps_ref, out_weight_ref, bias_ref, x_ref, bg_ref,
-    xs, bs, sems,
+    x_hbm, obs_hbm, index_hbm, bg_hbm, taps_hbm, out_weight_hbm, bias_hbm, first_ref, second_ref,
+    x_ref, bg_ref, obs_ref, index_ref, taps_ref, out_weight_ref, bias_ref, xs, bs, sems,
 ):
     copies = [
         pltpu.make_async_copy(source, target, sems.at[place])
@@ -99,7 +98,11 @@
     ]
     for copy in copies:
         copy.start()
-    copies[0].wait()
+    copies[1].wait()
+    copies[2].wait()
+    low, high = local_cells(index_ref[...])
+    values = with_ones(obs_ref[...])
+    sums = {row: observation_sums(values, low, high, row) for row in (0, 1, 6, 7)}
     even = lax.rem(lax.axis_index("lat"), 2) == 0
 
     def send(place, up, down):
@@ -107,36 +110,27 @@
         first_ref[at, :] = jnp.where(even, down, up).astype(BF16)
         second_ref[at, :] = jnp.where(even, up, down).astype(BF16)
 
+    copies[0].wait()
     xs[...] = x_ref[...].astype(F32).reshape(ROWS * C, LON)
     for row in range(4):
-        up, down = xs[latitude(row), :], xs[latitude(row + 4), :]
-        own_ref[row * C : (row + 1) * C, :] = up.astype(BF16)
-        own_ref[(row + 4) * C : (row + 5) * C, :] = down.astype(BF16)
-        send(row, up, down)
-    copies[1].wait()
-    copies[2].wait()
-    low, high = local_cells(index_ref[...])
-    values = with_ones(obs_ref[...])
+        send(row, xs[latitude(row), :], xs[latitude(row + 4), :])
     copies[3].wait()
     bs[...] = bg_ref[...].astype(F32).reshape(ROWS * C, LON)
     opening = lax.axis_index("tm") == 0
 
     def edge(row):
         own = xs[latitude(row), :]
-        ground = bs[latitude(row), :]
-        value = innovation_of(observation_sums(values, low, high, row), own)
-        return value + jnp.where(opening, own - ground, 0.0)
+        value = innovation_of(sums[row], own)
+        return value + jnp.where(opening, own - bs[latitude(row), :], 0.0)
 
     for row in range(2):
         send(4 + row, edge(row), edge(row + 6))
-    for row in range(ROWS):
-        bg_rows_ref[row * C : (row + 1) * C, :] = bs[latitude(row), :].astype(BF16)
     for copy in copies[4:]:
         copy.wait()
 
 
 def extend_kernel(
-    own_ref, first_ref, second_ref, ext_ref, near_ref, far_ref, above_edge_ref, below_edge_ref
+    own_ref, first_ref, second_ref, ext_ref, halo_ref, above_edge_ref, below_edge_ref
 ):
     strip = lax.axis_index("lat")
     even = lax.rem(strip, 2) == 0
@@ -147,11 +141,8 @@
     below_edge_ref[...] = below[X_PART:, :]
     above = jnp.where(strip > 0, above[:X_PART, :], zero)
     below = jnp.where(strip < lax.axis_size("lat") - 1, below[:X_PART, :], zero)
-    far_ref[: 3 * C, :] = above[C:, :]
-    far_ref[3 * C :, :] = below[: 3 * C, :]
-    near_ref[: 3 * C, :] = above[C:, :]
-    near_ref[3 * C : 11 * C, :] = own_ref[...]
-    near_ref[11 * C :, :] = below[: 3 * C, :]
+    halo_ref[: 3 * C, :] = above[C:, :]
+    halo_ref[3 * C :, :] = below[: 3 * C, :]
     ext_ref[:X_PART, :] = above
     ext_ref[X_PART : X_PART + ROWS * C, :] = own_ref[...]
     ext_ref[X_PART + ROWS * C :, :] = below
@@ -215,9 +206,14 @@
 
 
 def prepare_kernel(
-    obs_ref, index_ref, kernel_ref, bias_ref, out_weight_ref, sums_ref, conv_ref, back_ref,
-    wide_bias_ref, out_back_ref,
-):
+    x_ref, bg_ref, obs_ref, index_ref, kernel_ref, bias_ref, out_weight_ref, own_ref, bg_rows_ref,
+    sums_ref, conv_ref, back_ref, wide_bias_ref, out_back_ref, xs, bs,
+):
+    xs[...] = x_ref[...].astype(F32).reshape(ROWS * C, LON)
+    bs[...] = bg_ref[...].astype(F32).reshape(ROWS * C, LON)
+    for row in range(ROWS):
+        own_ref[row * C : (row + 1) * C, :] = xs[latitude(row), :].astype(BF16)
+        bg_rows_ref[row * C : (row + 1) * C, :] = bs[latitude(row), :].astype(BF16)
     low, high = local_cells(index_ref[...])
     values = with_ones(obs_ref[...])
     for row in range(ROWS):
@@ -304,7 +300,7 @@
 
 
 def first_near_kernel(
-    near_ref, far_own_ref, own_ref, active_in_ref, forecast_in_ref, active_out_ref, forecast_out_ref,
+    near_ref, near_own_ref, far_own_ref, own_ref, active_in_ref, forecast_in_ref, active_out_ref, forecast_out_ref,
     conv_ref, bias_ref, out_weight_ref, back_ref, out_back_ref, part_ref, inner_ref, mixed,
     cot, target,
 ):
@@ -315,11 +311,12 @@
         return take
 
     even, _, odd = branches()
+    near = rows_in(near_ref, 0, 3) + rows_in(near_own_ref, 0, ROWS) + rows_in(near_ref, 3, 3)
 
     @pl.when(jnp.logical_not(odd))
     def _():
         adjoint_part(
-            12, 2, rows_in(near_ref, 0, 14), split_rows(active_out_ref, active_in_ref),
+            12, 2, near, split_rows(active_out_ref, active_in_ref),
             split_rows(forecast_out_ref, forecast_in_ref), back_ref, out_back_ref, cot, target,
             put(part_ref),
         )
@@ -335,7 +332,7 @@
     @pl.when(odd)
     def _():
         residual_part(
-            TWELVE, rows_in(near_ref, 0, 14), own_ref, conv_ref, bias_ref, out_weight_ref,
+            TWELVE, near, own_ref, conv_ref, bias_ref, out_weight_ref,
             mixed, put(part_ref),
         )
 
@@ -526,10 +523,12 @@
         )(state, conv_weight, bias, out_weight)
 
     taps = jnp.transpose(input_kernel_weight, (0, 1, 3, 2)).reshape(9 * C, HID)
-    own, ground, first, second, observed, index, taps, out_weight, bias = call(
+    first, second, x, ground, observed, index, taps, out_weight, bias = call(
         pack_kernel,
         (
-            shape(ROWS * C), shape(ROWS * C), shape(PAYLOAD), shape(PAYLOAD),
+            shape(PAYLOAD), shape(PAYLOAD),
+            jax.ShapeDtypeStruct((C, ROWS, LON), BF16),
+            jax.ShapeDtypeStruct((C, ROWS, LON), BF16),
             jax.ShapeDtypeStruct((C, OBS), BF16),
             jax.ShapeDtypeStruct((1, OBS), jnp.int32),
             jax.ShapeDtypeStruct((9 * C, HID), BF16),
@@ -537,8 +536,6 @@
             jax.ShapeDtypeStruct((1, HID), F32),
         ),
         [
-            pltpu.VMEM((C, ROWS, LON), BF16),
-            pltpu.VMEM((C, ROWS, LON), BF16),
             pltpu.VMEM((C * ROWS, LON), F32),
             pltpu.VMEM((C * ROWS, LON), F32),
             pltpu.SemaphoreType.DMA((7,)),
@@ -555,35 +552,37 @@
     )
     second = exchange(second, far_strip)
     first = exchange(first, near_strip)
-    far_own = exchange(own, far_window)
-
-    sums, conv_weight, back_weight, bias, out_back = call(
+    own, ground, sums, conv_weight, back_weight, bias, out_back = call(
         prepare_kernel,
         (
+            shape(ROWS * C), shape(ROWS * C),
             jax.ShapeDtypeStruct((ROWS, 72, LON), F32),
             jax.ShapeDtypeStruct((4 * HID, 3 * C), BF16),
             jax.ShapeDtypeStruct((3 * C, 3 * HID), BF16),
             jax.ShapeDtypeStruct((HID, LON), F32),
             jax.ShapeDtypeStruct((HID, C), BF16),
         ),
-        [], ROWS * 2 * 80 * OBS * LON, 1 << 20,
-    )(observed, index, taps, bias, out_weight)
+        [pltpu.VMEM((C * ROWS, LON), F32), pltpu.VMEM((C * ROWS, LON), F32)],
+        ROWS * 2 * 80 * OBS * LON, 1 << 20,
+    )(x, ground, observed, index, taps, bias, out_weight)
+    far_own = exchange(own, far_window)
+    near_own = exchange(own, near_window)
     weights = (conv_weight, bias, out_weight, back_weight, out_back)
     inside = forward(INSIDE, own)
     first, second, inside, sums = lax.optimization_barrier((first, second, inside, sums))
 
-    ext, sent, halo, above_edge, below_edge = call(
+    ext, halo, above_edge, below_edge = call(
         extend_kernel,
-        (shape(16 * C), shape(14 * C), shape(6 * C), shape(2 * C), shape(2 * C)),
+        (shape(16 * C), shape(6 * C), shape(2 * C), shape(2 * C)),
         [], 0, 1 << 20,
     )(own, first, second)
     far = exchange(halo, far_window)
-    near = exchange(sent, near_window)
+    near = exchange(halo, near_window)
     outside = forward(OUTSIDE, ext)
     part, inner = call(
         first_near_kernel, (shape(12 * C), shape(12 * C)), gradient_scratch(12),
         row_flops(12), 2 << 20,
-    )(near, far_own, ext, *inside, *outside, *weights)
+    )(near, near_own, far_own, ext, *inside, *outside, *weights)
     state, sent = call(
         first_kernel, (shape(12 * C), shape(10 * C)), gradient_scratch(12), row_flops(12),
         2 << 20,

time: 30.4 us -> 27.6 us (0.908)
  the two profiles are of different devices: /device:TPU:43 before, /device:TPU:47 now
where the time goes in v10:
time: 27.6 us; the launch traced here: 27.4 us
  starting transfers between devices  12.6 us (46%)
  Pallas kernels  9.46 us (34%)
  waiting for transfers between devices  5.33 us (19%)
    ppermute x8, starting transfers between devices, exchange(): return lax.ppermute(value, ('tm', 'lat'), pairs)  12.6 us
    pallas_call x10, Pallas kernels, run(): pl.pallas_call(kernel, out_shape=outs, in_specs=[spec] * len(args), out_s...  9.46 us
    ppermute x8, waiting for transfers between devices, exchange(): return lax.ppermute(value, ('tm', 'lat'), pairs)  5.33 us
  transfers between devices with their start and end apart: 8, of which 3 were waited for; matrix products, arithmetic and copies ran while one was open for 0% of the time, Pallas kernels for 21%

profile of v10, /device:TPU:47, one launch (start us, length us, event | category | flops | bytes accessed | tf_op | source)
XLA Modules:
  0.0 27.4 jit_solution(8912731307540859568)
XLA Ops:
  0.0 1.2 %shard_map.73 = (bf16[384,128]{1,0:T(8,128)(2,1)S(1)}, bf16[384,128]{1,0:T(8,128)(2,1)S(1)}, bf16[64,8,128]{2,1,0:T(8,128)(2,1)S(1)}, bf16[64,8,128]{2,1,0:T(8,1...) custom-call(bf16[64,8,128]{2,1,0:T(8,128)(2,1)} %bitcast.8, ...), custom_call_target="tpu_custom_call" | custom-call | bytes 1048576 | tf_op jit(solution)/shard_map/pallas_call | solution.py:28
  1.3 2.1 %collective-permute-start = (bf16[384,128]{1,0:T(8,128)(2,1)S(1)}, bf16[384,128]{1,0:T(8,128)(2,1)S(1)}, u32[]{:S(2)}, u32[]{:S(2)}) collective-permute-start(bf16[384,128]{1,0:T(8,128)(2,1)S(1)} %get-tuple-element.48), channel_id=1, source_target_pairs={{0,1},{1,0},{2,3},{3,2},{4,5},{5,4},{6,7},{7,6},{8,9},{9,8},{10,11... | collective-permute-start | bytes 294920 | tf_op jit(solution)/shard_map/ppermute | solution.py:468
  3.3 1.2 %collective-permute-start.1 = (bf16[384,128]{1,0:T(8,128)(2,1)S(1)}, bf16[384,128]{1,0:T(8,128)(2,1)S(1)}, u32[]{:S(2)}, u32[]{:S(2)}) collective-permute-start(bf16[384,128]{1,0:T(8,128)(2,1)S(1)} %get-tuple-element.49), channel_id=1, source_target_pairs={{0,8},{1,2},{2,1},{3,4},{4,3},{5,6},{6,5},{7,15},{8,0},{9,10},{10,... | collective-permute-start | bytes 294920 | tf_op jit(solution)/shard_map/ppermute | solution.py:468
  4.6 0.4 %shard_map.74 = (bf16[512,128]{1,0:T(8,128)(2,1)S(1)}, bf16[512,128]{1,0:T(8,128)(2,1)S(1)}, f32[8,72,128]{2,1,0:T(8,128)S(1)}, bf16[1024,192]{1,0:T(8,128)(2,1)...) custom-call(bf16[64,8,128]{2,1,0:T(8,128)(2,1)S(1)} %get-tuple-element.40.x_ref, ...), custom_call_target="tpu_custom_call" | custom-call | flops 41943040 | bytes 1048576 | tf_op jit(solution)/shard_map/pallas_call | solution.py:28
  5.0 1.3 %collective-permute-start.5 = (bf16[512,128]{1,0:T(8,128)(2,1)S(1)}, bf16[512,128]{1,0:T(8,128)(2,1)S(1)}, u32[]{:S(2)}, u32[]{:S(2)}) collective-permute-start(bf16[512,128]{1,0:T(8,128)(2,1)S(1)} %get-tuple-element.47.state_ref.own_ref), channel_id=1, source_target_pairs={{0,8},{1,9},{2,10},{3,11},{4,12},{5,13},{6,14},{7,15},{8,0},{9,1},... | collective-permute-start | bytes 393224 | tf_op jit(solution)/shard_map/ppermute | solution.py:468
  6.3 1.5 %collective-permute-start.3 = (bf16[512,128]{1,0:T(8,128)(2,1)S(1)}, bf16[512,128]{1,0:T(8,128)(2,1)S(1)}, u32[]{:S(2)}, u32[]{:S(2)}) collective-permute-start(bf16[512,128]{1,0:T(8,128)(2,1)S(1)} %get-tuple-element.47.state_ref.own_ref), channel_id=1, source_target_pairs={{0,2},{1,3},{2,0},{3,1},{4,6},{5,7},{6,4},{7,5},{8,16},{9,17},{10,... | collective-permute-start | bytes 393224 | tf_op jit(solution)/shard_map/ppermute | solution.py:468
  7.8 0.9 %shard_map.75 = (bf16[1536,128]{1,0:T(8,128)(2,1)S(1)}, bf16[384,128]{1,0:T(8,128)(2,1)S(1)}) custom-call(bf16[512,128]{1,0:T(8,128)(2,1)S(1)} %get-tuple-element.47.state_ref.own_ref, bf16[1024,192]{1,0:T(8,128)(2,1)S(1)} %get-tuple-element.50.conv_ref, f32[256,128]{1,0:T(8,128)S(1)} %get-tuple-element.51.bias_ref, ...), custom_call_target="tpu_custom_call" | custom-call | flops 251658240 | bytes 2097152 | tf_op jit(solution)/shard_map/pallas_call | solution.py:28
  8.7 0.0 collective-permute-done.first_ref
  8.7 0.6 %collective-permute-done.1.second_ref = bf16[384,128]{1,0:T(8,128)(2,1)S(1)} collective-permute-done((bf16[384,128]{1,0:T(8,128)(2,1)S(1)}, bf16[384,128]{1,0:T(8,128)(2,1)S(1)}, u32[]{:S(2)}, u32[]{:S(2)}) %collective-permute-start.1) | collective-permute-done | bytes 98336 | tf_op jit(solution)/shard_map/ppermute | solution.py:468
  9.3 0.1 shard_map.76
  9.4 2.1 %collective-permute-start.4 = (bf16[384,128]{1,0:T(8,128)(2,1)S(1)}, bf16[384,128]{1,0:T(8,128)(2,1)S(1)}, u32[]{:S(2)}, u32[]{:S(2)}) collective-permute-start(bf16[384,128]{1,0:T(8,128)(2,1)S(1)} %get-tuple-element.57), channel_id=1, source_target_pairs={{0,8},{1,9},{2,10},{3,11},{4,12},{5,13},{6,14},{7,15},{8,0},{9,1},... | collective-permute-start | bytes 294920 | tf_op jit(solution)/shard_map/ppermute | solution.py:468
  11.5 2.4 %collective-permute-start.2 = (bf16[384,128]{1,0:T(8,128)(2,1)S(1)}, bf16[384,128]{1,0:T(8,128)(2,1)S(1)}, u32[]{:S(2)}, u32[]{:S(2)}) collective-permute-start(bf16[384,128]{1,0:T(8,128)(2,1)S(1)} %get-tuple-element.57), channel_id=1, source_target_pairs={{0,2},{1,3},{2,0},{3,1},{4,6},{5,7},{6,4},{7,5},{8,16},{9,17},{10,... | collective-permute-start | bytes 294920 | tf_op jit(solution)/shard_map/ppermute | solution.py:468
  13.9 0.9 %shard_map.77 = (bf16[2048,128]{1,0:T(8,128)(2,1)S(1)}, bf16[512,128]{1,0:T(8,128)(2,1)S(1)}) custom-call(bf16[1024,128]{1,0:T(8,128)(2,1)S(1)} %get-tuple-element.58.state_ref.own_ref, bf16[1024,192]{1,0:T(8,128)(2,1)S(1)} %get-tuple-element.50.conv_ref, f32[256,128]{1,0:T(8,128)S(1)} %get-tuple-element.51.bias_ref, ...), custom_call_target="tpu_custom_call" | custom-call | flops 335544320 | bytes 2097152 | tf_op jit(solution)/shard_map/pallas_call | solution.py:28
  14.8 0.0 collective-permute-done.5.near_own_ref
  14.8 0.0 collective-permute-done.3.far_own_ref
  14.8 0.0 collective-permute-done.4.near_ref
  14.8 1.2 %shard_map.78 = (bf16[768,128]{1,0:T(8,128)(2,1)S(1)}, bf16[768,128]{1,0:T(8,128)(2,1)S(1)}) custom-call(bf16[384,128]{1,0:T(8,128)(2,1)S(1)} %collective-permute-done.4.near_ref, bf16[512,128]{1,0:T(8,128)(2,1)S(1)} %collective-permute-done.5.near_own_ref, bf16[512,128]{1,0:T(8,128)(2,1)S(1)} %collective-permute-done.3.far_own_ref, ...), custom_call_target="tpu_custom_call" | custom-call | flops 503316480 | bytes 2097152 | tf_op jit(solution)/shard_map/pallas_call | solution.py:28
  16.0 1.3 %collective-permute-done.2.far_ref = bf16[384,128]{1,0:T(8,128)(2,1)S(1)} collective-permute-done((bf16[384,128]{1,0:T(8,128)(2,1)S(1)}, bf16[384,128]{1,0:T(8,128)(2,1)S(1)}, u32[]{:S(2)}, u32[]{:S(2)}) %collective-permute-start.2) | collective-permute-done | bytes 98336 | tf_op jit(solution)/shard_map/ppermute | solution.py:468
  17.3 1.1 %shard_map.79 = (bf16[768,128]{1,0:T(8,128)(2,1)S(1)}, bf16[640,128]{1,0:T(8,128)(2,1)S(1)}) custom-call(bf16[384,128]{1,0:T(8,128)(2,1)S(1)} %collective-permute-done.2.far_ref, bf16[512,128]{1,0:T(8,128)(2,1)S(1)} %collective-permute-done.3.far_own_ref, bf16[768,128]{1,0:T(8,128)(2,1)S(1)} %get-tuple-element.65.part_ref, ...), custom_call_target="tpu_custom_call" | custom-call | flops 503316480 | bytes 2097152 | tf_op jit(solution)/shard_map/pallas_call | solution.py:28
  18.4 0.1 collective-permute-start.7
  18.5 1.9 %collective-permute-start.6 = (bf16[640,128]{1,0:T(8,128)(2,1)S(1)}, bf16[640,128]{1,0:T(8,128)(2,1)S(1)}, u32[]{:S(2)}, u32[]{:S(2)}) collective-permute-start(bf16[640,128]{1,0:T(8,128)(2,1)S(1)} %get-tuple-element.71), channel_id=1, source_target_pairs={{0,2},{1,3},{2,0},{3,1},{4,6},{5,7},{6,4},{7,5},{8,16},{9,17},{10,... | collective-permute-start | bytes 491528 | tf_op jit(solution)/shard_map/ppermute | solution.py:468
  20.4 1.2 %shard_map.80 = (bf16[2560,128]{1,0:T(8,128)(2,1)S(1)}, bf16[640,128]{1,0:T(8,128)(2,1)S(1)}) custom-call(bf16[768,128]{1,0:T(8,128)(2,1)S(1)} %get-tuple-element.72.state_ref.own_ref, bf16[1024,192]{1,0:T(8,128)(2,1)S(1)} %get-tuple-element.50.conv_ref, f32[256,128]{1,0:T(8,128)S(1)} %get-tuple-element.51.bias_ref, ...), custom_call_target="tpu_custom_call" | custom-call | flops 419430400 | bytes 2097152 | tf_op jit(solution)/shard_map/pallas_call | solution.py:28
  21.6 0.0 collective-permute-done.7.near_ref
  21.6 0.9 %shard_map.81.part_ref = bf16[512,128]{1,0:T(8,128)(2,1)S(1)} custom-call(bf16[640,128]{1,0:T(8,128)(2,1)S(1)} %collective-permute-done.7.near_ref, bf16[768,128]{1,0:T(8,128)(2,1)S(1)} %get-tuple-element.72.state_ref.own_ref, bf16[2560,128]{1,0:T(8,128)(2,1)S(1)} %get-tuple-element.73.active_ref, bf16[640,128]{1,0:T(8,128)(2,1)S(1)} %get-tuple-element.74.forecast_ref, ...), custom_call_target="tpu_custom_call" | custom-call | flops 335544320 | bytes 2097152 | tf_op jit(solution)/shard_map/pallas_call | solution.py:28
  22.5 3.4 %collective-permute-done.6.far_ref = bf16[640,128]{1,0:T(8,128)(2,1)S(1)} collective-permute-done((bf16[640,128]{1,0:T(8,128)(2,1)S(1)}, bf16[640,128]{1,0:T(8,128)(2,1)S(1)}, u32[]{:S(2)}, u32[]{:S(2)}) %collective-permute-start.6) | collective-permute-done | bytes 163872 | tf_op jit(solution)/shard_map/ppermute | solution.py:468
  25.9 1.5 %shard_map.82 = bf16[64,8,128]{2,1,0:T(8,128)(2,1)} custom-call(bf16[640,128]{1,0:T(8,128)(2,1)S(1)} %collective-permute-done.6.far_ref, bf16[512,128]{1,0:T(8,128)(2,1)S(1)} %shard_map.81.part_ref, bf16[768,128]{1,0:T(8,128)(2,1)S(1)} %get-tuple-element.72.state_ref.own_ref, bf16[512,128]{1,0:T(8,128)(2,1)S(1)} %get-tuple-element.67.bg_ref, ...), custom_call_target="tpu_custom_call" | custom-call | flops 335544320 | bytes 2097152 | tf_op jit(solution)/shard_map/pallas_call | solution.py:28
Async XLA Ops:
  1.3 7.5 %collective-permute-start = (bf16[384,128]{1,0:T(8,128)(2,1)S(1)}, bf16[384,128]{1,0:T(8,128)(2,1)S(1)}, u32[]{:S(2)}, u32[]{:S(2)}) collective-permute-start(bf16[384,128]{1,0:T(8,128)(2,1)S(1)} %get-tuple-element.48), channel_id=1, source_target_pairs={{0,1},{1,0},{2,3},{3,2},{4,5},{5,4},{6,7},{7,6},{8,9},{9,8},{10,11... | collective-permute-start | bytes 294920 | tf_op jit(solution)/shard_map/ppermute | solution.py:468
  3.3 6.0 %collective-permute-start.1 = (bf16[384,128]{1,0:T(8,128)(2,1)S(1)}, bf16[384,128]{1,0:T(8,128)(2,1)S(1)}, u32[]{:S(2)}, u32[]{:S(2)}) collective-permute-start(bf16[384,128]{1,0:T(8,128)(2,1)S(1)} %get-tuple-element.49), channel_id=1, source_target_pairs={{0,8},{1,2},{2,1},{3,4},{4,3},{5,6},{6,5},{7,15},{8,0},{9,10},{10,... | collective-permute-start | bytes 294920 | tf_op jit(solution)/shard_map/ppermute | solution.py:468
  5.0 9.8 %collective-permute-start.5 = (bf16[512,128]{1,0:T(8,128)(2,1)S(1)}, bf16[512,128]{1,0:T(8,128)(2,1)S(1)}, u32[]{:S(2)}, u32[]{:S(2)}) collective-permute-start(bf16[512,128]{1,0:T(8,128)(2,1)S(1)} %get-tuple-element.47.state_ref.own_ref), channel_id=1, source_target_pairs={{0,8},{1,9},{2,10},{3,11},{4,12},{5,13},{6,14},{7,15},{8,0},{9,1},... | collective-permute-start | bytes 393224 | tf_op jit(solution)/shard_map/ppermute | solution.py:468
  6.3 8.5 %collective-permute-start.3 = (bf16[512,128]{1,0:T(8,128)(2,1)S(1)}, bf16[512,128]{1,0:T(8,128)(2,1)S(1)}, u32[]{:S(2)}, u32[]{:S(2)}) collective-permute-start(bf16[512,128]{1,0:T(8,128)(2,1)S(1)} %get-tuple-element.47.state_ref.own_ref), channel_id=1, source_target_pairs={{0,2},{1,3},{2,0},{3,1},{4,6},{5,7},{6,4},{7,5},{8,16},{9,17},{10,... | collective-permute-start | bytes 393224 | tf_op jit(solution)/shard_map/ppermute | solution.py:468
  9.4 5.4 %collective-permute-start.4 = (bf16[384,128]{1,0:T(8,128)(2,1)S(1)}, bf16[384,128]{1,0:T(8,128)(2,1)S(1)}, u32[]{:S(2)}, u32[]{:S(2)}) collective-permute-start(bf16[384,128]{1,0:T(8,128)(2,1)S(1)} %get-tuple-element.57), channel_id=1, source_target_pairs={{0,8},{1,9},{2,10},{3,11},{4,12},{5,13},{6,14},{7,15},{8,0},{9,1},... | collective-permute-start | bytes 294920 | tf_op jit(solution)/shard_map/ppermute | solution.py:468
  11.5 5.9 %collective-permute-start.2 = (bf16[384,128]{1,0:T(8,128)(2,1)S(1)}, bf16[384,128]{1,0:T(8,128)(2,1)S(1)}, u32[]{:S(2)}, u32[]{:S(2)}) collective-permute-start(bf16[384,128]{1,0:T(8,128)(2,1)S(1)} %get-tuple-element.57), channel_id=1, source_target_pairs={{0,2},{1,3},{2,0},{3,1},{4,6},{5,7},{6,4},{7,5},{8,16},{9,17},{10,... | collective-permute-start | bytes 294920 | tf_op jit(solution)/shard_map/ppermute | solution.py:468
  18.4 3.2 %collective-permute-start.7 = (bf16[640,128]{1,0:T(8,128)(2,1)S(1)}, bf16[640,128]{1,0:T(8,128)(2,1)S(1)}, u32[]{:S(2)}, u32[]{:S(2)}) collective-permute-start(bf16[640,128]{1,0:T(8,128)(2,1)S(1)} %get-tuple-element.71), channel_id=1, source_target_pairs={{0,8},{1,9},{2,10},{3,11},{4,12},{5,13},{6,14},{7,15},{8,0},{9,1},... | collective-permute-start | bytes 491528 | tf_op jit(solution)/shard_map/ppermute | solution.py:468
  18.5 7.4 %collective-permute-start.6 = (bf16[640,128]{1,0:T(8,128)(2,1)S(1)}, bf16[640,128]{1,0:T(8,128)(2,1)S(1)}, u32[]{:S(2)}, u32[]{:S(2)}) collective-permute-start(bf16[640,128]{1,0:T(8,128)(2,1)S(1)} %get-tuple-element.71), channel_id=1, source_target_pairs={{0,2},{1,3},{2,0},{3,1},{4,6},{5,7},{6,4},{7,5},{8,16},{9,17},{10,... | collective-permute-start | bytes 491528 | tf_op jit(solution)/shard_map/ppermute | solution.py:468

commit v11 on v10

--- a/solution.py
+++ b/solution.py
@@ -114,17 +114,24 @@
     xs[...] = x_ref[...].astype(F32).reshape(ROWS * C, LON)
     for row in range(4):
         send(row, xs[latitude(row), :], xs[latitude(row + 4), :])
-    copies[3].wait()
-    bs[...] = bg_ref[...].astype(F32).reshape(ROWS * C, LON)
-    opening = lax.axis_index("tm") == 0
 
     def edge(row):
-        own = xs[latitude(row), :]
-        value = innovation_of(sums[row], own)
-        return value + jnp.where(opening, own - bs[latitude(row), :], 0.0)
+        return innovation_of(sums[row], xs[latitude(row), :])
 
     for row in range(2):
         send(4 + row, edge(row), edge(row + 6))
+    copies[3].wait()
+
+    @pl.when(lax.axis_index("tm") == 0)
+    def _():
+        bs[...] = bg_ref[...].astype(F32).reshape(ROWS * C, LON)
+
+        def opening_edge(row):
+            return edge(row) + (xs[latitude(row), :] - bs[latitude(row), :])
+
+        for row in range(2):
+            send(4 + row, opening_edge(row), opening_edge(row + 6))
+
     for copy in copies[4:]:
         copy.wait()
 

time: 27.6 us -> 27.5 us (level)
  transfers between devices with their start and end apart: 8 -> 8, of which waited for: 3 -> 3; matrix products, arithmetic and copies ran while one was open for 0% -> 0% of each run, Pallas kernels for 21% -> 20%
where the time goes in v11:
time: 27.5 us; the launch traced here: 27.4 us
  starting transfers between devices  12.6 us (46%)
  Pallas kernels  9.39 us (34%)
  waiting for transfers between devices  5.33 us (19%)
    ppermute x8, starting transfers between devices, exchange(): return lax.ppermute(value, ('tm', 'lat'), pairs)  12.6 us
    pallas_call x10, Pallas kernels, run(): pl.pallas_call(kernel, out_shape=outs, in_specs=[spec] * len(args), out_s...  9.39 us
    ppermute x8, waiting for transfers between devices, exchange(): return lax.ppermute(value, ('tm', 'lat'), pairs)  5.33 us
  transfers between devices with their start and end apart: 8, of which 3 were waited for; matrix products, arithmetic and copies ran while one was open for 0% of the time, Pallas kernels for 20%

profile of v11, /device:TPU:47, one launch (start us, length us, event | category | flops | bytes accessed | tf_op | source)
XLA Modules:
  0.0 27.4 jit_solution(2969719058692051437)
XLA Ops:
  0.0 1.2 %shard_map.73 = (bf16[384,128]{1,0:T(8,128)(2,1)S(1)}, bf16[384,128]{1,0:T(8,128)(2,1)S(1)}, bf16[64,8,128]{2,1,0:T(8,128)(2,1)S(1)}, bf16[64,8,128]{2,1,0:T(8,1...) custom-call(bf16[64,8,128]{2,1,0:T(8,128)(2,1)} %bitcast.8, ...), custom_call_target="tpu_custom_call" | custom-call | bytes 1048576 | tf_op jit(solution)/shard_map/pallas_call | solution.py:28
  1.2 2.1 %collective-permute-start = (bf16[384,128]{1,0:T(8,128)(2,1)S(1)}, bf16[384,128]{1,0:T(8,128)(2,1)S(1)}, u32[]{:S(2)}, u32[]{:S(2)}) collective-permute-start(bf16[384,128]{1,0:T(8,128)(2,1)S(1)} %get-tuple-element.48), channel_id=1, source_target_pairs={{0,1},{1,0},{2,3},{3,2},{4,5},{5,4},{6,7},{7,6},{8,9},{9,8},{10,11... | collective-permute-start | bytes 294920 | tf_op jit(solution)/shard_map/ppermute | solution.py:475
  3.3 1.2 %collective-permute-start.1 = (bf16[384,128]{1,0:T(8,128)(2,1)S(1)}, bf16[384,128]{1,0:T(8,128)(2,1)S(1)}, u32[]{:S(2)}, u32[]{:S(2)}) collective-permute-start(bf16[384,128]{1,0:T(8,128)(2,1)S(1)} %get-tuple-element.49), channel_id=1, source_target_pairs={{0,8},{1,2},{2,1},{3,4},{4,3},{5,6},{6,5},{7,15},{8,0},{9,10},{10,... | collective-permute-start | bytes 294920 | tf_op jit(solution)/shard_map/ppermute | solution.py:475
  4.5 0.4 %shard_map.74 = (bf16[512,128]{1,0:T(8,128)(2,1)S(1)}, bf16[512,128]{1,0:T(8,128)(2,1)S(1)}, f32[8,72,128]{2,1,0:T(8,128)S(1)}, bf16[1024,192]{1,0:T(8,128)(2,1)...) custom-call(bf16[64,8,128]{2,1,0:T(8,128)(2,1)S(1)} %get-tuple-element.40.x_ref, ...), custom_call_target="tpu_custom_call" | custom-call | flops 41943040 | bytes 1048576 | tf_op jit(solution)/shard_map/pallas_call | solution.py:28
  5.0 1.3 %collective-permute-start.5 = (bf16[512,128]{1,0:T(8,128)(2,1)S(1)}, bf16[512,128]{1,0:T(8,128)(2,1)S(1)}, u32[]{:S(2)}, u32[]{:S(2)}) collective-permute-start(bf16[512,128]{1,0:T(8,128)(2,1)S(1)} %get-tuple-element.47.state_ref.own_ref), channel_id=1, source_target_pairs={{0,8},{1,9},{2,10},{3,11},{4,12},{5,13},{6,14},{7,15},{8,0},{9,1},... | collective-permute-start | bytes 393224 | tf_op jit(solution)/shard_map/ppermute | solution.py:475
  6.3 1.5 %collective-permute-start.3 = (bf16[512,128]{1,0:T(8,128)(2,1)S(1)}, bf16[512,128]{1,0:T(8,128)(2,1)S(1)}, u32[]{:S(2)}, u32[]{:S(2)}) collective-permute-start(bf16[512,128]{1,0:T(8,128)(2,1)S(1)} %get-tuple-element.47.state_ref.own_ref), channel_id=1, source_target_pairs={{0,2},{1,3},{2,0},{3,1},{4,6},{5,7},{6,4},{7,5},{8,16},{9,17},{10,... | collective-permute-start | bytes 393224 | tf_op jit(solution)/shard_map/ppermute | solution.py:475
  7.8 0.9 %shard_map.75 = (bf16[1536,128]{1,0:T(8,128)(2,1)S(1)}, bf16[384,128]{1,0:T(8,128)(2,1)S(1)}) custom-call(bf16[512,128]{1,0:T(8,128)(2,1)S(1)} %get-tuple-element.47.state_ref.own_ref, bf16[1024,192]{1,0:T(8,128)(2,1)S(1)} %get-tuple-element.50.conv_ref, f32[256,128]{1,0:T(8,128)S(1)} %get-tuple-element.51.bias_ref, ...), custom_call_target="tpu_custom_call" | custom-call | flops 251658240 | bytes 2097152 | tf_op jit(solution)/shard_map/pallas_call | solution.py:28
  8.6 0.0 collective-permute-done.first_ref
  8.7 0.6 %collective-permute-done.1.second_ref = bf16[384,128]{1,0:T(8,128)(2,1)S(1)} collective-permute-done((bf16[384,128]{1,0:T(8,128)(2,1)S(1)}, bf16[384,128]{1,0:T(8,128)(2,1)S(1)}, u32[]{:S(2)}, u32[]{:S(2)}) %collective-permute-start.1) | collective-permute-done | bytes 98336 | tf_op jit(solution)/shard_map/ppermute | solution.py:475
  9.3 0.1 shard_map.76
  9.3 2.1 %collective-permute-start.4 = (bf16[384,128]{1,0:T(8,128)(2,1)S(1)}, bf16[384,128]{1,0:T(8,128)(2,1)S(1)}, u32[]{:S(2)}, u32[]{:S(2)}) collective-permute-start(bf16[384,128]{1,0:T(8,128)(2,1)S(1)} %get-tuple-element.57), channel_id=1, source_target_pairs={{0,8},{1,9},{2,10},{3,11},{4,12},{5,13},{6,14},{7,15},{8,0},{9,1},... | collective-permute-start | bytes 294920 | tf_op jit(solution)/shard_map/ppermute | solution.py:475
  11.4 2.4 %collective-permute-start.2 = (bf16[384,128]{1,0:T(8,128)(2,1)S(1)}, bf16[384,128]{1,0:T(8,128)(2,1)S(1)}, u32[]{:S(2)}, u32[]{:S(2)}) collective-permute-start(bf16[384,128]{1,0:T(8,128)(2,1)S(1)} %get-tuple-element.57), channel_id=1, source_target_pairs={{0,2},{1,3},{2,0},{3,1},{4,6},{5,7},{6,4},{7,5},{8,16},{9,17},{10,... | collective-permute-start | bytes 294920 | tf_op jit(solution)/shard_map/ppermute | solution.py:475
  13.8 0.9 %shard_map.77 = (bf16[2048,128]{1,0:T(8,128)(2,1)S(1)}, bf16[512,128]{1,0:T(8,128)(2,1)S(1)}) custom-call(bf16[1024,128]{1,0:T(8,128)(2,1)S(1)} %get-tuple-element.58.state_ref.own_ref, bf16[1024,192]{1,0:T(8,128)(2,1)S(1)} %get-tuple-element.50.conv_ref, f32[256,128]{1,0:T(8,128)S(1)} %get-tuple-element.51.bias_ref, ...), custom_call_target="tpu_custom_call" | custom-call | flops 335544320 | bytes 2097152 | tf_op jit(solution)/shard_map/pallas_call | solution.py:28
  14.7 0.0 collective-permute-done.5.near_own_ref
  14.7 0.0 collective-permute-done.3.far_own_ref
  14.7 0.0 collective-permute-done.4.near_ref
  14.7 1.2 %shard_map.78 = (bf16[768,128]{1,0:T(8,128)(2,1)S(1)}, bf16[768,128]{1,0:T(8,128)(2,1)S(1)}) custom-call(bf16[384,128]{1,0:T(8,128)(2,1)S(1)} %collective-permute-done.4.near_ref, bf16[512,128]{1,0:T(8,128)(2,1)S(1)} %collective-permute-done.5.near_own_ref, bf16[512,128]{1,0:T(8,128)(2,1)S(1)} %collective-permute-done.3.far_own_ref, ...), custom_call_target="tpu_custom_call" | custom-call | flops 503316480 | bytes 2097152 | tf_op jit(solution)/shard_map/pallas_call | solution.py:28
  16.0 1.3 %collective-permute-done.2.far_ref = bf16[384,128]{1,0:T(8,128)(2,1)S(1)} collective-permute-done((bf16[384,128]{1,0:T(8,128)(2,1)S(1)}, bf16[384,128]{1,0:T(8,128)(2,1)S(1)}, u32[]{:S(2)}, u32[]{:S(2)}) %collective-permute-start.2) | collective-permute-done | bytes 98336 | tf_op jit(solution)/shard_map/ppermute | solution.py:475
  17.3 1.1 %shard_map.79 = (bf16[768,128]{1,0:T(8,128)(2,1)S(1)}, bf16[640,128]{1,0:T(8,128)(2,1)S(1)}) custom-call(bf16[384,128]{1,0:T(8,128)(2,1)S(1)} %collective-permute-done.2.far_ref, bf16[512,128]{1,0:T(8,128)(2,1)S(1)} %collective-permute-done.3.far_own_ref, bf16[768,128]{1,0:T(8,128)(2,1)S(1)} %get-tuple-element.65.part_ref, ...), custom_call_target="tpu_custom_call" | custom-call | flops 503316480 | bytes 2097152 | tf_op jit(solution)/shard_map/pallas_call | solution.py:28
  18.4 0.1 collective-permute-start.7
  18.4 1.9 %collective-permute-start.6 = (bf16[640,128]{1,0:T(8,128)(2,1)S(1)}, bf16[640,128]{1,0:T(8,128)(2,1)S(1)}, u32[]{:S(2)}, u32[]{:S(2)}) collective-permute-start(bf16[640,128]{1,0:T(8,128)(2,1)S(1)} %get-tuple-element.71), channel_id=1, source_target_pairs={{0,2},{1,3},{2,0},{3,1},{4,6},{5,7},{6,4},{7,5},{8,16},{9,17},{10,... | collective-permute-start | bytes 491528 | tf_op jit(solution)/shard_map/ppermute | solution.py:475
  20.3 1.2 %shard_map.80 = (bf16[2560,128]{1,0:T(8,128)(2,1)S(1)}, bf16[640,128]{1,0:T(8,128)(2,1)S(1)}) custom-call(bf16[768,128]{1,0:T(8,128)(2,1)S(1)} %get-tuple-element.72.state_ref.own_ref, bf16[1024,192]{1,0:T(8,128)(2,1)S(1)} %get-tuple-element.50.conv_ref, f32[256,128]{1,0:T(8,128)S(1)} %get-tuple-element.51.bias_ref, ...), custom_call_target="tpu_custom_call" | custom-call | flops 419430400 | bytes 2097152 | tf_op jit(solution)/shard_map/pallas_call | solution.py:28
  21.5 0.0 collective-permute-done.7.near_ref
  21.5 0.9 %shard_map.81.part_ref = bf16[512,128]{1,0:T(8,128)(2,1)S(1)} custom-call(bf16[640,128]{1,0:T(8,128)(2,1)S(1)} %collective-permute-done.7.near_ref, bf16[768,128]{1,0:T(8,128)(2,1)S(1)} %get-tuple-element.72.state_ref.own_ref, bf16[2560,128]{1,0:T(8,128)(2,1)S(1)} %get-tuple-element.73.active_ref, bf16[640,128]{1,0:T(8,128)(2,1)S(1)} %get-tuple-element.74.forecast_ref, ...), custom_call_target="tpu_custom_call" | custom-call | flops 335544320 | bytes 2097152 | tf_op jit(solution)/shard_map/pallas_call | solution.py:28
  22.5 3.4 %collective-permute-done.6.far_ref = bf16[640,128]{1,0:T(8,128)(2,1)S(1)} collective-permute-done((bf16[640,128]{1,0:T(8,128)(2,1)S(1)}, bf16[640,128]{1,0:T(8,128)(2,1)S(1)}, u32[]{:S(2)}, u32[]{:S(2)}) %collective-permute-start.6) | collective-permute-done | bytes 163872 | tf_op jit(solution)/shard_map/ppermute | solution.py:475
  25.9 1.5 %shard_map.82 = bf16[64,8,128]{2,1,0:T(8,128)(2,1)} custom-call(bf16[640,128]{1,0:T(8,128)(2,1)S(1)} %collective-permute-done.6.far_ref, bf16[512,128]{1,0:T(8,128)(2,1)S(1)} %shard_map.81.part_ref, bf16[768,128]{1,0:T(8,128)(2,1)S(1)} %get-tuple-element.72.state_ref.own_ref, bf16[512,128]{1,0:T(8,128)(2,1)S(1)} %get-tuple-element.67.bg_ref, ...), custom_call_target="tpu_custom_call" | custom-call | flops 335544320 | bytes 2097152 | tf_op jit(solution)/shard_map/pallas_call | solution.py:28
Async XLA Ops:
  1.2 7.4 %collective-permute-start = (bf16[384,128]{1,0:T(8,128)(2,1)S(1)}, bf16[384,128]{1,0:T(8,128)(2,1)S(1)}, u32[]{:S(2)}, u32[]{:S(2)}) collective-permute-start(bf16[384,128]{1,0:T(8,128)(2,1)S(1)} %get-tuple-element.48), channel_id=1, source_target_pairs={{0,1},{1,0},{2,3},{3,2},{4,5},{5,4},{6,7},{7,6},{8,9},{9,8},{10,11... | collective-permute-start | bytes 294920 | tf_op jit(solution)/shard_map/ppermute | solution.py:475
  3.3 6.0 %collective-permute-start.1 = (bf16[384,128]{1,0:T(8,128)(2,1)S(1)}, bf16[384,128]{1,0:T(8,128)(2,1)S(1)}, u32[]{:S(2)}, u32[]{:S(2)}) collective-permute-start(bf16[384,128]{1,0:T(8,128)(2,1)S(1)} %get-tuple-element.49), channel_id=1, source_target_pairs={{0,8},{1,2},{2,1},{3,4},{4,3},{5,6},{6,5},{7,15},{8,0},{9,10},{10,... | collective-permute-start | bytes 294920 | tf_op jit(solution)/shard_map/ppermute | solution.py:475
  5.0 9.8 %collective-permute-start.5 = (bf16[512,128]{1,0:T(8,128)(2,1)S(1)}, bf16[512,128]{1,0:T(8,128)(2,1)S(1)}, u32[]{:S(2)}, u32[]{:S(2)}) collective-permute-start(bf16[512,128]{1,0:T(8,128)(2,1)S(1)} %get-tuple-element.47.state_ref.own_ref), channel_id=1, source_target_pairs={{0,8},{1,9},{2,10},{3,11},{4,12},{5,13},{6,14},{7,15},{8,0},{9,1},... | collective-permute-start | bytes 393224 | tf_op jit(solution)/shard_map/ppermute | solution.py:475
  6.3 8.5 %collective-permute-start.3 = (bf16[512,128]{1,0:T(8,128)(2,1)S(1)}, bf16[512,128]{1,0:T(8,128)(2,1)S(1)}, u32[]{:S(2)}, u32[]{:S(2)}) collective-permute-start(bf16[512,128]{1,0:T(8,128)(2,1)S(1)} %get-tuple-element.47.state_ref.own_ref), channel_id=1, source_target_pairs={{0,2},{1,3},{2,0},{3,1},{4,6},{5,7},{6,4},{7,5},{8,16},{9,17},{10,... | collective-permute-start | bytes 393224 | tf_op jit(solution)/shard_map/ppermute | solution.py:475
  9.3 5.4 %collective-permute-start.4 = (bf16[384,128]{1,0:T(8,128)(2,1)S(1)}, bf16[384,128]{1,0:T(8,128)(2,1)S(1)}, u32[]{:S(2)}, u32[]{:S(2)}) collective-permute-start(bf16[384,128]{1,0:T(8,128)(2,1)S(1)} %get-tuple-element.57), channel_id=1, source_target_pairs={{0,8},{1,9},{2,10},{3,11},{4,12},{5,13},{6,14},{7,15},{8,0},{9,1},... | collective-permute-start | bytes 294920 | tf_op jit(solution)/shard_map/ppermute | solution.py:475
  11.4 5.9 %collective-permute-start.2 = (bf16[384,128]{1,0:T(8,128)(2,1)S(1)}, bf16[384,128]{1,0:T(8,128)(2,1)S(1)}, u32[]{:S(2)}, u32[]{:S(2)}) collective-permute-start(bf16[384,128]{1,0:T(8,128)(2,1)S(1)} %get-tuple-element.57), channel_id=1, source_target_pairs={{0,2},{1,3},{2,0},{3,1},{4,6},{5,7},{6,4},{7,5},{8,16},{9,17},{10,... | collective-permute-start | bytes 294920 | tf_op jit(solution)/shard_map/ppermute | solution.py:475
  18.4 3.2 %collective-permute-start.7 = (bf16[640,128]{1,0:T(8,128)(2,1)S(1)}, bf16[640,128]{1,0:T(8,128)(2,1)S(1)}, u32[]{:S(2)}, u32[]{:S(2)}) collective-permute-start(bf16[640,128]{1,0:T(8,128)(2,1)S(1)} %get-tuple-element.71), channel_id=1, source_target_pairs={{0,8},{1,9},{2,10},{3,11},{4,12},{5,13},{6,14},{7,15},{8,0},{9,1},... | collective-permute-start | bytes 491528 | tf_op jit(solution)/shard_map/ppermute | solution.py:475
  18.4 7.4 %collective-permute-start.6 = (bf16[640,128]{1,0:T(8,128)(2,1)S(1)}, bf16[640,128]{1,0:T(8,128)(2,1)S(1)}, u32[]{:S(2)}, u32[]{:S(2)}) collective-permute-start(bf16[640,128]{1,0:T(8,128)(2,1)S(1)} %get-tuple-element.71), channel_id=1, source_target_pairs={{0,2},{1,3},{2,0},{3,1},{4,6},{5,7},{6,4},{7,5},{8,16},{9,17},{10,... | collective-permute-start | bytes 491528 | tf_op jit(solution)/shard_map/ppermute | solution.py:475
